TPU v7x, 32 devices: a whole 2x2x4 slice. The times are simulated.
32 devices in a mesh: dp: 8 (over z, y), seq: 4 (over x, core).
Axes of the slice: x: 2, y: 2, z: 4, core: 2. Of those that a mesh axis runs over, the one named last changes fastest.
Arguments:
- hidden_in: bfloat16 [16, 1024, 1024], P('dp', 'seq'), may hold values from -6 to 6
- attn_gain: bfloat16 [1024], P(('dp', 'seq')), may hold values from 0.25 to 1.75
- w_query: bfloat16 [1024, 2048], P(('dp', 'seq')), may hold values from -0.1875 to 0.1875
- key_weight: bfloat16 [1024, 1024], P(('dp', 'seq')), may hold values from -0.1875 to 0.1875
- value_weight: bfloat16 [1024, 1024], P(('dp', 'seq')), may hold values from -0.1875 to 0.1875
- query_gain: bfloat16 [128], replicated, may hold values from 0.25 to 1.75
- key_gain: bfloat16 [128], replicated, may hold values from 0.25 to 1.75
- w_out: bfloat16 [2048, 1024], P(('dp', 'seq')), may hold values from -1.5 to 1.5
- mlp_gain: bfloat16 [1024], P(('dp', 'seq')), may hold values from 0.25 to 1.75
- w_gate: bfloat16 [1024, 3072], P(('dp', 'seq')), may hold values from -0.1875 to 0.1875
- w_up: bfloat16 [1024, 3072], P(('dp', 'seq')), may hold values from -0.1875 to 0.1875
- w_down: bfloat16 [3072, 1024], P(('dp', 'seq')), may hold values from -0.21875 to 0.21875
- cotangent: bfloat16 [16, 1024, 1024], P('dp', 'seq'), may hold values from -6 to 6
Outputs:
- hidden_out: bfloat16 [16, 1024, 1024], P('dp', 'seq')
- grad_in: float32 [16, 1024, 1024], P('dp', 'seq')
- grad_attn_gain: float32 [1024], P(('dp', 'seq'))
- grad_query_w: float32 [1024, 2048], P(('dp', 'seq'))
- grad_key_w: float32 [1024, 1024], P(('dp', 'seq'))
- grad_value_w: float32 [1024, 1024], P(('dp', 'seq'))
- grad_query_gain: float32 [128], replicated
- grad_key_gain: float32 [128], replicated
- grad_out_w: float32 [2048, 1024], P(('dp', 'seq'))
- grad_mlp_gain: float32 [1024], P(('dp', 'seq'))
- grad_gate_w: float32 [1024, 3072], P(('dp', 'seq'))
- grad_up_w: float32 [1024, 3072], P(('dp', 'seq'))
- grad_down_w: float32 [3072, 1024], P(('dp', 'seq'))
All inputs are finite; a program needn't handle non-finite values.
Results may differ from a plain program's by a relative error of at most 0.017.
Values may be sent and summed in bfloat16 or wider, within the bound.
A program may use at most 320 MiB of HBM per device.

v0:
```python
import jax
import jax.numpy as jnp
from jax import lax
from jax.sharding import PartitionSpec as P

HEAD_SIZE = 128


EPS = 1e-06
ROPE_THETA = 1000000.0


def shortened(array):
    return jax.tree.map(lambda a: a.astype(jnp.bfloat16) if a.dtype == jnp.float32 else a, array)


def rms_scale(value_rows):
    return lax.rsqrt(jnp.mean(value_rows * value_rows, axis=-1, keepdims=True) + EPS)


def rope_tables(positions):
    halfway = HEAD_SIZE // 2
    inverse = jnp.power(
        jnp.float32(ROPE_THETA), -(jnp.arange(halfway).astype(jnp.float32) * 2.0) / HEAD_SIZE
    )
    angles = positions.astype(jnp.float32)[:, None] * inverse[None, :]
    angles = jnp.concatenate([angles, angles], axis=-1)
    return (jnp.cos(angles), jnp.sin(angles))


def rotate(value_rows, cosine, sine):
    halfway = value_rows.shape[-1] // 2
    turned = jnp.concatenate([-value_rows[..., halfway:], value_rows[..., :halfway]], axis=-1)
    return value_rows * cosine[:, None, :] + turned * sine[:, None, :]


def prepare(projected, gain, cosine, sine):
    shaped = projected.reshape(projected.shape[:-1] + (-1, HEAD_SIZE))
    normed = shaped * rms_scale(shaped) * gain
    return rotate(normed, cosine, sine).reshape(projected.shape)


def norm_apply(value_rows, gain):
    return value_rows * rms_scale(value_rows) * gain


def swiglu(gate, upward):
    return jax.nn.silu(gate) * upward


def masked_scores(query_rows, keys, positions):
    piece = query_rows.shape[0]
    length = keys.shape[0]
    heads_kv = keys.shape[1] // HEAD_SIZE
    grouped = query_rows.reshape(piece, heads_kv, -1, HEAD_SIZE)
    key_heads = keys.reshape(length, heads_kv, HEAD_SIZE)
    raw = jnp.einsum(
        "qkgd,tkd->kgqt", grouped, key_heads, preferred_element_type=jnp.float32
    ) * HEAD_SIZE ** (-0.5)
    allowed = jnp.arange(length)[None, :] <= positions[:, None]
    return (jnp.where(allowed, raw, -jnp.inf), grouped, key_heads)


def attention_forward(query_rows, keys, value_rows, positions):
    scores, grouped, key_heads = masked_scores(query_rows, keys, positions)
    highest = jnp.max(scores, axis=-1, keepdims=True)
    exponent = jnp.exp(scores - highest)
    total = jnp.sum(exponent, axis=-1, keepdims=True)
    probs = (exponent / total).astype(jnp.bfloat16)
    value_heads = value_rows.reshape(key_heads.shape)
    mixed = jnp.einsum("kgqt,tkd->qkgd", probs, value_heads, preferred_element_type=jnp.float32)
    return (mixed.reshape(query_rows.shape).astype(jnp.bfloat16), highest + jnp.log(total))


def attention_backward(query_rows, keys, value_rows, grad_mixed, log_total, positions):
    scores, grouped, key_heads = masked_scores(query_rows, keys, positions)
    probs = jnp.exp(scores - log_total)
    low_probs = probs.astype(jnp.bfloat16)
    value_heads = value_rows.reshape(key_heads.shape)
    grad_heads = grad_mixed.reshape(grouped.shape)
    grad_values = jnp.einsum(
        "kgqt,qkgd->tkd", low_probs, grad_heads, preferred_element_type=jnp.float32
    )
    grad_probs = jnp.einsum(
        "qkgd,tkd->kgqt", grad_heads, value_heads, preferred_element_type=jnp.float32
    )
    inner = jnp.sum(probs * grad_probs, axis=-1, keepdims=True)
    grad_scores = (probs * (grad_probs - inner)).astype(jnp.bfloat16)
    grad_query = jnp.einsum(
        "kgqt,tkd->qkgd", grad_scores, key_heads, preferred_element_type=jnp.float32
    ) * HEAD_SIZE ** (-0.5)
    grad_keys = jnp.einsum(
        "kgqt,qkgd->tkd", grad_scores, grouped, preferred_element_type=jnp.float32
    ) * HEAD_SIZE ** (-0.5)
    length = keys.shape[0]
    return (
        grad_query.reshape(query_rows.shape[0], -1),
        grad_keys.reshape(length, -1),
        grad_values.reshape(length, -1),
    )


def layer_forward(tokens, full, head_gains, sequences, positions, cosine, sine, gather_keys):
    attn_gain, w_query, key_weight, value_weight, w_out, mlp_gain, w_gate, w_up, w_down = full
    query_gain, key_gain = head_gains
    piece = positions.shape[0]
    normed = norm_apply(tokens, attn_gain.astype(jnp.float32)).astype(jnp.bfloat16)
    query_proj = jnp.dot(normed, w_query, preferred_element_type=jnp.float32)
    key_proj = jnp.dot(normed, key_weight, preferred_element_type=jnp.float32)
    value_rows = jnp.dot(normed, value_weight, preferred_element_type=jnp.float32).astype(
        jnp.bfloat16
    )
    query_rows = prepare(query_proj, query_gain, cosine, sine).astype(jnp.bfloat16)
    keys = prepare(key_proj, key_gain, cosine, sine).astype(jnp.bfloat16)
    keys_all, values_all = gather_keys(
        (keys.reshape(sequences, piece, -1), value_rows.reshape(sequences, piece, -1))
    )
    query_seqwise = query_rows.reshape(sequences, piece, -1)
    mixed, log_total = lax.map(
        lambda item: attention_forward(item[0], item[1], item[2], positions),
        (query_seqwise, keys_all, values_all),
    )
    mixed_rows = mixed.reshape(tokens.shape[0], -1)
    residual = tokens + jnp.dot(mixed_rows, w_out, preferred_element_type=jnp.float32)
    normed_mlp = norm_apply(residual, mlp_gain.astype(jnp.float32)).astype(jnp.bfloat16)
    gate = jnp.dot(normed_mlp, w_gate, preferred_element_type=jnp.float32)
    upward = jnp.dot(normed_mlp, w_up, preferred_element_type=jnp.float32)
    hidden = swiglu(gate, upward).astype(jnp.bfloat16)
    output = residual + jnp.dot(hidden, w_down, preferred_element_type=jnp.float32)
    saved = (
        normed,
        query_proj,
        key_proj,
        query_seqwise,
        keys_all,
        values_all,
        log_total,
        mixed_rows,
        residual,
        normed_mlp,
        gate,
        upward,
        hidden,
    )
    return (output, saved)


def body(
    hidden_in,
    attn_gain,
    w_query,
    key_weight,
    value_weight,
    query_gain,
    key_gain,
    w_out,
    mlp_gain,
    w_gate,
    w_up,
    w_down,
    cotangent,
):
    sequences, piece, width = hidden_in.shape
    rows = sequences * piece
    positions = lax.axis_index("seq") * piece + jnp.arange(piece)
    cosine, sine = rope_tables(jnp.tile(positions, sequences))
    tokens = hidden_in.reshape(rows, width).astype(jnp.float32)
    shards = (attn_gain, w_query, key_weight, value_weight, w_out, mlp_gain, w_gate, w_up, w_down)
    head_gains = (query_gain.astype(jnp.float32), key_gain.astype(jnp.float32))
    full = (
        lax.all_gather(shards[0], ("dp", "seq"), axis=0, tiled=True),
        lax.all_gather(shards[1], ("dp", "seq"), axis=0, tiled=True),
        lax.all_gather(shards[2], ("dp", "seq"), axis=0, tiled=True),
        lax.all_gather(shards[3], ("dp", "seq"), axis=0, tiled=True),
        lax.all_gather(shards[4], ("dp", "seq"), axis=0, tiled=True),
        lax.all_gather(shards[5], ("dp", "seq"), axis=0, tiled=True),
        lax.all_gather(shards[6], ("dp", "seq"), axis=0, tiled=True),
        lax.all_gather(shards[7], ("dp", "seq"), axis=0, tiled=True),
        lax.all_gather(shards[8], ("dp", "seq"), axis=0, tiled=True),
    )
    output, saved = layer_forward(
        tokens,
        full,
        head_gains,
        sequences,
        positions,
        cosine,
        sine,
        lambda pair: jax.tree.map(
            lambda part, own: part.astype(own.dtype),
            lax.all_gather(shortened(pair), "seq", axis=1, tiled=True),
            pair,
        ),
    )
    again, shards_again, finished = lax.optimization_barrier((tokens, shards, output))
    full = (
        lax.all_gather(shards_again[0], ("dp", "seq"), axis=0, tiled=True),
        lax.all_gather(shards_again[1], ("dp", "seq"), axis=0, tiled=True),
        lax.all_gather(shards_again[2], ("dp", "seq"), axis=0, tiled=True),
        lax.all_gather(shards_again[3], ("dp", "seq"), axis=0, tiled=True),
        lax.all_gather(shards_again[4], ("dp", "seq"), axis=0, tiled=True),
        lax.all_gather(shards_again[5], ("dp", "seq"), axis=0, tiled=True),
        lax.all_gather(shards_again[6], ("dp", "seq"), axis=0, tiled=True),
        lax.all_gather(shards_again[7], ("dp", "seq"), axis=0, tiled=True),
        lax.all_gather(shards_again[8], ("dp", "seq"), axis=0, tiled=True),
    )
    unused, saved = layer_forward(
        again,
        full,
        head_gains,
        sequences,
        positions,
        cosine,
        sine,
        lambda pair: jax.tree.map(
            lambda part, own: part.astype(own.dtype),
            lax.all_gather(shortened(pair), "seq", axis=1, tiled=True),
            pair,
        ),
    )
    (
        normed,
        query_proj,
        key_proj,
        query_seqwise,
        keys_all,
        values_all,
        log_total,
        mixed_rows,
        residual,
        normed_mlp,
        gate,
        upward,
        hidden,
    ) = saved
    (
        full_attn_gain,
        full_query,
        full_key,
        full_value,
        full_out,
        full_mlp_gain,
        full_gate,
        full_up,
        full_down,
    ) = full
    grad_top = cotangent.reshape(rows, width)
    grad_down = jnp.dot(hidden.T, grad_top, preferred_element_type=jnp.float32)
    grad_hidden = jnp.dot(grad_top, full_down.T, preferred_element_type=jnp.float32)
    unused, pull = jax.vjp(swiglu, gate, upward)
    grad_gate, grad_upward = pull(grad_hidden)
    grad_gate = grad_gate.astype(jnp.bfloat16)
    grad_upward = grad_upward.astype(jnp.bfloat16)
    grad_w_gate = jnp.dot(normed_mlp.T, grad_gate, preferred_element_type=jnp.float32)
    grad_w_up = jnp.dot(normed_mlp.T, grad_upward, preferred_element_type=jnp.float32)
    grad_normed_mlp = jnp.dot(grad_gate, full_gate.T, preferred_element_type=jnp.float32) + jnp.dot(
        grad_upward, full_up.T, preferred_element_type=jnp.float32
    )
    unused, pull = jax.vjp(norm_apply, residual, full_mlp_gain.astype(jnp.float32))
    grad_res_part, grad_mlp_gain = pull(grad_normed_mlp)
    grad_residual = grad_top.astype(jnp.float32) + grad_res_part
    grad_branch = grad_residual.astype(jnp.bfloat16)
    grad_w_out = jnp.dot(mixed_rows.T, grad_branch, preferred_element_type=jnp.float32)
    grad_mixed = jnp.dot(grad_branch, full_out.T, preferred_element_type=jnp.float32).astype(
        jnp.bfloat16
    )
    grad_query, grad_keys_all, grad_values_all = lax.map(
        lambda item: attention_backward(item[0], item[1], item[2], item[3], item[4], positions),
        (query_seqwise, keys_all, values_all, grad_mixed.reshape(sequences, piece, -1), log_total),
    )
    grad_keys, grad_values = (
        lax.psum_scatter(
            grad_keys_all.astype(jnp.bfloat16), "seq", scatter_dimension=1, tiled=True
        ).astype(jnp.float32),
        lax.psum_scatter(
            grad_values_all.astype(jnp.bfloat16), "seq", scatter_dimension=1, tiled=True
        ).astype(jnp.float32),
    )
    unused, pull = jax.vjp(
        lambda projected, gain: prepare(projected, gain, cosine, sine), query_proj, head_gains[0]
    )
    grad_query_proj, grad_query_gain = pull(grad_query.reshape(rows, -1))
    unused, pull = jax.vjp(
        lambda projected, gain: prepare(projected, gain, cosine, sine), key_proj, head_gains[1]
    )
    grad_key_proj, grad_key_gain = pull(grad_keys.reshape(rows, -1))
    grad_query_proj = grad_query_proj.astype(jnp.bfloat16)
    grad_key_proj = grad_key_proj.astype(jnp.bfloat16)
    grad_value_proj = grad_values.reshape(rows, -1).astype(jnp.bfloat16)
    grad_w_query = jnp.dot(normed.T, grad_query_proj, preferred_element_type=jnp.float32)
    grad_w_key = jnp.dot(normed.T, grad_key_proj, preferred_element_type=jnp.float32)
    grad_w_value = jnp.dot(normed.T, grad_value_proj, preferred_element_type=jnp.float32)
    grad_normed = (
        jnp.dot(grad_query_proj, full_query.T, preferred_element_type=jnp.float32)
        + jnp.dot(grad_key_proj, full_key.T, preferred_element_type=jnp.float32)
        + jnp.dot(grad_value_proj, full_value.T, preferred_element_type=jnp.float32)
    )
    unused, pull = jax.vjp(norm_apply, tokens, full_attn_gain.astype(jnp.float32))
    grad_tok_part, grad_attn_gain = pull(grad_normed)
    grad_tokens = grad_residual + grad_tok_part
    gradients = (
        grad_attn_gain,
        grad_w_query,
        grad_w_key,
        grad_w_value,
        grad_w_out,
        grad_mlp_gain,
        grad_w_gate,
        grad_w_up,
        grad_down,
    )
    devices = lax.axis_size(("dp", "seq"))
    flat = jnp.concatenate([member.reshape(devices, -1) for member in gradients], axis=1)
    owned_flat = lax.psum_scatter(flat, ("dp", "seq"), scatter_dimension=0, tiled=True)[0]
    owned = []
    offset = 0
    for member in gradients:
        length = member.size // devices
        owned.append(
            owned_flat[offset : offset + length].reshape(
                (member.shape[0] // devices,) + member.shape[1:]
            )
        )
        offset = offset + length
    gain_sums = lax.psum((grad_query_gain, grad_key_gain), ("dp", "seq"))
    return (
        output.reshape(sequences, piece, width).astype(jnp.bfloat16),
        grad_tokens.reshape(sequences, piece, width),
        owned[0],
        owned[1],
        owned[2],
        owned[3],
        gain_sums[0],
        gain_sums[1],
        owned[4],
        owned[5],
        owned[6],
        owned[7],
        owned[8],
    )


def solution(mesh):
    return jax.shard_map(
        body,
        mesh=mesh,
        in_specs=(
            P("dp", "seq", None),
            P(("dp", "seq")),
            P(("dp", "seq"), None),
            P(("dp", "seq"), None),
            P(("dp", "seq"), None),
            P(),
            P(),
            P(("dp", "seq"), None),
            P(("dp", "seq")),
            P(("dp", "seq"), None),
            P(("dp", "seq"), None),
            P(("dp", "seq"), None),
            P("dp", "seq", None),
        ),
        out_specs=(
            P("dp", "seq", None),
            P("dp", "seq", None),
            P(("dp", "seq")),
            P(("dp", "seq"), None),
            P(("dp", "seq"), None),
            P(("dp", "seq"), None),
            P(),
            P(),
            P(("dp", "seq"), None),
            P(("dp", "seq")),
            P(("dp", "seq"), None),
            P(("dp", "seq"), None),
            P(("dp", "seq"), None),
        ),
        check_vma=False,
    )
```

profile of v0, /device:TPU:0, one launch (start us, length us, event | category | flops | bytes accessed | tf_op | source)
XLA Modules:
  0.0 2624.6 jit_solution(16350051220491306582)
XLA Ops:
  11.1 42.1 %all-reduce.11 = (bf16[1024]{0:T(1024)(128)(2,1)S(1)}, bf16[1024]{0:T(1024)(128)(2,1)S(1)}) all-reduce(bf16[1024]{0:T(1024)(128)(2,1)S(1)} %dynamic-update-slice, bf16[1024]{0:T(1024)(128)(2,1)S(1)} %dynamic-update-slice.1), channel_id=1, replica_groups=mesh['dp'=8,'seq'=4] {'dp','seq'}, use_global_device_ids=true, to_apply=%add.4 | all-reduce | flops 2048 | bytes 8192
  55.4 14.5 all-gather.19.cloned.1.call-done
  76.0 51.8 %all-gather.23.cloned.1.call-done = bf16[1024,1024]{1,0:T(8,128)(2,1)} async-done(((bf16[32,1024]{1,0:T(8,128)(2,1)}), bf16[1024,1024]{1,0:T(8,128)(2,1)}) %all-gather.23.cloned.1.call-update) | async-done | bytes 2097168 | tf_op jit(solution)/shard_map/all_gather | solution.py:173
  144.9 46.4 %all-gather.27.cloned.1.call-done = bf16[1024,2048]{1,0:T(8,128)(2,1)} async-done(((bf16[32,2048]{1,0:T(8,128)(2,1)}), bf16[1024,2048]{1,0:T(8,128)(2,1)}) %all-gather.27.cloned.1.call-update) | async-done | bytes 4194320 | tf_op jit(solution)/shard_map/all_gather | solution.py:172
  211.3 15.8 all-gather.21.cloned.1.call-done
  227.1 36.4 %all-gather.25.cloned.1.call-done = bf16[2,1024,1024]{1,2,0:T(8,128)(2,1)} async-done(((bf16[2,256,1024]{1,2,0:T(8,128)(2,1)}), bf16[2,1024,1024]{1,2,0:T(8,128)(2,1)}) %all-gather.25.cloned.1.call-update) | async-done | bytes 4194320 | tf_op jit(solution)/shard_map/all_gather | solution.py:191
  265.1 47.3 %while.39 = (s32[]{:T(128)}, bf16[2,256,2048]{2,1,0:T(8,128)(2,1)}, bf16[2,1024,1024]{1,2,0:T(8,128)(2,1)}, bf16[2,1024,1024]{1,2,0:T(8,128)(2,1)}, bf16[2,256,2048]{1,2,0:T(8,128)(2,1)}, /*index=5*/s32[]{:T(128)}, s32[]{:T(128)}) while((s32[]{:T(128)}, bf16[2,256,2048]{2,1,0:T(8,128)(2,1)}, bf16[2,1024,1024]{1,2,0:T(8,128)(2,1)}, ...), condition=%wide.region_6.7_spmd.clone, body=%wide.region_3.6_spmd.clone.sunk | while | flops 2173437184 | bytes 63473792 | solution.py:119
  269.5 10.3 fusion.174
  293.0 10.3 fusion.174
  312.4 15.6 all-gather.29.cloned.1.call-done
  333.6 65.3 %all-gather.31.cloned.1.call-done = bf16[1024,3072]{1,0:T(8,128)(2,1)} async-done(((bf16[32,3072]{1,0:T(8,128)(2,1)}), bf16[1024,3072]{1,0:T(8,128)(2,1)}) %all-gather.31.cloned.1.call-update) | async-done | bytes 6291472 | tf_op jit(solution)/shard_map/all_gather | solution.py:177
  398.9 8.3 fusion.47
  407.1 62.3 %all-gather.35.cloned.1.call-done = bf16[3072,1024]{1,0:T(8,128)(2,1)} async-done(((bf16[96,1024]{1,0:T(8,128)(2,1)}), bf16[3072,1024]{1,0:T(8,128)(2,1)}) %all-gather.35.cloned.1.call-update) | async-done | bytes 6291472 | tf_op jit(solution)/shard_map/all_gather | solution.py:179
  469.4 70.6 %all-gather.33.cloned.1.call-done = bf16[1024,3072]{1,0:T(8,128)(2,1)} async-done(((bf16[32,3072]{1,0:T(8,128)(2,1)}), bf16[1024,3072]{1,0:T(8,128)(2,1)}) %all-gather.33.cloned.1.call-update) | async-done | bytes 6291472 | tf_op jit(solution)/shard_map/all_gather | solution.py:178
  540.0 15.4 fusion.45
  557.3 39.4 %all-reduce.10 = (bf16[1024]{0:T(1024)(128)(2,1)S(1)}, bf16[1024]{0:T(1024)(128)(2,1)S(1)}) all-reduce(bf16[1024]{0:T(1024)(128)(2,1)S(1)} %dynamic-update-slice.2, bf16[1024]{0:T(1024)(128)(2,1)S(1)} %dynamic-update-slice.3), channel_id=1, replica_groups=mesh['dp'=8,'seq'=4] {'dp','seq'}, use_global_device_ids=true, to_apply=%add.6 | all-reduce | flops 2048 | bytes 8192
  597.2 13.3 all-gather.39.cloned.1.call-done
  617.1 51.4 %all-gather.43.cloned.1.call-done = bf16[1024,1024]{1,0:T(8,128)(2,1)} async-done(((bf16[32,1024]{1,0:T(8,128)(2,1)}), bf16[1024,1024]{1,0:T(8,128)(2,1)}) %all-gather.43.cloned.1.call-update) | async-done | bytes 2097168 | tf_op jit(solution)/shard_map/all_gather | solution.py:199
  697.6 34.2 %all-gather.47.cloned.1.call-done = bf16[1024,2048]{1,0:T(8,128)(2,1)} async-done(((bf16[32,2048]{1,0:T(8,128)(2,1)}), bf16[1024,2048]{1,0:T(8,128)(2,1)}) %all-gather.47.cloned.1.call-update) | async-done | bytes 4194320 | tf_op jit(solution)/shard_map/all_gather | solution.py:198
  765.2 9.3 add_convert_fusion
  777.6 26.0 all-gather.45.cloned.1.call-done
  805.1 63.6 %while.40 = (s32[]{:T(128)}, bf16[2,256,2048]{2,1,0:T(8,128)(2,1)}, f32[2,8,2,256,1]{3,2,1,4,0:T(2,128)S(1)}, bf16[2,1024,1024]{1,2,0:T(8,128)(2,1)}, bf16[2,102...) while((s32[]{:T(128)}, bf16[2,256,2048]{2,1,0:T(8,128)(2,1)}, ...), condition=%wide.region_14.15_spmd.clone, body=%wide.region_11.14_spmd.clone.sunk | while | flops 2198597888 | bytes 72484968 | solution.py:119
  808.5 7.4 fusion.179
  815.9 9.1 fusion.180
  825.0 9.3 fusion.181
  847.1 9.7 fusion.180
  856.8 9.4 fusion.181
  876.3 62.4 %all-gather.53.cloned.1.call-done = bf16[1024,3072]{1,0:T(8,128)(2,1)} async-done(((bf16[32,3072]{1,0:T(8,128)(2,1)}), bf16[1024,3072]{1,0:T(8,128)(2,1)}) %all-gather.53.cloned.1.call-update) | async-done | bytes 6291472 | tf_op jit(solution)/shard_map/all_gather | solution.py:203
  938.7 8.0 fusion.73
  946.8 62.4 %all-gather.51.cloned.1.call-done = bf16[1024,3072]{1,0:T(8,128)(2,1)} async-done(((bf16[32,3072]{1,0:T(8,128)(2,1)}), bf16[1024,3072]{1,0:T(8,128)(2,1)}) %all-gather.51.cloned.1.call-update) | async-done | bytes 6291472 | tf_op jit(solution)/shard_map/all_gather | solution.py:204
  1009.2 8.2 fusion.72
  1017.4 62.2 %all-gather.37.cloned.1.call-done = bf16[3072,1024]{1,0:T(8,128)(2,1)} async-done(((bf16[96,1024]{1,0:T(8,128)(2,1)}), bf16[3072,1024]{1,0:T(8,128)(2,1)}) %all-gather.37.cloned.1.call-update) | async-done | bytes 6291472 | tf_op jit(solution)/shard_map/all_gather | solution.py:205
  1079.6 10.3 fusion.33
  1090.0 7.9 fusion.74
  1108.1 241.6 %while.41 = (s32[]{:T(128)}, f32[2,256,2048]{1,0,2:T(2,128)}, bf16[2,1024,1024]{1,2,0:T(8,128)(2,1)}, bf16[2,1024,1024]{2,1,0:T(8,128)(2,1)}, bf16[2,1024,1024]{...) while((s32[]{:T(128)}, f32[2,256,2048]{1,0,2:T(2,128)}, ...), condition=%wide.region_19.20_spmd.clone, body=%wide.region_17.19_spmd.clone.sunk | while | flops 5409337344 | bytes 279529856 | solution.py:267
  1116.4 10.1 fusion.192
  1128.0 12.4 fusion.193
  1140.4 11.5 fusion.194
  1155.3 8.5 copy.191
  1163.7 42.0 %dynamic_update_slice.44 = f32[2,256,2048]{1,0,2:T(2,128)} dynamic-update-slice(f32[2,256,2048]{1,0,2:T(2,128)} %get-tuple-element.611, f32[1,256,2048]{1,0,2:T(1,128)S(1)} %copy.191, s32[]{:T(128)S(6)} %copy.222, s32[]{:T(128)} %constant.99.clone.1..sunk, s32[]{:T(128)} %constant.99.clone.1..sunk) | dynamic-update-slice | bytes 4194308 | tf_op jit(solution)/shard_map/while/body/jit(dynamic_update_index_in_dim)/dynamic_update_slice | solution.py:267
  1214.3 8.6 fusion.195
  1236.9 10.1 fusion.192
  1248.5 12.4 fusion.193
  1260.9 11.5 fusion.194
  1275.7 8.5 copy.191
  1284.2 42.0 %dynamic_update_slice.44 = f32[2,256,2048]{1,0,2:T(2,128)} dynamic-update-slice(f32[2,256,2048]{1,0,2:T(2,128)} %get-tuple-element.611, f32[1,256,2048]{1,0,2:T(1,128)S(1)} %copy.191, s32[]{:T(128)S(6)} %copy.222, s32[]{:T(128)} %constant.99.clone.1..sunk, s32[]{:T(128)} %constant.99.clone.1..sunk) | dynamic-update-slice | bytes 4194308 | tf_op jit(solution)/shard_map/while/body/jit(dynamic_update_index_in_dim)/dynamic_update_slice | solution.py:267
  1334.8 8.6 fusion.195
  1374.6 7.7 reshape.486
  1389.6 7.6 reshape.489
  1397.3 9.1 fusion.80
  1406.4 10.1 reshape.491
  1416.5 8.4 fusion.81
  1424.9 10.1 reshape.492
  1435.0 11.5 fusion.38
  1446.5 10.0 reshape.493
  1495.7 25.9 dynamic-update-slice.5
  1521.7 14.8 dynamic-update-slice.6
  1536.5 14.8 dynamic-update-slice.7
  1551.3 25.9 dynamic-update-slice.8
  1578.8 37.1 %dynamic-update-slice.10 = f32[32,491584]{1,0:T(8,128)} dynamic-update-slice(f32[32,491584]{1,0:T(8,128)} %dynamic-update-slice.9, f32[32,98304]{1,0:T(8,128)} %reshape.491, s32[]{} %constant.154, s32[]{} %constant.160) | dynamic-update-slice | bytes 25165828
  1615.8 37.1 %dynamic-update-slice.11 = f32[32,491584]{1,0:T(8,128)} dynamic-update-slice(f32[32,491584]{1,0:T(8,128)} %dynamic-update-slice.10, f32[32,98304]{1,0:T(8,128)} %reshape.492, s32[]{} %constant.154, s32[]{} %constant.161) | dynamic-update-slice | bytes 25165828
  1652.9 36.7 %dynamic-update-slice.12 = f32[32,491584]{1,0:T(8,128)} dynamic-update-slice(f32[32,491584]{1,0:T(8,128)} %dynamic-update-slice.11, f32[32,98304]{1,0:T(8,128)} %reshape.493, s32[]{} %constant.154, s32[]{} %constant.162) | dynamic-update-slice | bytes 25165828 | tf_op jit(solution)/shard_map/concatenate | solution.py:313
  1689.7 41.9 %all-reduce.9 = (f32[128]{0:T(128)}, f32[128]{0:T(128)}) all-reduce(f32[128]{0:T(128)S(1)} %get-tuple-element.284, f32[128]{0:T(128)S(1)} %get-tuple-element.290), channel_id=1, replica_groups=mesh['dp'=8,'seq'=4] {'dp','seq'}, use_global_device_ids=true, to_apply=%region_29.30 | all-reduce | flops 256 | bytes 2048 | tf_op jit(solution)/shard_map/psum | solution.py:325
  1735.0 862.6 %all-reduce.14.cloned.1.call-done = f32[32,491584]{1,0:T(8,128)} async-done(((f32[32,491584]{1,0:T(8,128)}), f32[32,491584]{1,0:T(8,128)}) %all-reduce.14.cloned.1.call-update) | async-done | bytes 62922768
  (402 shorter events, 344.7 us)
Async XLA Ops:
  7.2 62.7 %all-gather.19.cloned.1.call-start = ((), (), s32[]{:S(2)}) async-start(), calls=%async_computation.2 | async-start | bytes 2162688 | tf_op jit(solution)/shard_map/all_gather | solution.py:174
  7.9 119.9 %all-gather.23.cloned.1.call-start = ((), (), s32[]{:S(2)}) async-start(), calls=%async_computation.4 | async-start | bytes 2162688 | tf_op jit(solution)/shard_map/all_gather | solution.py:173
  8.7 182.7 %all-gather.27.cloned.1.call-start = ((), (), s32[]{:S(2)}) async-start(), calls=%async_computation.6 | async-start | bytes 4325376 | tf_op jit(solution)/shard_map/all_gather | solution.py:172
  9.4 217.7 %all-gather.21.cloned.1.call-start = ((), (), s32[]{:S(2)}) async-start(), calls=%async_computation.3 | async-start | bytes 5242880 | tf_op jit(solution)/shard_map/all_gather | solution.py:191
  55.4 17.8 copy-start.60
  74.5 189.1 %all-gather.25.cloned.1.call-start = ((), (), s32[]{:S(2)}) async-start(), calls=%async_computation.5 | async-start | bytes 5242880 | tf_op jit(solution)/shard_map/all_gather | solution.py:191
  74.6 60.8 %copy-start.54 = (f32[128]{0:T(128)}, f32[128]{0:T(128)S(1)}, u32[]{:S(2)}) copy-start(f32[128]{0:T(128)S(1)} %convert_element_type.196) | copy-start | bytes 1540
  75.7 128.8 %copy-start.18 = (f32[512,128]{0,1:T(8,128)}, f32[512,128]{0,1:T(8,128)S(1)}, u32[]{:S(2)}) copy-start(f32[512,128]{0,1:T(8,128)S(1)} %get-tuple-element.374) | copy-start | bytes 786436
  75.7 128.8 %copy-start.21 = (f32[512,128]{0,1:T(8,128)}, f32[512,128]{0,1:T(8,128)S(1)}, u32[]{:S(2)}) copy-start(f32[512,128]{0,1:T(8,128)S(1)} %get-tuple-element.375) | copy-start | bytes 786436
  76.0 58.6 %copy-start.34 = (bf16[2,256,1024]{2,1,0:T(8,128)(2,1)}, bf16[2,256,1024]{2,1,0:T(8,128)(2,1)S(1)}, u32[]{:S(2)}) copy-start(bf16[2,256,1024]{2,1,0:T(8,128)(2,1)S(1)} %multiply_convert_fusion.6) | copy-start | bytes 3145732
  138.5 5.8 copy-start.70
  139.6 188.4 %all-gather.29.cloned.1.call-start = ((), (), s32[]{:S(2)}) async-start(), calls=%async_computation.7 | async-start | bytes 4325376 | tf_op jit(solution)/shard_map/all_gather | solution.py:175
  140.2 258.6 %all-gather.31.cloned.1.call-start = ((), (), s32[]{:S(2)}) async-start(), calls=%async_computation.8 | async-start | bytes 6488064 | tf_op jit(solution)/shard_map/all_gather | solution.py:177
  141.0 328.5 %all-gather.35.cloned.1.call-start = ((), (), s32[]{:S(2)}) async-start(), calls=%async_computation.10 | async-start | bytes 6488064 | tf_op jit(solution)/shard_map/all_gather | solution.py:179
  141.7 398.3 %all-gather.33.cloned.1.call-start = ((), (), s32[]{:S(2)}) async-start(), calls=%async_computation.9 | async-start | bytes 6488064 | tf_op jit(solution)/shard_map/all_gather | solution.py:178
  142.4 468.1 %all-gather.39.cloned.1.call-start = ((), (), s32[]{:S(2)}) async-start(), calls=%async_computation.12 | async-start | bytes 2162688 | tf_op jit(solution)/shard_map/all_gather | solution.py:200
  144.3 60.2 %copy-start.57 = (f32[128]{0:T(128)}, f32[128]{0:T(128)S(1)}, u32[]{:S(2)}) copy-start(f32[128]{0:T(128)S(1)} %convert_element_type.202) | copy-start | bytes 1540
  191.3 6.6 copy-start.35
  265.1 4.3 copy-start.10
  288.6 4.3 copy-start.10
  328.0 70.8 %copy-start.63 = (f32[1024]{0:T(1024)S(1)}, f32[1024]{0:T(1024)}, u32[]{:S(2)}) copy-start(f32[1024]{0:T(1024)} %convert_element_type.205) | copy-start | bytes 12292
  333.6 65.3 %copy-start.75 = (f32[512,1024]{1,0:T(8,128)}, f32[512,1024]{1,0:T(8,128)S(1)}, u32[]{:S(2)}) copy-start(f32[512,1024]{1,0:T(8,128)S(1)} %get-tuple-element.383) | copy-start | bytes 6291460
  407.1 149.7 %copy-start.71 = (bf16[32]{0:T(256)(128)(2,1)S(1)}, bf16[32]{0:T(256)(128)(2,1)}, u32[]{:S(2)}) copy-start(bf16[32]{0:T(256)(128)(2,1)} %param.20) | copy-start | bytes 196
  407.1 150.0 %copy-start.72 = (bf16[32]{0:T(256)(128)(2,1)S(1)}, bf16[32]{0:T(256)(128)(2,1)}, u32[]{:S(2)}) copy-start(bf16[32]{0:T(256)(128)(2,1)} %param.27) | copy-start | bytes 196
  407.1 189.6 %copy-start.11 = (f32[512,1024]{1,0:T(8,128)S(1)}, f32[512,1024]{1,0:T(8,128)}, u32[]{:S(2)}) copy-start(f32[512,1024]{1,0:T(8,128)} %bitcast_convert_fusion) | copy-start | bytes 6291460
  555.5 113.0 %all-gather.43.cloned.1.call-start = ((), (), s32[]{:S(2)}) async-start(), calls=%async_computation.14 | async-start | bytes 2162688 | tf_op jit(solution)/shard_map/all_gather | solution.py:199
  556.2 175.6 %all-gather.47.cloned.1.call-start = ((), (), s32[]{:S(2)}) async-start(), calls=%async_computation.16 | async-start | bytes 4325376 | tf_op jit(solution)/shard_map/all_gather | solution.py:198
  556.8 220.8 %all-gather.41.cloned.1.call-start = ((), (), s32[]{:S(2)}) async-start(), calls=%async_computation.13 | async-start | bytes 5242880 | tf_op jit(solution)/shard_map/all_gather | solution.py:217
  596.7 13.8 copy-start.49
  597.2 71.3 %copy-start.26 = (bf16[512,1024]{1,0:T(8,128)(2,1)}, bf16[512,1024]{1,0:T(8,128)(2,1)S(1)}, u32[]{:S(2)}) copy-start(bf16[512,1024]{1,0:T(8,128)(2,1)S(1)} %multiply_convert_fusion.4) | copy-start | bytes 3145732
  614.7 188.9 %all-gather.45.cloned.1.call-start = ((), (), s32[]{:S(2)}) async-start(), calls=%async_computation.15 | async-start | bytes 5242880 | tf_op jit(solution)/shard_map/all_gather | solution.py:217
  687.1 181.6 %all-gather.49.cloned.1.call-start = ((), (), s32[]{:S(2)}) async-start(), calls=%async_computation.17 | async-start | bytes 4325376 | tf_op jit(solution)/shard_map/all_gather | solution.py:201
  687.7 251.0 %all-gather.53.cloned.1.call-start = ((), (), s32[]{:S(2)}) async-start(), calls=%async_computation.19 | async-start | bytes 6488064 | tf_op jit(solution)/shard_map/all_gather | solution.py:203
  688.3 320.9 %all-gather.51.cloned.1.call-start = ((), (), s32[]{:S(2)}) async-start(), calls=%async_computation.18 | async-start | bytes 6488064 | tf_op jit(solution)/shard_map/all_gather | solution.py:204
  688.9 390.7 %all-gather.37.cloned.1.call-start = ((), (), s32[]{:S(2)}) async-start(), calls=%async_computation.11 | async-start | bytes 6488064 | tf_op jit(solution)/shard_map/all_gather | solution.py:205
  691.4 5.5 copy-start.58
  691.5 40.3 %copy-start.27 = (bf16[512,1024]{1,0:T(8,128)(2,1)S(1)}, bf16[512,1024]{1,0:T(8,128)(2,1)}, u32[]{:S(2)}) copy-start(bf16[512,1024]{1,0:T(8,128)(2,1)} %copy-done.26) | copy-start | bytes 3145732
  697.5 758.9 %reduce-scatter.3.cloned.1.call-start = ((), (), s32[]{:S(2)}) async-start(), calls=%async_computation.20 | async-start | bytes 5242880 | tf_op jit(solution)/shard_map/reduce_scatter | solution.py:272
  747.4 9.8 copy-start.41
  868.8 7.3 copy-start.51
  876.3 132.9 %copy-start.36 = (bf16[512,1024]{1,0:T(8,128)(2,1)}, bf16[512,1024]{1,0:T(8,128)(2,1)S(1)}, u32[]{:S(2)}) copy-start(bf16[512,1024]{1,0:T(8,128)(2,1)S(1)} %multiply_convert_fusion.3) | copy-start | bytes 3145732
  1090.0 7.9 copy-start.74
  1090.0 7.9 copy-start.73
  1090.0 7.9 copy-start.25
  1090.0 7.9 copy-start.64
  1097.9 4.3 copy-start.38
  1109.7 4.2 copy-start.17
  1116.4 10.1 copy-start.1
  1205.7 6.4 copy-start.30
  1230.1 4.2 copy-start.17
  1236.9 10.1 copy-start.1
  1326.2 6.4 copy-start.30
  1349.7 121.1 %reduce-scatter.5.cloned.1.call-start = ((), (), s32[]{:S(2)}) async-start(), calls=%async_computation.21 | async-start | bytes 5242880 | tf_op jit(solution)/shard_map/reduce_scatter | solution.py:275
  1350.3 1247.3 %all-reduce.14.cloned.1.call-start = ((), (), s32[]{:S(2)}) async-start(), calls=%async_computation.22 | async-start | bytes 125861888
  1350.4 6.7 copy-start.23
  1357.1 3.8 copy-start.42
  1374.6 7.7 copy-start.13
  1389.6 7.6 copy-start.62
  1389.6 7.7 copy-start.37
  1424.9 10.1 copy-start.39
  1470.8 4.6 copy-start.40
  1470.9 4.6 copy-start.67
  1689.6 41.9 %copy-start.53 = (f32[1,2,2,128]{3,1,2,0:T(2,128)S(1)}, f32[1,2,2,128]{3,1,2,0:T(2,128)}, u32[]{:S(2)}) copy-start(f32[1,2,2,128]{3,1,2,0:T(2,128)} %copy-done.52) | copy-start | bytes 6148
  1689.6 41.9 %copy-start.14 = (f32[512,1024]{1,0:T(8,128)S(1)}, f32[512,1024]{1,0:T(8,128)}, u32[]{:S(2)}) copy-start(f32[512,1024]{1,0:T(8,128)} %copy-done.12) | copy-start | bytes 6291460
  (42 other events, 90.0 us)
Sparse Core Ops, SparseCore 0:
  10.8 59.0 all-gather.18
  72.8 55.0 all-gather.22
  130.7 60.5 all-gather.26
  193.3 33.7 all-gather.20
  228.5 34.9 all-gather.24
  266.3 61.7 all-gather.28
  330.9 67.9 all-gather.30
  401.7 67.6 all-gather.34
  472.3 67.6 all-gather.32
  555.6 54.8 all-gather.38
  613.4 55.0 all-gather.42
  671.2 60.5 all-gather.46
  733.3 33.7 all-gather.40
  768.5 34.9 all-gather.44
  806.3 61.7 all-gather.48
  870.8 67.9 all-gather.52
  941.4 67.6 all-gather.50
  1011.9 67.6 all-gather.36
  1349.8 42.9 reduce-scatter.2
  1395.2 44.5 reduce-scatter.4
  1689.8 907.7 all-reduce.13
where the time goes:
time: 2640 us; the launch traced here: 2620 us
  waiting for transfers between devices  1560 us (59%)
  local copies, waits for them, and re-layouts  524 us (20%)
  matrix products  305 us (12%)
  blocking collectives  123 us (5%)
  other arithmetic  92.5 us (4%)
    unnamed x22, waiting for transfers between devices  871 us
    unnamed x155, local copies, waits for them, and re-layouts  179 us
    dynamic_update_slice x10, local copies, waits for them, and re-layouts, body(): lax.map(lambda item: attention_backward(item[0], item[1], item[2], item[3...  113 us
    unnamed x2, blocking collectives  81.5 us
    all_gather x4, waiting for transfers between devices, body(): lax.all_gather(shortened(pair), 'seq', axis=1, tiled=True)  78.3 us
    all_gather x1, waiting for transfers between devices, body(): lax.all_gather(shards[7], ('dp', 'seq'), axis=0, tiled=True)  70.6 us
    all_gather x1, waiting for transfers between devices, body(): lax.all_gather(shards[6], ('dp', 'seq'), axis=0, tiled=True)  65.3 us
    all_gather x1, waiting for transfers between devices, body(): lax.all_gather(shards_again[6], ('dp', 'seq'), axis=0, tiled=True)  62.4 us
  transfers between devices with their start and end apart: 21, of which 17 were waited for; matrix products, arithmetic and copies ran while one was open for 15% of the time, Pallas kernels for 0%

commit v1 on v0

v1 whole, which is shorter than its diff:
```python
import functools

import jax
import jax.numpy as jnp
from jax import lax
from jax.experimental import pallas as pl
from jax.experimental.pallas import tpu as pltpu
from jax.sharding import PartitionSpec as P

HEAD_SIZE = 128
EPS = 1e-06
ROPE_THETA = 1000000.0
AXES = ("dp", "seq")
SCALE = HEAD_SIZE ** (-0.5)
F32 = jnp.float32
BF16 = jnp.bfloat16


def log2(n):
    return n.bit_length() - 1


class Wires:
    def __init__(self, dp, seq):
        self.dp, self.seq, self.count = dp, seq, dp * seq
        self.dp_bits, self.seq_bits = log2(dp), log2(seq)
        self.x_count = seq // 2
        y_bits = min(log2(self.x_count), self.dp_bits)
        self.dp_order = list(range(y_bits, self.dp_bits)) + list(range(y_bits))
        self.x_bits = list(range(1, self.seq_bits))
        self.d = lax.axis_index("dp")
        self.s = lax.axis_index("seq")

    def swap(self, value, mask, only=None):
        pairs = [(i, i ^ mask) for i in range(self.count) if only is None or only(i)]
        return lax.ppermute(value, AXES, pairs)

    def dp_swap(self, value, bit, only=None):
        return self.swap(value, (1 << bit) * self.seq, only)

    def bit_d(self, bit):
        return (self.d >> bit) & 1

    def bit_s(self, bit):
        return (self.s >> bit) & 1

    def gather_dp(self, shard):
        pieces = {0: shard}
        for bit in self.dp_order:
            pieces.update({r | (1 << bit): self.dp_swap(v, bit) for r, v in list(pieces.items())})
        full = jnp.zeros((self.dp,) + shard.shape, shard.dtype)
        for r, v in pieces.items():
            full = lax.dynamic_update_index_in_dim(full, v, self.d ^ r, 0)
        return full

    def scatter_dp(self, value):
        rest = value.shape[1:]
        held = list(range(self.dp_bits - 1, -1, -1))
        value = value.reshape((2,) * self.dp_bits + rest)
        for bit in reversed(self.dp_order):
            axis = held.index(bit)
            held.pop(axis)
            mine = lax.dynamic_index_in_dim(value, self.bit_d(bit), axis, keepdims=False)
            other = lax.dynamic_index_in_dim(value, 1 - self.bit_d(bit), axis, keepdims=False)
            got = self.dp_swap(other, bit)
            value = (mine.astype(F32) + got.astype(F32)).astype(BF16)
        return value

    def exchange_seq(self, value):
        rest = value.shape[1:]
        for bit in self.x_bits + [0]:
            value = value.reshape((self.seq >> (bit + 1), 2, 1 << bit) + rest)
            me = self.bit_s(bit)
            mine = lax.dynamic_index_in_dim(value, me, 1, keepdims=False)
            other = lax.dynamic_index_in_dim(value, 1 - me, 1, keepdims=False)
            got = self.swap(other, 1 << bit)
            low = jnp.where(me == 0, mine, got)
            high = jnp.where(me == 0, got, mine)
            value = jnp.stack([low, high], axis=1).reshape((self.seq,) + rest)
        return value

    def gather_seq_relative(self, value):
        pieces = [value]
        for bit in self.x_bits:
            pieces = pieces + [self.swap(v, 1 << bit) for v in pieces]
        return pieces + [self.swap(v, 1) for v in pieces]

    def sum_x(self, value):
        n = self.x_count
        shape = value.shape
        for bit in self.x_bits:
            got = self.swap(value.astype(BF16), 1 << bit).astype(F32)
            blocks = got.reshape((n, shape[0] // n) + shape[1:])
            flip = [i ^ (1 << (bit - 1)) for i in range(n)]
            value = value + jnp.concatenate([blocks[i] for i in flip], axis=0)
        return value

    def scatter_x(self, value):
        n = self.x_count
        for bit in reversed(self.x_bits):
            half = value.shape[0] // 2
            got = self.swap(value[half:].astype(BF16), 1 << bit)
            value = value[:half] + got.astype(F32)
        return value

    def sum_all(self, value):
        for bit in range(log2(self.count)):
            value = value + self.swap(value, 1 << bit)
        return value

    def head_bits(self, heads_kv):
        low = self.dp_bits - log2(heads_kv)
        partner = {0: 1, 1: 0, 2: 2}
        matched = [(low + k, partner[k]) for k in range(self.seq_bits)]
        free = [low + k for k in range(self.seq_bits, log2(heads_kv))]
        return low, matched, free

    def heads_of(self, t, heads_kv):
        low, matched, free = self.head_bits(heads_kv)
        heads = [0]
        for bit, tbit in matched:
            heads = [h | (((t >> tbit) & 1) << (bit - low)) for h in heads]
        for bit in free:
            heads = heads + [h | (1 << (bit - low)) for h in heads]
        return heads

    def matches(self, i, pairs):
        return all(((i // self.seq) >> b) & 1 == (i >> t) & 1 for b, t in pairs)

    def gather_out(self, shard, heads_kv):
        low, matched, free = self.head_bits(heads_kv)
        value = shard
        for bit in self.x_bits + [0]:
            pass
        value = shard[None]
        for bit in [0] + self.x_bits:
            got = self.swap(value, 1 << bit)
            value = self.ordered(value, got, self.bit_s(bit))
        for bit in range(low):
            got = self.dp_swap(value, bit)
            value = self.ordered(value, got, self.bit_d(bit))
        for n, (bit, tbit) in enumerate(matched):
            got = self.dp_swap(value, bit, lambda i: self.matches(i, matched[n:]))
            value = jnp.where(self.bit_d(bit) == self.bit_s(tbit), value, got)
        for bit in free:
            got = self.dp_swap(value, bit)
            value = self.ordered(value, got, self.bit_d(bit))
        return value.reshape((-1,) + shard.shape[1:])

    def ordered(self, own, got, bit):
        return jnp.concatenate(
            [jnp.where(bit == 0, own, got), jnp.where(bit == 0, got, own)], axis=0
        )

    def halves(self, value, bit):
        half = value.shape[0] // 2
        mine = lax.dynamic_slice_in_dim(value, bit * half, half, 0)
        other = lax.dynamic_slice_in_dim(value, (1 - bit) * half, half, 0)
        return mine, other

    def scatter_out(self, value, heads_kv):
        low, matched, free = self.head_bits(heads_kv)
        for bit in reversed(free):
            mine, other = self.halves(value, self.bit_d(bit))
            got = self.dp_swap(other, bit)
            value = (mine.astype(F32) + got.astype(F32)).astype(BF16)
        for n in reversed(range(len(matched))):
            bit, tbit = matched[n]
            got = self.dp_swap(
                value,
                bit,
                lambda i: self.matches(i, matched[n + 1 :]) and not self.matches(i, [matched[n]]),
            )
            value = (value.astype(F32) + got.astype(F32)).astype(BF16)
        for bit in reversed(range(low)):
            mine, other = self.halves(value, self.bit_d(bit))
            got = self.dp_swap(other, bit, lambda i: self.matches(i, matched))
            value = (mine.astype(F32) + got.astype(F32)).astype(BF16)
        todo = dict((tbit, bit) for bit, tbit in matched)
        for tbit in reversed(self.x_bits):
            value = self.hand_out(value, tbit, todo)
        return self.hand_out(value, 0, todo)

    def hand_out(self, value, tbit, todo):
        bit = todo.pop(tbit)
        left = [(b, t) for t, b in todo.items()]
        mine, other = self.halves(value, self.bit_s(tbit))
        got = self.swap(
            other, 1 << tbit, lambda i: self.matches(i, left) and self.matches(i, [(bit, tbit)])
        )
        return jnp.where(self.bit_d(bit) == self.bit_s(tbit), mine, got)


def dot(a, b):
    return lax.dot_general(a, b, (((1,), (0,)), ((), ())), preferred_element_type=F32)


def dot_t(a, b):
    return lax.dot_general(a, b, (((1,), (1,)), ((), ())), preferred_element_type=F32)


def t_dot(a, b):
    return lax.dot_general(a, b, (((0,), (0,)), ((), ())), preferred_element_type=F32)


def rms_scale(rows):
    return lax.rsqrt(jnp.mean(rows * rows, axis=-1, keepdims=True) + EPS)


def rope_tables(length):
    halfway = HEAD_SIZE // 2
    inverse = jnp.power(F32(ROPE_THETA), -(jnp.arange(halfway).astype(F32) * 2.0) / HEAD_SIZE)
    angles = jnp.arange(length).astype(F32)[:, None] * inverse[None, :]
    cosine, sine = jnp.cos(angles), jnp.sin(angles)
    return (
        jnp.concatenate([cosine, cosine], axis=-1),
        jnp.concatenate([-sine, sine], axis=-1),
    )


def place(block, s, x_count):
    return ((block & 1) ^ (s & 1)) * x_count + ((block >> 1) ^ (s >> 1))


def project_kernel(s_ref, x_ref, w_ref, gain_ref, qg_ref, kg_ref, cos_ref, sin_ref, n_ref, qkv_ref, pre_ref):
    x = x_ref[0].astype(F32)
    normed = (x * rms_scale(x) * gain_ref[...]).astype(BF16)
    n_ref[0] = normed
    y = dot(normed, w_ref[...])
    cosine, sine = cos_ref[...], sin_ref[...]
    for j in range(y.shape[1] // (4 * HEAD_SIZE)):
        for part in range(4):
            at = slice((4 * j + part) * HEAD_SIZE, (4 * j + part + 1) * HEAD_SIZE)
            head = y[:, at]
            if part < 3:
                pre_ref[:, (3 * j + part) * HEAD_SIZE : (3 * j + part + 1) * HEAD_SIZE] = head
                gain = qg_ref[...] if part < 2 else kg_ref[...]
                head = head * rms_scale(head) * gain
                head = head * cosine + pltpu.roll(head, HEAD_SIZE // 2, 1) * sine
            qkv_ref[:, at] = head.astype(BF16)


def project(s, x_rel, w, gain, query_gain, key_gain, cosine, sine, x_count):
    blocks, piece, width = x_rel.shape
    length, columns = blocks * piece, w.shape[1]
    heads = columns // (4 * HEAD_SIZE)
    whole = lambda shape: pl.BlockSpec(shape, lambda i, s_ref: (0,) * len(shape))
    rel = pl.BlockSpec((1, piece, width), lambda i, s_ref: (place(i, s_ref[0], x_count), 0, 0))
    table = pl.BlockSpec((piece, HEAD_SIZE), lambda i, s_ref: (i, 0))
    return pl.pallas_call(
        project_kernel,
        name="project",
        out_shape=(
            jax.ShapeDtypeStruct((blocks, piece, width), BF16),
            jax.ShapeDtypeStruct((length, columns), BF16),
            jax.ShapeDtypeStruct((length, 3 * heads * HEAD_SIZE), F32),
        ),
        grid_spec=pltpu.PrefetchScalarGridSpec(
            num_scalar_prefetch=1,
            grid=(blocks,),
            in_specs=[
                rel,
                whole(w.shape),
                whole((1, width)),
                whole((1, HEAD_SIZE)),
                whole((1, HEAD_SIZE)),
                table,
                table,
            ],
            out_specs=[
                rel,
                pl.BlockSpec((piece, columns), lambda i, s_ref: (i, 0)),
                pl.BlockSpec((piece, 3 * heads * HEAD_SIZE), lambda i, s_ref: (i, 0)),
            ],
        ),
        cost_estimate=pl.CostEstimate(
            flops=2 * length * width * columns,
            bytes_accessed=2 * (2 * length * width + width * columns + 4 * length * columns),
            transcendentals=0,
        ),
    )(s, x_rel, w, gain, query_gain, key_gain, cosine, sine)


def masked_exp(k_ref, query, i, piece, offset):
    diagonal = dot_t(k_ref[i * piece : (i + 1) * piece, :], query) * SCALE
    key_at = lax.broadcasted_iota(jnp.int32, (piece, piece), 0)
    query_at = lax.broadcasted_iota(jnp.int32, (piece, piece), 1)
    diagonal = jnp.where(key_at <= query_at, diagonal, -jnp.inf)
    if i == 0:
        scores = diagonal
    else:
        scores = jnp.concatenate(
            [dot_t(k_ref[: i * piece, :], query) * SCALE, diagonal], axis=0
        )
    if offset is None:
        offset = jnp.max(scores, axis=0, keepdims=True)
    return jnp.exp(scores - offset), offset


def forward_kernel(blocks, x_count, s_ref, q_ref, k_ref, v_ref, o_ref, log_ref):
    piece = q_ref.shape[0] // blocks
    values_t = v_ref[...].T
    for i in range(blocks):
        query = q_ref[i * piece : (i + 1) * piece, :]
        exponent, highest = masked_exp(k_ref, query, i, piece, None)
        total = jnp.sum(exponent, axis=0, keepdims=True)
        probs = (exponent * (1.0 / total)).astype(BF16)
        mixed = dot(values_t[:, : (i + 1) * piece], probs)
        o_ref[place(i, s_ref[0], x_count)] = mixed.T.astype(BF16)
        log_ref[0, :, i * piece : (i + 1) * piece] = highest + jnp.log(total)


def attend(s, qkv, blocks, x_count):
    length, columns = qkv.shape
    heads = columns // (2 * HEAD_SIZE)
    piece = length // blocks
    head = lambda part: pl.BlockSpec(
        (length, HEAD_SIZE), lambda h, s_ref: (0, 4 * (h // 2) + (h % 2 if part == 0 else part))
    )
    return pl.pallas_call(
        functools.partial(forward_kernel, blocks, x_count),
        name="attend",
        out_shape=(
            jax.ShapeDtypeStruct((blocks, piece, heads * HEAD_SIZE), BF16),
            jax.ShapeDtypeStruct((heads, 1, length), F32),
        ),
        grid_spec=pltpu.PrefetchScalarGridSpec(
            num_scalar_prefetch=1,
            grid=(heads,),
            in_specs=[head(0), head(2), head(3)],
            out_specs=[
                pl.BlockSpec((blocks, piece, HEAD_SIZE), lambda h, s_ref: (0, 0, h)),
                pl.BlockSpec((1, 1, length), lambda h, s_ref: (h, 0, 0)),
            ],
        ),
        cost_estimate=pl.CostEstimate(
            flops=2 * heads * length * length * HEAD_SIZE * 2,
            bytes_accessed=2 * heads * length * HEAD_SIZE * 4,
            transcendentals=heads * length * length // 2,
        ),
    )(s, qkv, qkv, qkv)


def head_back(grad, pre, gain, cosine, sine):
    turned = grad * cosine - pltpu.roll(grad, HEAD_SIZE // 2, 1) * sine
    scale = rms_scale(pre)
    part = turned * gain
    result = scale * part - pre * (scale * scale * scale * jnp.mean(part * pre, axis=-1, keepdims=True))
    return result, jnp.sum(turned * pre * scale, axis=0, keepdims=True)


def backward_kernel(
    blocks, x_count, s_ref, q_ref, k_ref, v_ref, do_ref, log_ref, qp_ref, kp_ref, qg_ref, kg_ref,
    cos_ref, sin_ref, grad_ref, qgain_ref, kgain_ref, dk_ref, dv_ref,
):
    piece = q_ref.shape[0] // blocks
    second = pl.program_id(1)

    @pl.when((pl.program_id(0) == 0) & (second == 0))
    def _():
        qgain_ref[...] = jnp.zeros_like(qgain_ref)
        kgain_ref[...] = jnp.zeros_like(kgain_ref)

    @pl.when(second == 0)
    def _():
        dk_ref[...] = jnp.zeros_like(dk_ref)
        dv_ref[...] = jnp.zeros_like(dv_ref)

    keys_t = k_ref[...].T
    column = pl.ds(pl.multiple_of(second * HEAD_SIZE, HEAD_SIZE), HEAD_SIZE)
    for i in range(blocks):
        rows = slice(i * piece, (i + 1) * piece)
        end = (i + 1) * piece
        at = place(i, s_ref[0], x_count)
        query = q_ref[rows, :]
        grad_out = do_ref[at]
        probs, _ = masked_exp(k_ref, query, i, piece, log_ref[0, :, rows])
        dv_ref[:end, :] += dot(probs.astype(BF16), grad_out)
        grad_probs = dot_t(v_ref[:end, :], grad_out)
        inner = jnp.sum(probs * grad_probs, axis=0, keepdims=True)
        grad_scores = (probs * (grad_probs - inner)).astype(BF16)
        dk_ref[:end, :] += dot(grad_scores, query)
        grad_query = dot(keys_t[:, :end], grad_scores).T * SCALE
        result, gain = head_back(grad_query, qp_ref[rows, :], qg_ref[...], cos_ref[rows, :], sin_ref[rows, :])
        grad_ref[at, :, column] = result.astype(BF16)
        qgain_ref[...] += gain

    @pl.when(second == 1)
    def _():
        for i in range(blocks):
            rows = slice(i * piece, (i + 1) * piece)
            at = place(i, s_ref[0], x_count)
            result, gain = head_back(
                dk_ref[rows, :] * SCALE, kp_ref[rows, :], kg_ref[...], cos_ref[rows, :], sin_ref[rows, :]
            )
            grad_ref[at, :, 2 * HEAD_SIZE : 3 * HEAD_SIZE] = result.astype(BF16)
            grad_ref[at, :, 3 * HEAD_SIZE :] = dv_ref[rows, :].astype(BF16)
            kgain_ref[...] += gain


def attend_back(s, qkv, pre, log_total, grad_mixed, query_gain, key_gain, cosine, sine, blocks, x_count):
    length, columns = qkv.shape
    heads_kv = columns // (4 * HEAD_SIZE)
    piece = length // blocks
    head = lambda part: pl.BlockSpec(
        (length, HEAD_SIZE), lambda j, g, s_ref: (0, 4 * j + (g if part == 0 else part))
    )
    pre_head = lambda part: pl.BlockSpec(
        (length, HEAD_SIZE), lambda j, g, s_ref: (0, 3 * j + (g if part == 0 else part))
    )
    whole = lambda shape: pl.BlockSpec(shape, lambda j, g, s_ref: (0,) * len(shape))
    return pl.pallas_call(
        functools.partial(backward_kernel, blocks, x_count),
        name="attend_back",
        out_shape=(
            jax.ShapeDtypeStruct((blocks, piece, columns), BF16),
            jax.ShapeDtypeStruct((1, HEAD_SIZE), F32),
            jax.ShapeDtypeStruct((1, HEAD_SIZE), F32),
        ),
        grid_spec=pltpu.PrefetchScalarGridSpec(
            num_scalar_prefetch=1,
            grid=(heads_kv, 2),
            in_specs=[
                head(0),
                head(2),
                head(3),
                pl.BlockSpec((blocks, piece, HEAD_SIZE), lambda j, g, s_ref: (0, 0, 2 * j + g)),
                pl.BlockSpec((1, 1, length), lambda j, g, s_ref: (2 * j + g, 0, 0)),
                pre_head(0),
                pre_head(2),
                whole((1, HEAD_SIZE)),
                whole((1, HEAD_SIZE)),
                whole((length, HEAD_SIZE)),
                whole((length, HEAD_SIZE)),
            ],
            out_specs=[
                pl.BlockSpec((blocks, piece, 4 * HEAD_SIZE), lambda j, g, s_ref: (0, 0, j)),
                whole((1, HEAD_SIZE)),
                whole((1, HEAD_SIZE)),
            ],
            scratch_shapes=[pltpu.VMEM((length, HEAD_SIZE), F32), pltpu.VMEM((length, HEAD_SIZE), F32)],
        ),
        cost_estimate=pl.CostEstimate(
            flops=2 * 2 * heads_kv * length * length * HEAD_SIZE * 5 // 2,
            bytes_accessed=2 * heads_kv * length * HEAD_SIZE * 24,
            transcendentals=heads_kv * length * length,
        ),
    )(s, qkv, qkv, qkv, grad_mixed, log_total, pre, pre, query_gain, key_gain, cosine, sine)


def body(
    hidden_in,
    attn_gain,
    w_query,
    key_weight,
    value_weight,
    query_gain,
    key_gain,
    w_out,
    mlp_gain,
    w_gate,
    w_up,
    w_down,
    cotangent,
):
    wires = Wires(lax.axis_size("dp"), lax.axis_size("seq"))
    dp, seq, x_count = wires.dp, wires.seq, wires.x_count
    count = wires.count
    sequences, piece, width = hidden_in.shape
    length = seq * piece
    part = x_count * piece
    heads_kv = key_weight.shape[1] // HEAD_SIZE
    s_index = wires.s.reshape(1).astype(jnp.int32)
    cosine, sine = rope_tables(length)
    query_gain_row = query_gain.astype(F32).reshape(1, -1)
    key_gain_row = key_gain.astype(F32).reshape(1, -1)

    gains = jnp.zeros((2, count, width // count), BF16)
    own_gains = jnp.stack([attn_gain, mlp_gain]).reshape(2, 1, -1)
    index = wires.d * seq + wires.s
    gains = lax.dynamic_update_slice(gains, own_gains, (0, index, 0))
    gains = wires.sum_all(gains.reshape(2, width)).astype(F32)
    attn_gain_row, mlp_gain_row = gains[:1], gains[1:]

    rows = w_query.shape[0]
    by_head = jnp.concatenate(
        [
            w_query.reshape(rows, heads_kv, -1),
            key_weight.reshape(rows, heads_kv, -1),
            value_weight.reshape(rows, heads_kv, -1),
        ],
        axis=2,
    )
    order = [wires.heads_of(t, heads_kv) for t in range(seq)]
    package = jnp.stack([jnp.concatenate([by_head[:, j] for j in order[t]], axis=1) for t in range(seq)])
    package = wires.exchange_seq(package).reshape(seq * rows, -1)
    w_in = wires.gather_dp(package).reshape(width, -1)

    x_pieces = wires.gather_seq_relative(hidden_in)
    x_rel = jnp.stack(x_pieces, axis=1)

    w_o = wires.gather_out(w_out, heads_kv)

    down_rows = w_down.shape[0]

    def by_unit(w):
        return w.reshape(rows, dp, seq, down_rows).transpose(2, 0, 1, 3).reshape(seq, rows, -1)

    units = dp * down_rows
    package = jnp.concatenate([by_unit(w_gate), by_unit(w_up)], axis=2)
    package = wires.exchange_seq(package).reshape(seq * rows, -1)
    w_mlp = wires.gather_dp(package).reshape(width, -1)

    g_pieces = wires.gather_seq_relative(cotangent)
    g_rel = jnp.stack(g_pieces, axis=1)

    w_d = wires.gather_dp(w_down).reshape(units, width)

    kept = []
    outs = []
    for n in range(sequences):
        normed, qkv, pre = project(
            s_index, x_rel[n], w_in, attn_gain_row, query_gain_row, key_gain_row, cosine, sine, x_count
        )
        mixed, log_total = attend(s_index, qkv, seq, x_count)
        mixed_rows = mixed.reshape(length, -1)
        other = wires.swap(dot(mixed_rows[part:], w_o).astype(BF16), 1)
        total = wires.sum_x(dot(mixed_rows[:part], w_o) + other.astype(F32))
        residual = total + x_rel[n].reshape(length, width)[:part].astype(F32)
        scale = rms_scale(residual)
        normed_mlp = (residual * scale * mlp_gain_row).astype(BF16)
        normed_mlp = jnp.concatenate([normed_mlp, wires.swap(normed_mlp, 1)], axis=0)
        both = dot(normed_mlp, w_mlp)
        gate, upward = both[:, :units], both[:, units:]
        sigmoid = jax.nn.sigmoid(gate)
        silu = gate * sigmoid
        hidden = (silu * upward).astype(BF16)
        other = wires.swap(dot(hidden[part:], w_d).astype(BF16), 1)
        total = wires.scatter_x(dot(hidden[:part], w_d) + other.astype(F32))
        outs.append((residual[:piece] + total).astype(BF16))

        grad_top = g_rel[n].reshape(length, width)
        grad_hidden = dot_t(grad_top, w_d)
        grad_gate = (grad_hidden * upward * sigmoid * (1.0 + gate * (1.0 - sigmoid))).astype(BF16)
        grad_upward = (grad_hidden * silu).astype(BF16)
        grad_both = jnp.concatenate([grad_gate, grad_upward], axis=1)
        other = wires.swap(dot_t(grad_both[part:], w_mlp).astype(BF16), 1)
        grad_normed = wires.sum_x(dot_t(grad_both[:part], w_mlp) + other.astype(F32))
        scaled = grad_normed * mlp_gain_row
        grad_residual = (
            grad_top[:part].astype(F32)
            + scale * scaled
            - residual * (scale * scale * scale * jnp.mean(scaled * residual, axis=-1, keepdims=True))
        )
        grad_mlp_gain = jnp.sum((grad_normed * residual * scale)[:piece], axis=0)
        branch = grad_residual.astype(BF16)
        branch = jnp.concatenate([branch, wires.swap(branch, 1)], axis=0)
        grad_mixed = dot_t(branch, w_o).astype(BF16).reshape(mixed.shape)
        grad_qkv, grad_query_gain, grad_key_gain = attend_back(
            s_index, qkv, pre, log_total, grad_mixed, query_gain_row, key_gain_row, cosine, sine, seq, x_count
        )
        grad_rows = grad_qkv.reshape(length, -1)
        other = wires.swap(dot_t(grad_rows[part:], w_in).astype(BF16), 1)
        grad_first = wires.scatter_x(dot_t(grad_rows[:part], w_in) + other.astype(F32))
        tokens = hidden_in[n].astype(F32)
        scale = rms_scale(tokens)
        scaled = grad_first * attn_gain_row
        grad_tokens = (
            grad_residual[:piece]
            + scale * scaled
            - tokens * (scale * scale * scale * jnp.mean(scaled * tokens, axis=-1, keepdims=True))
        )
        grad_attn_gain = jnp.sum(grad_first * tokens * scale, axis=0)
        kept.append(
            dict(
                normed=normed.reshape(length, width),
                mixed=mixed_rows,
                normed_mlp=normed_mlp,
                hidden=hidden,
                grad_both=grad_both,
                branch=branch,
                grad_rows=grad_rows,
                grad_tokens=grad_tokens,
                gains=jnp.concatenate(
                    [grad_attn_gain, grad_mlp_gain, grad_query_gain[0], grad_key_gain[0]]
                ),
            )
        )

    def over(name):
        return jnp.concatenate([k[name] for k in kept], axis=0)

    grad_down = t_dot(over("hidden"), g_rel.reshape(-1, width)).astype(BF16)
    grad_down = wires.scatter_dp(grad_down.reshape(dp, down_rows, width)).astype(F32)

    grad_mlp = t_dot(over("normed_mlp"), over("grad_both")).astype(BF16)
    grad_mlp = wires.scatter_dp(grad_mlp.reshape(dp, seq * rows, -1))
    grad_mlp = wires.exchange_seq(grad_mlp.reshape(seq, rows, -1)).astype(F32)

    def from_unit(g):
        return g.reshape(seq, rows, dp, down_rows).transpose(1, 2, 0, 3).reshape(rows, -1)

    grad_gate, grad_up = from_unit(grad_mlp[..., :units]), from_unit(grad_mlp[..., units:])

    grad_out = t_dot(over("mixed"), over("branch")).astype(BF16)
    grad_out = wires.scatter_out(grad_out, heads_kv).astype(F32)

    grad_in = t_dot(over("normed"), over("grad_rows")).astype(BF16)
    grad_in = wires.scatter_dp(grad_in.reshape(dp, seq * rows, -1))
    grad_in = wires.exchange_seq(grad_in.reshape(seq, rows, -1)).astype(F32)
    pieces = [None] * heads_kv
    for t in range(seq):
        for m, j in enumerate(order[t]):
            pieces[j] = grad_in[t, :, m * 4 * HEAD_SIZE : (m + 1) * 4 * HEAD_SIZE]
    grad_query = jnp.concatenate([p[:, : 2 * HEAD_SIZE] for p in pieces], axis=1)
    grad_key = jnp.concatenate([p[:, 2 * HEAD_SIZE : 3 * HEAD_SIZE] for p in pieces], axis=1)
    grad_value = jnp.concatenate([p[:, 3 * HEAD_SIZE :] for p in pieces], axis=1)

    gain_sums = wires.sum_all(sum(k["gains"] for k in kept))
    own = width // count
    grad_attn_gain = lax.dynamic_slice_in_dim(gain_sums, index * own, own)
    grad_mlp_gain = lax.dynamic_slice_in_dim(gain_sums, width + index * own, own)
    return (
        jnp.stack(outs),
        jnp.stack([k["grad_tokens"] for k in kept]),
        grad_attn_gain,
        grad_query,
        grad_key,
        grad_value,
        gain_sums[2 * width : 2 * width + HEAD_SIZE],
        gain_sums[2 * width + HEAD_SIZE :],
        grad_out,
        grad_mlp_gain,
        grad_gate,
        grad_up,
        grad_down,
    )


def solution(mesh):
    rows = P(("dp", "seq"), None)
    line = P(("dp", "seq"))
    tokens = P("dp", "seq", None)
    return jax.shard_map(
        body,
        mesh=mesh,
        in_specs=(tokens, line, rows, rows, rows, P(), P(), rows, line, rows, rows, rows, tokens),
        out_specs=(tokens, tokens, line, rows, rows, rows, P(), P(), rows, line, rows, rows, rows),
        check_vma=False,
    )
```

time: 2640 us -> 563 us (0.21)
  waiting for transfers between devices: 1560 us -> 217 us
  local copies, waits for them, and re-layouts: 524 us -> 49.8 us
  matrix products: 305 us -> 80.4 us
  blocking collectives: 123 us -> 0 us
  starting transfers between devices: 1 us -> 90.3 us
  Pallas kernels: 0 us -> 71.6 us
  other arithmetic: 92.5 us -> 41.9 us
    unnamed x22 -> x0, waiting for transfers between devices: 871 us -> none
    all_gather x18 -> x0, waiting for transfers between devices: 691 us -> none  [the longest x4 78.3 us: body(): lax.all_gather(shortened(pair), 'seq', axis=1, tiled=True)]
    ppermute x0 -> x84, waiting for transfers between devices: none -> 217 us  [swap(): return lax.ppermute(value, AXES, pairs)]
    dot_general x42 -> x26, matrix products: 284 us -> 80.4 us  [the longest x12 36.1 us: dot_t(): lax.dot_general(a, b, (((1,), (1,)), ((), ())), preferred_element_type=F32)]
    unnamed x155 -> x188, local copies, waits for them, and re-layouts: 179 us -> 9.85 us
    dynamic_update_slice x18 -> x25, local copies, waits for them, and re-layouts: 122 us -> 12.9 us  [the longest x24 12.9 us: gather_dp(): full = lax.dynamic_update_index_in_dim(full, v, self.d ^ r, 0)]
    ppermute x0 -> x84, starting transfers between devices: none -> 90.3 us  [swap(): return lax.ppermute(value, AXES, pairs)]
    unnamed x2 -> x0, blocking collectives: 81.5 us -> none
  transfers between devices with their start and end apart: 21 -> 84, of which waited for: 17 -> 40; matrix products, arithmetic and copies ran while one was open for 15% -> 28% of each run, Pallas kernels for 0% -> 13%
where the time goes in v1:
time: 563 us; the launch traced here: 555 us
  waiting for transfers between devices  217 us (39%)
  starting transfers between devices  90.3 us (16%)
  matrix products  80.4 us (14%)
  Pallas kernels  71.6 us (13%)
  local copies, waits for them, and re-layouts  49.8 us (9%)
  other arithmetic  41.9 us (7%)
    ppermute x84, waiting for transfers between devices, swap(): return lax.ppermute(value, AXES, pairs)  217 us
    ppermute x84, starting transfers between devices, swap(): return lax.ppermute(value, AXES, pairs)  90.3 us
    dot_general x12, matrix products, dot_t(): lax.dot_general(a, b, (((1,), (1,)), ((), ())), preferred_element_type=F32)  36.1 us
    pallas_call x2, Pallas kernels, attend_back(): pl.pallas_call(functools.partial(backward_kernel, blocks, x_count), name=...  34.7 us
    dot_general x4, matrix products, t_dot(): lax.dot_general(a, b, (((0,), (0,)), ((), ())), preferred_element_type=F32)  23.7 us
    pallas_call x2, Pallas kernels, attend(): pl.pallas_call(functools.partial(forward_kernel, blocks, x_count), name='...  20.7 us
    dot_general x10, matrix products, dot(): lax.dot_general(a, b, (((1,), (0,)), ((), ())), preferred_element_type=F32)  20.6 us
    pallas_call x2, Pallas kernels, project(): pl.pallas_call(project_kernel, name='project', out_shape=(jax.ShapeDtypeS...  16.2 us
  transfers between devices with their start and end apart: 84, of which 40 were waited for; matrix products, arithmetic and copies ran while one was open for 28% of the time, Pallas kernels for 13%

profile of v1, /device:TPU:0, one launch (start us, length us, event | category | flops | bytes accessed | tf_op | source)
XLA Modules:
  0.0 554.8 jit_solution(10781121312591180978)
XLA Ops:
  0.6 3.0 collective-permute-start
  5.3 2.6 collective-permute-start.35
  23.9 3.2 collective-permute-done.13
  34.5 2.9 collective-permute-start.16
  43.4 2.8 collective-permute-done.3
  48.0 4.5 collective-permute-done.25
  59.1 5.1 collective-permute-done.18
  64.1 2.6 collective-permute-start.36
  67.8 8.1 %collective-permute-done.36 = bf16[96,1024]{1,0:T(8,128)(2,1)S(1)} collective-permute-done((bf16[96,1024]{1,0:T(8,128)(2,1)}, bf16[96,1024]{1,0:T(8,128)(2,1)S(1)}, u32[]{:S(2)}, u32[]{:S(2)}) %collective-permute-start.36) | collective-permute-done | bytes 196640 | tf_op jit(solution)/shard_map/ppermute | solution.py:36
  78.6 3.3 collective-permute-start.6
  84.8 4.0 collective-permute-done.5
  90.3 4.0 collective-permute-done.6
  94.5 3.4 collective-permute-start.19
  98.6 6.1 %collective-permute-done.7 = bf16[128,1024]{1,0:T(8,128)(2,1)S(1)} collective-permute-done((bf16[128,1024]{1,0:T(8,128)(2,1)S(1)}, bf16[128,1024]{1,0:T(8,128)(2,1)S(1)}, u32[]{:S(2)}, u32[]{:S(2)}) %collective-permute-start.7) | collective-permute-done | bytes 262176 | tf_op jit(solution)/shard_map/ppermute | solution.py:36
  106.8 6.1 %collective-permute-done.9 = bf16[128,1024]{1,0:T(8,128)(2,1)S(1)} collective-permute-done((bf16[128,1024]{1,0:T(8,128)(2,1)S(1)}, bf16[128,1024]{1,0:T(8,128)(2,1)S(1)}, u32[]{:S(2)}, u32[]{:S(2)}) %collective-permute-start.9) | collective-permute-done | bytes 262176 | tf_op jit(solution)/shard_map/ppermute | solution.py:36
  116.5 3.4 collective-permute-start.28
  120.0 11.5 %collective-permute-done.27 = bf16[128,1536]{1,0:T(8,128)(2,1)} collective-permute-done((bf16[128,1536]{1,0:T(8,128)(2,1)S(1)}, bf16[128,1536]{1,0:T(8,128)(2,1)}, u32[]{:S(2)}, u32[]{:S(2)}) %collective-permute-start.27) | collective-permute-done | bytes 393248 | tf_op jit(solution)/shard_map/ppermute | solution.py:36
  136.7 2.9 collective-permute-done.20
  139.7 6.0 %collective-permute-start.21 = (bf16[4,64,1024]{2,1,0:T(8,128)(2,1)S(1)}, bf16[4,64,1024]{2,1,0:T(8,128)(2,1)S(1)}, u32[]{:S(2)}, u32[]{:S(2)}) collective-permute-start(bf16[4,64,1024]{2,1,0:T(8,128)(2,1)S(1)} %broadcast_select_fusion.1), channel_id=1, source_target_pairs={{0,16},{1,17},{2,18},{3,19},{4,20},{5,21},{6,22},{7,23},{8,24},{9,... | collective-permute-start | bytes 1572872 | tf_op jit(solution)/shard_map/ppermute | solution.py:36
  150.5 13.8 %collective-permute-done.21 = bf16[4,64,1024]{2,1,0:T(8,128)(2,1)S(1)} collective-permute-done((bf16[4,64,1024]{2,1,0:T(8,128)(2,1)S(1)}, bf16[4,64,1024]{2,1,0:T(8,128)(2,1)S(1)}, u32[]{:S(2)}, u32[]{:S(2)}) %collective-permute-start.21) | collective-permute-done | bytes 524320 | tf_op jit(solution)/shard_map/ppermute | solution.py:36
  164.5 3.1 collective-permute-start.31
  172.1 8.1 %project.2 = (bf16[4,256,1024]{2,1,0:T(8,128)(2,1)}, bf16[1024,1024]{1,0:T(8,128)(2,1)}, f32[1024,768]{1,0:T(8,128)}) custom-call(s32[1]{0:T(128)} %bitcast.s_ref, bf16[4,256,1024]{2,1,0:T(8,128)(2,1)} %get-tuple-element.73.x_ref, bf16[1024,1024]{1,0:T(8,128)(2,1)} %bitcast.433, f32[1,1024]{1,0:T(1,128)} %get-tuple-element.162.gain_ref, ...), custom_call_target="tpu_custom_call" | custom-call | flops 2147483648 | bytes 14680064 | tf_op jit(solution)/shard_map/project/pallas_call | solution.py:250
  180.2 10.3 %attend.2 = (bf16[4,256,512]{2,1,0:T(8,128)(2,1)}, f32[4,1,1024]{2,1,0:T(1,128)}) custom-call(s32[1]{0:T(128)} %bitcast.s_ref, bf16[1024,1024]{1,0:T(8,128)(2,1)} %get-tuple-element.29.q_ref.k_ref.v_ref, bf16[1024,1024]{1,0:T(8,128)(2,1)} %get-tuple-element.29.q_ref.k_ref.v_ref, bf16[1024,1024]{1,0:T(8,128)(2,1)} %get-tuple-element.29.q_ref.k_ref.v_ref), custom_call_target="tpu_custom_call" | custom-call | flops 2147483648 | bytes 4194304 | tf_op jit(solution)/shard_map/attend/pallas_call | solution.py:320
  193.5 8.1 %project.3 = (bf16[4,256,1024]{2,1,0:T(8,128)(2,1)}, bf16[1024,1024]{1,0:T(8,128)(2,1)}, f32[1024,768]{1,0:T(8,128)}) custom-call(s32[1]{0:T(128)} %bitcast.s_ref, bf16[4,256,1024]{2,1,0:T(8,128)(2,1)} %get-tuple-element.74.x_ref, bf16[1024,1024]{1,0:T(8,128)(2,1)} %bitcast.434, f32[1,1024]{1,0:T(1,128)} %get-tuple-element.162.gain_ref, ...), custom_call_target="tpu_custom_call" | custom-call | flops 2147483648 | bytes 14680064 | tf_op jit(solution)/shard_map/project/pallas_call | solution.py:250
  201.7 10.4 %attend.3 = (bf16[4,256,512]{2,1,0:T(8,128)(2,1)}, f32[4,1,1024]{2,1,0:T(1,128)}) custom-call(s32[1]{0:T(128)} %bitcast.s_ref, bf16[1024,1024]{1,0:T(8,128)(2,1)} %get-tuple-element.31.q_ref.k_ref.v_ref, bf16[1024,1024]{1,0:T(8,128)(2,1)} %get-tuple-element.31.q_ref.k_ref.v_ref, bf16[1024,1024]{1,0:T(8,128)(2,1)} %get-tuple-element.31.q_ref.k_ref.v_ref), custom_call_target="tpu_custom_call" | custom-call | flops 2147483648 | bytes 4194304 | tf_op jit(solution)/shard_map/attend/pallas_call | solution.py:320
  228.5 17.8 %collective-permute-done.23 = bf16[512,1024]{1,0:T(8,128)(2,1)S(1)} collective-permute-done((bf16[512,1024]{1,0:T(8,128)(2,1)S(1)}, bf16[512,1024]{1,0:T(8,128)(2,1)S(1)}, u32[]{:S(2)}, u32[]{:S(2)}) %collective-permute-start.23) | collective-permute-done | bytes 1048608 | tf_op jit(solution)/shard_map/ppermute | solution.py:36
  246.6 22.0 %collective-permute-done.44 = bf16[512,1024]{1,0:T(8,128)(2,1)S(1)} collective-permute-done((bf16[512,1024]{1,0:T(8,128)(2,1)S(1)}, bf16[512,1024]{1,0:T(8,128)(2,1)S(1)}, u32[]{:S(2)}, u32[]{:S(2)}) %collective-permute-start.44) | collective-permute-done | bytes 1048608 | tf_op jit(solution)/shard_map/ppermute | solution.py:36
  275.5 3.4 fusion.43
  278.9 3.2 multiply_convert_fusion.3
  282.2 2.5 convolution_convert_fusion.1
  284.7 3.4 fusion.48
  288.1 4.3 multiply_convert_fusion.1
  292.4 3.5 fusion.71
  298.6 2.8 fusion.96
  301.6 2.8 fusion.95
  304.7 10.8 %fusion.30 = bf16[1024,1536]{1,0:T(8,128)(2,1)S(1)} fusion(bf16[1024,768]{1,0:T(8,128)(2,1)} %get-tuple-element.66, bf16[1024,768]{1,0:T(8,128)(2,1)} %copy-done.76, bf16[1024,768]{1,0:T(8,128)(2,1)} %copy-done.74, bf16[1024,768]{1,0:T(8,128)(2,1)} %copy-done.72, bf16[512,1024]{1,0:T(8,128)(2,1)} %copy-done.65, bf16[512,1024]{1,0:T(8,128)(2,1)} %copy-done.37, ...), kind=kOutput, calls=%fused_computation.32 | convolution fusion | flops 6485966848 | bytes 13631488 | tf_op jit(solution)/shard_map/dot_general | solution.py:203
  315.5 4.2 convolution_convert_fusion
  321.9 3.0 collective-permute-start.82
  324.9 4.4 fusion.201
  330.4 4.4 fusion.200
  337.6 5.1 collective-permute-done.82
  346.0 4.0 collective-permute-done.83
  352.0 4.5 collective-permute-done.76
  357.8 2.9 collective-permute-start.77
  360.9 17.0 %collective-permute-done.52 = bf16[512,1024]{1,0:T(8,128)(2,1)S(1)} collective-permute-done((bf16[512,1024]{1,0:T(8,128)(2,1)S(1)}, bf16[512,1024]{1,0:T(8,128)(2,1)S(1)}, u32[]{:S(2)}, u32[]{:S(2)}) %collective-permute-start.52) | collective-permute-done | bytes 1048608 | tf_op jit(solution)/shard_map/ppermute | solution.py:36
  378.0 3.2 multiply_reduce_fusion.1
  381.2 13.7 %collective-permute-done.77 = bf16[2,128,1536]{2,1,0:T(8,128)(2,1)} collective-permute-done((bf16[2,128,1536]{2,1,0:T(8,128)(2,1)}, bf16[2,128,1536]{2,1,0:T(8,128)(2,1)}, u32[]{:S(2)}, u32[]{:S(2)}) %collective-permute-start.77) | collective-permute-done | bytes 786464 | tf_op jit(solution)/shard_map/ppermute | solution.py:36
  396.4 2.5 fusion.180
  401.4 5.2 collective-permute-done.78
  409.2 3.2 collective-permute-done.79
  418.8 17.2 %attend_back.3 = (bf16[4,256,1024]{2,1,0:T(8,128)(2,1)}, f32[1,128]{1,0:T(1,128)}, f32[1,128]{1,0:T(1,128)}) custom-call(s32[1]{0:T(128)} %bitcast.s_ref, bf16[1024,1024]{1,0:T(8,128)(2,1)} %get-tuple-element.31.q_ref.k_ref.v_ref, bf16[1024,1024]{1,0:T(8,128)(2,1)} %get-tuple-element.31.q_ref.k_ref.v_ref, ...), custom_call_target="tpu_custom_call" | custom-call | flops 2684354560 | bytes 12582912 | tf_op jit(solution)/shard_map/attend_back/pallas_call | solution.py:412
  436.0 3.2 fusion.185
  441.6 17.4 %attend_back.2 = (bf16[4,256,1024]{2,1,0:T(8,128)(2,1)}, f32[1,128]{1,0:T(1,128)}, f32[1,128]{1,0:T(1,128)}) custom-call(s32[1]{0:T(128)} %bitcast.s_ref, bf16[1024,1024]{1,0:T(8,128)(2,1)} %get-tuple-element.29.q_ref.k_ref.v_ref, bf16[1024,1024]{1,0:T(8,128)(2,1)} %get-tuple-element.29.q_ref.k_ref.v_ref, ...), custom_call_target="tpu_custom_call" | custom-call | flops 2684354560 | bytes 12582912 | tf_op jit(solution)/shard_map/attend_back/pallas_call | solution.py:412
  459.0 2.9 fusion.186
  461.9 7.0 %fusion.66 = bf16[1024,1024]{1,0:T(8,128)(2,1)S(1)} fusion(bf16[1024,1024]{1,0:T(8,128)(2,1)S(1)} %bitcast.441, bf16[1024,1024]{1,0:T(8,128)(2,1)S(1)} %bitcast.442, bf16[1024,1024]{1,0:T(8,128)(2,1)} %bitcast.510, bf16[1024,1024]{1,0:T(8,128)(2,1)} %bitcast.509), kind=kOutput, calls=%fused_computation.105 | convolution fusion | flops 4312793088 | bytes 10485760 | tf_op jit(solution)/shard_map/dot_general | solution.py:203
  484.7 11.2 %collective-permute-done.66 = bf16[2,2,128,1024]{3,2,1,0:T(8,128)(2,1)} collective-permute-done((bf16[2,2,128,1024]{3,2,1,0:T(8,128)(2,1)}, bf16[2,2,128,1024]{3,2,1,0:T(8,128)(2,1)}, u32[]{:S(2)}, u32[]{:S(2)}) %collective-permute-start.66) | collective-permute-done | bytes 1048608 | tf_op jit(solution)/shard_map/ppermute | solution.py:36
  497.9 2.7 collective-permute-start.67
  500.6 2.6 convert_add_fusion.4
  503.7 2.5 convert_add_fusion.6
  509.6 14.0 %collective-permute-done.67 = bf16[2,128,1024]{2,1,0:T(8,128)(2,1)S(1)} collective-permute-done((bf16[2,128,1024]{2,1,0:T(8,128)(2,1)S(1)}, bf16[2,128,1024]{2,1,0:T(8,128)(2,1)S(1)}, u32[]{:S(2)}, u32[]{:S(2)}) %collective-permute-start.67) | collective-permute-done | bytes 524320 | tf_op jit(solution)/shard_map/ppermute | solution.py:36
  523.9 3.6 collective-permute-done.55
  530.9 2.5 collective-permute-done.62
  537.7 3.2 collective-permute-done.64
  549.2 2.5 collective-permute-done.69
  (497 shorter events, 165.6 us)
Async XLA Ops:
  0.6 136.0 %collective-permute-start = (bf16[2,256,1024]{2,1,0:T(8,128)(2,1)}, bf16[2,256,1024]{2,1,0:T(8,128)(2,1)S(1)}, u32[]{:S(2)}, u32[]{:S(2)}) collective-permute-start(bf16[2,256,1024]{2,1,0:T(8,128)(2,1)} %param.13), channel_id=1, source_target_pairs={{0,2},{1,3},{2,0},{3,1},{4,6},{5,7},{6,4},{7,5},{8,10},{9,11},{10,... | collective-permute-start | bytes 3145736 | tf_op jit(solution)/shard_map/ppermute | solution.py:36
  3.7 160.8 %collective-permute-start.1 = (bf16[2,256,1024]{2,1,0:T(8,128)(2,1)}, bf16[2,256,1024]{2,1,0:T(8,128)(2,1)}, u32[]{:S(2)}, u32[]{:S(2)}) collective-permute-start(bf16[2,256,1024]{2,1,0:T(8,128)(2,1)} %param.13), channel_id=1, source_target_pairs={{0,1},{1,0},{2,3},{3,2},{4,5},{5,4},{6,7},{7,6},{8,9},{9,8},{10,11... | collective-permute-start | bytes 3145736 | tf_op jit(solution)/shard_map/ppermute | solution.py:36
  3.7 50.6 %collective-permute-start.34 = (bf16[96,1024]{1,0:T(8,128)(2,1)}, bf16[96,1024]{1,0:T(8,128)(2,1)}, u32[]{:S(2)}, u32[]{:S(2)}) collective-permute-start(bf16[96,1024]{1,0:T(8,128)(2,1)} %param.24), channel_id=1, source_target_pairs={{0,8},{1,9},{2,10},{3,11},{4,12},{5,13},{6,14},{7,15},{8,0},{9,1},... | collective-permute-start | bytes 589832 | tf_op jit(solution)/shard_map/ppermute | solution.py:36
  5.3 50.1 %collective-permute-start.35 = (bf16[96,1024]{1,0:T(8,128)(2,1)}, bf16[96,1024]{1,0:T(8,128)(2,1)}, u32[]{:S(2)}, u32[]{:S(2)}) collective-permute-start(bf16[96,1024]{1,0:T(8,128)(2,1)} %param.24), channel_id=1, source_target_pairs={{0,16},{1,17},{2,18},{3,19},{4,20},{5,21},{6,22},{7,23},{8,24},{9,... | collective-permute-start | bytes 589832 | tf_op jit(solution)/shard_map/ppermute | solution.py:36
  8.7 14.6 %collective-permute-start.12 = (bf16[2,1024]{1,0:T(2,128)(2,1)S(1)}, bf16[2,1024]{1,0:T(2,128)(2,1)S(1)}, u32[]{:S(2)}, u32[]{:S(2)}) collective-permute-start(bf16[2,1024]{1,0:T(2,128)(2,1)S(1)} %reshape.306), channel_id=1, source_target_pairs={{0,1},{1,0},{2,3},{3,2},{4,5},{5,4},{6,7},{7,6},{8,9},{9,8},{10,11... | collective-permute-start | bytes 12296 | tf_op jit(solution)/shard_map/ppermute | solution.py:36
  46.2 6.3 %collective-permute-start.25 = (bf16[1,2,32,1536]{3,2,1,0:T(8,128)(2,1)}, bf16[1,2,32,1536]{3,2,1,0:T(8,128)(2,1)S(1)}, u32[]{:S(2)}, u32[]{:S(2)}) collective-permute-start(bf16[1,2,32,1536]{3,2,1,0:T(8,128)(2,1)} %dynamic-slice_bitcast_fusion.10), channel_id=1, source_target_pairs={{0,2},{1,3},{2,0},{3,1},{4,6},{5,7},{6,4},{7,5},{8,10},{9,11},{10,... | collective-permute-start | bytes 589832 | tf_op jit(solution)/shard_map/ppermute | solution.py:36
  52.5 24.5 %collective-permute-start.37 = (bf16[96,1024]{1,0:T(8,128)(2,1)}, bf16[96,1024]{1,0:T(8,128)(2,1)S(1)}, u32[]{:S(2)}, u32[]{:S(2)}) collective-permute-start(bf16[96,1024]{1,0:T(8,128)(2,1)} %param.24), channel_id=1, source_target_pairs={{0,4},{1,5},{2,6},{3,7},{4,0},{5,1},{6,2},{7,3},{8,12},{9,13},{10,... | collective-permute-start | bytes 589832 | tf_op jit(solution)/shard_map/ppermute | solution.py:36
  55.4 8.8 %collective-permute-start.18 = (bf16[2,64,1024]{2,1,0:T(8,128)(2,1)S(1)}, bf16[2,64,1024]{2,1,0:T(8,128)(2,1)S(1)}, u32[]{:S(2)}, u32[]{:S(2)}) collective-permute-start(bf16[2,64,1024]{2,1,0:T(8,128)(2,1)S(1)} %pad_maximum_fusion.21), channel_id=1, source_target_pairs={{0,2},{1,3},{2,0},{3,1},{4,6},{5,7},{6,4},{7,5},{8,10},{9,11},{10,... | collective-permute-start | bytes 786440 | tf_op jit(solution)/shard_map/ppermute | solution.py:36
  57.9 8.9 %collective-permute-start.26 = (bf16[2,1,32,1536]{3,2,0,1:T(8,128)(2,1)S(1)}, bf16[2,1,32,1536]{3,2,0,1:T(8,128)(2,1)S(1)}, u32[]{:S(2)}, u32[]{:S(2)}) collective-permute-start(bf16[2,1,32,1536]{3,2,0,1:T(8,128)(2,1)S(1)} %fusion.142), channel_id=1, source_target_pairs={{0,1},{1,0},{2,3},{3,2},{4,5},{5,4},{6,7},{7,6},{8,9},{9,8},{10,11... | collective-permute-start | bytes 589832 | tf_op jit(solution)/shard_map/ppermute | solution.py:36
  64.1 11.8 %collective-permute-start.36 = (bf16[96,1024]{1,0:T(8,128)(2,1)}, bf16[96,1024]{1,0:T(8,128)(2,1)S(1)}, u32[]{:S(2)}, u32[]{:S(2)}) collective-permute-start(bf16[96,1024]{1,0:T(8,128)(2,1)} %collective-permute-done.34), channel_id=1, source_target_pairs={{0,16},{1,17},{2,18},{3,19},{4,20},{5,21},{6,22},{7,23},{8,24},{9,... | collective-permute-start | bytes 589832 | tf_op jit(solution)/shard_map/ppermute | solution.py:36
  66.8 11.7 %collective-permute-start.38 = (bf16[96,1024]{1,0:T(8,128)(2,1)}, bf16[96,1024]{1,0:T(8,128)(2,1)S(1)}, u32[]{:S(2)}, u32[]{:S(2)}) collective-permute-start(bf16[96,1024]{1,0:T(8,128)(2,1)} %collective-permute-done.34), channel_id=1, source_target_pairs={{0,4},{1,5},{2,6},{3,7},{4,0},{5,1},{6,2},{7,3},{8,12},{9,13},{10,... | collective-permute-start | bytes 589832 | tf_op jit(solution)/shard_map/ppermute | solution.py:36
  75.9 6.7 %collective-permute-start.39 = (bf16[96,1024]{1,0:T(8,128)(2,1)}, bf16[96,1024]{1,0:T(8,128)(2,1)S(1)}, u32[]{:S(2)}, u32[]{:S(2)}) collective-permute-start(bf16[96,1024]{1,0:T(8,128)(2,1)} %collective-permute-done.35), channel_id=1, source_target_pairs={{0,4},{1,5},{2,6},{3,7},{4,0},{5,1},{6,2},{7,3},{8,12},{9,13},{10,... | collective-permute-start | bytes 589832 | tf_op jit(solution)/shard_map/ppermute | solution.py:36
  77.0 11.7 %collective-permute-start.5 = (bf16[128,1024]{1,0:T(8,128)(2,1)S(1)}, bf16[128,1024]{1,0:T(8,128)(2,1)S(1)}, u32[]{:S(2)}, u32[]{:S(2)}) collective-permute-start(bf16[128,1024]{1,0:T(8,128)(2,1)S(1)} %bitcast.462), channel_id=1, source_target_pairs={{0,8},{1,9},{2,10},{3,11},{4,12},{5,13},{6,14},{7,15},{8,0},{9,1},... | collective-permute-start | bytes 786440 | tf_op jit(solution)/shard_map/ppermute | solution.py:36
  78.6 15.8 %collective-permute-start.6 = (bf16[128,1024]{1,0:T(8,128)(2,1)S(1)}, bf16[128,1024]{1,0:T(8,128)(2,1)S(1)}, u32[]{:S(2)}, u32[]{:S(2)}) collective-permute-start(bf16[128,1024]{1,0:T(8,128)(2,1)S(1)} %bitcast.463), channel_id=1, source_target_pairs={{0,16},{1,17},{2,18},{3,19},{4,20},{5,21},{6,22},{7,23},{8,24},{9,... | collective-permute-start | bytes 786440 | tf_op jit(solution)/shard_map/ppermute | solution.py:36
  82.6 23.7 %collective-permute-start.8 = (bf16[128,1024]{1,0:T(8,128)(2,1)S(1)}, bf16[128,1024]{1,0:T(8,128)(2,1)S(1)}, u32[]{:S(2)}, u32[]{:S(2)}) collective-permute-start(bf16[128,1024]{1,0:T(8,128)(2,1)S(1)} %bitcast.464), channel_id=1, source_target_pairs={{0,4},{1,5},{2,6},{3,7},{4,0},{5,1},{6,2},{7,3},{8,12},{9,13},{10,... | collective-permute-start | bytes 786440 | tf_op jit(solution)/shard_map/ppermute | solution.py:36
  94.4 10.3 %collective-permute-start.7 = (bf16[128,1024]{1,0:T(8,128)(2,1)S(1)}, bf16[128,1024]{1,0:T(8,128)(2,1)S(1)}, u32[]{:S(2)}, u32[]{:S(2)}) collective-permute-start(bf16[128,1024]{1,0:T(8,128)(2,1)S(1)} %collective-permute-done.5), channel_id=1, source_target_pairs={{0,16},{1,17},{2,18},{3,19},{4,20},{5,21},{6,22},{7,23},{8,24},{9,... | collective-permute-start | bytes 786440 | tf_op jit(solution)/shard_map/ppermute | solution.py:36
  94.5 22.1 %collective-permute-start.19 = (bf16[4,64,1024]{2,1,0:T(8,128)(2,1)S(1)}, bf16[4,64,1024]{2,1,0:T(8,128)(2,1)S(1)}, u32[]{:S(2)}, u32[]{:S(2)}) collective-permute-start(bf16[4,64,1024]{2,1,0:T(8,128)(2,1)S(1)} %pad_maximum_fusion.17), channel_id=1, source_target_pairs={{0,4},{6,2},{9,13},{15,11},{16,20},{22,18},{25,29},{31,27}} | collective-permute-start | bytes 1572872 | tf_op jit(solution)/shard_map/ppermute | solution.py:36
  104.7 8.3 %collective-permute-start.9 = (bf16[128,1024]{1,0:T(8,128)(2,1)S(1)}, bf16[128,1024]{1,0:T(8,128)(2,1)S(1)}, u32[]{:S(2)}, u32[]{:S(2)}) collective-permute-start(bf16[128,1024]{1,0:T(8,128)(2,1)S(1)} %collective-permute-done.5), channel_id=1, source_target_pairs={{0,4},{1,5},{2,6},{3,7},{4,0},{5,1},{6,2},{7,3},{8,12},{9,13},{10,... | collective-permute-start | bytes 786440 | tf_op jit(solution)/shard_map/ppermute | solution.py:36
  106.2 9.5 %collective-permute-start.10 = (bf16[128,1024]{1,0:T(8,128)(2,1)S(1)}, bf16[128,1024]{1,0:T(8,128)(2,1)S(1)}, u32[]{:S(2)}, u32[]{:S(2)}) collective-permute-start(bf16[128,1024]{1,0:T(8,128)(2,1)S(1)} %collective-permute-done.6), channel_id=1, source_target_pairs={{0,4},{1,5},{2,6},{3,7},{4,0},{5,1},{6,2},{7,3},{8,12},{9,13},{10,... | collective-permute-start | bytes 786440 | tf_op jit(solution)/shard_map/ppermute | solution.py:36
  113.0 34.2 %collective-permute-start.48 = (bf16[2,256,1024]{2,1,0:T(8,128)(2,1)S(1)}, bf16[2,256,1024]{2,1,0:T(8,128)(2,1)S(1)}, u32[]{:S(2)}, u32[]{:S(2)}) collective-permute-start(bf16[2,256,1024]{2,1,0:T(8,128)(2,1)S(1)} %copy-done.5), channel_id=1, source_target_pairs={{0,2},{1,3},{2,0},{3,1},{4,6},{5,7},{6,4},{7,5},{8,10},{9,11},{10,... | collective-permute-start | bytes 3145736 | tf_op jit(solution)/shard_map/ppermute | solution.py:36
  115.8 15.8 %collective-permute-start.27 = (bf16[128,1536]{1,0:T(8,128)(2,1)S(1)}, bf16[128,1536]{1,0:T(8,128)(2,1)}, u32[]{:S(2)}, u32[]{:S(2)}) collective-permute-start(bf16[128,1536]{1,0:T(8,128)(2,1)S(1)} %bitcast.456), channel_id=1, source_target_pairs={{0,8},{1,9},{2,10},{3,11},{4,12},{5,13},{6,14},{7,15},{8,0},{9,1},... | collective-permute-start | bytes 1179656 | tf_op jit(solution)/shard_map/ppermute | solution.py:36
  116.5 18.6 %collective-permute-start.28 = (bf16[128,1536]{1,0:T(8,128)(2,1)S(1)}, bf16[128,1536]{1,0:T(8,128)(2,1)S(1)}, u32[]{:S(2)}, u32[]{:S(2)}) collective-permute-start(bf16[128,1536]{1,0:T(8,128)(2,1)S(1)} %bitcast.457), channel_id=1, source_target_pairs={{0,16},{1,17},{2,18},{3,19},{4,20},{5,21},{6,22},{7,23},{8,24},{9,... | collective-permute-start | bytes 1179656 | tf_op jit(solution)/shard_map/ppermute | solution.py:36
  131.6 8.0 %collective-permute-start.20 = (bf16[4,64,1024]{2,1,0:T(8,128)(2,1)S(1)}, bf16[4,64,1024]{2,1,0:T(8,128)(2,1)S(1)}, u32[]{:S(2)}, u32[]{:S(2)}) collective-permute-start(bf16[4,64,1024]{2,1,0:T(8,128)(2,1)S(1)} %broadcast_select_fusion), channel_id=1, source_target_pairs={{0,8},{2,10},{4,12},{6,14},{9,1},{11,3},{13,5},{15,7},{16,24},{18,... | collective-permute-start | bytes 1572872 | tf_op jit(solution)/shard_map/ppermute | solution.py:36
  135.1 13.8 %collective-permute-start.11 = (bf16[128,1024]{1,0:T(8,128)(2,1)S(1)}, bf16[128,1024]{1,0:T(8,128)(2,1)S(1)}, u32[]{:S(2)}, u32[]{:S(2)}) collective-permute-start(bf16[128,1024]{1,0:T(8,128)(2,1)S(1)} %collective-permute-done.7), channel_id=1, source_target_pairs={{0,4},{1,5},{2,6},{3,7},{4,0},{5,1},{6,2},{7,3},{8,12},{9,13},{10,... | collective-permute-start | bytes 786440 | tf_op jit(solution)/shard_map/ppermute | solution.py:36
  136.6 31.0 %collective-permute-start.2 = (bf16[2,256,1024]{2,1,0:T(8,128)(2,1)S(1)}, bf16[2,256,1024]{2,1,0:T(8,128)(2,1)S(1)}, u32[]{:S(2)}, u32[]{:S(2)}) collective-permute-start(bf16[2,256,1024]{2,1,0:T(8,128)(2,1)S(1)} %collective-permute-done), channel_id=1, source_target_pairs={{0,1},{1,0},{2,3},{3,2},{4,5},{5,4},{6,7},{7,6},{8,9},{9,8},{10,11... | collective-permute-start | bytes 3145736 | tf_op jit(solution)/shard_map/ppermute | solution.py:36
  139.7 24.6 %collective-permute-start.21 = (bf16[4,64,1024]{2,1,0:T(8,128)(2,1)S(1)}, bf16[4,64,1024]{2,1,0:T(8,128)(2,1)S(1)}, u32[]{:S(2)}, u32[]{:S(2)}) collective-permute-start(bf16[4,64,1024]{2,1,0:T(8,128)(2,1)S(1)} %broadcast_select_fusion.1), channel_id=1, source_target_pairs={{0,16},{1,17},{2,18},{3,19},{4,20},{5,21},{6,22},{7,23},{8,24},{9,... | collective-permute-start | bytes 1572872 | tf_op jit(solution)/shard_map/ppermute | solution.py:36
  147.2 125.2 %collective-permute-start.49 = (bf16[2,256,1024]{2,1,0:T(8,128)(2,1)S(1)}, bf16[2,256,1024]{2,1,0:T(8,128)(2,1)}, u32[]{:S(2)}, u32[]{:S(2)}) collective-permute-start(bf16[2,256,1024]{2,1,0:T(8,128)(2,1)S(1)} %copy-done.5), channel_id=1, source_target_pairs={{0,1},{1,0},{2,3},{3,2},{4,5},{5,4},{6,7},{7,6},{8,9},{9,8},{10,11... | collective-permute-start | bytes 3145736 | tf_op jit(solution)/shard_map/ppermute | solution.py:36
  148.9 67.5 %collective-permute-start.30 = (bf16[128,1536]{1,0:T(8,128)(2,1)S(1)}, bf16[128,1536]{1,0:T(8,128)(2,1)}, u32[]{:S(2)}, u32[]{:S(2)}) collective-permute-start(bf16[128,1536]{1,0:T(8,128)(2,1)S(1)} %bitcast.458), channel_id=1, source_target_pairs={{0,4},{1,5},{2,6},{3,7},{4,0},{5,1},{6,2},{7,3},{8,12},{9,13},{10,... | collective-permute-start | bytes 1179656 | tf_op jit(solution)/shard_map/ppermute | solution.py:36
  164.3 49.8 %collective-permute-start.29 = (bf16[128,1536]{1,0:T(8,128)(2,1)}, bf16[128,1536]{1,0:T(8,128)(2,1)}, u32[]{:S(2)}, u32[]{:S(2)}) collective-permute-start(bf16[128,1536]{1,0:T(8,128)(2,1)} %collective-permute-done.27), channel_id=1, source_target_pairs={{0,16},{1,17},{2,18},{3,19},{4,20},{5,21},{6,22},{7,23},{8,24},{9,... | collective-permute-start | bytes 1179656 | tf_op jit(solution)/shard_map/ppermute | solution.py:36
  164.5 58.5 %collective-permute-start.31 = (bf16[128,1536]{1,0:T(8,128)(2,1)}, bf16[128,1536]{1,0:T(8,128)(2,1)}, u32[]{:S(2)}, u32[]{:S(2)}) collective-permute-start(bf16[128,1536]{1,0:T(8,128)(2,1)} %collective-permute-done.27), channel_id=1, source_target_pairs={{0,4},{1,5},{2,6},{3,7},{4,0},{5,1},{6,2},{7,3},{8,12},{9,13},{10,... | collective-permute-start | bytes 1179656 | tf_op jit(solution)/shard_map/ppermute | solution.py:36
  193.5 24.7 %collective-permute-start.22 = (bf16[512,1024]{1,0:T(8,128)(2,1)}, bf16[512,1024]{1,0:T(8,128)(2,1)}, u32[]{:S(2)}, u32[]{:S(2)}) collective-permute-start(bf16[512,1024]{1,0:T(8,128)(2,1)} %convolution_convert_fusion.5), channel_id=1, source_target_pairs={{0,1},{1,0},{2,3},{3,2},{4,5},{5,4},{6,7},{7,6},{8,9},{9,8},{10,11... | collective-permute-start | bytes 3145736 | tf_op jit(solution)/shard_map/ppermute | solution.py:36
  216.4 11.0 %collective-permute-start.32 = (bf16[128,1536]{1,0:T(8,128)(2,1)S(1)}, bf16[128,1536]{1,0:T(8,128)(2,1)S(1)}, u32[]{:S(2)}, u32[]{:S(2)}) collective-permute-start(bf16[128,1536]{1,0:T(8,128)(2,1)S(1)} %copy-done.42), channel_id=1, source_target_pairs={{0,4},{1,5},{2,6},{3,7},{4,0},{5,1},{6,2},{7,3},{8,12},{9,13},{10,... | collective-permute-start | bytes 1179656 | tf_op jit(solution)/shard_map/ppermute | solution.py:36
  218.3 54.2 %collective-permute-start.50 = (bf16[2,256,1024]{2,1,0:T(8,128)(2,1)S(1)}, bf16[2,256,1024]{2,1,0:T(8,128)(2,1)S(1)}, u32[]{:S(2)}, u32[]{:S(2)}) collective-permute-start(bf16[2,256,1024]{2,1,0:T(8,128)(2,1)S(1)} %copy-done.7), channel_id=1, source_target_pairs={{0,1},{1,0},{2,3},{3,2},{4,5},{5,4},{6,7},{7,6},{8,9},{9,8},{10,11... | collective-permute-start | bytes 3145736 | tf_op jit(solution)/shard_map/ppermute | solution.py:36
  220.2 26.1 %collective-permute-start.23 = (bf16[512,1024]{1,0:T(8,128)(2,1)S(1)}, bf16[512,1024]{1,0:T(8,128)(2,1)S(1)}, u32[]{:S(2)}, u32[]{:S(2)}) collective-permute-start(bf16[512,1024]{1,0:T(8,128)(2,1)S(1)} %get-tuple-element.170), channel_id=1, source_target_pairs={{0,2},{1,3},{2,0},{3,1},{4,6},{5,7},{6,4},{7,5},{8,10},{9,11},{10,... | collective-permute-start | bytes 3145736 | tf_op jit(solution)/shard_map/ppermute | solution.py:36
  223.0 45.5 %collective-permute-start.44 = (bf16[512,1024]{1,0:T(8,128)(2,1)S(1)}, bf16[512,1024]{1,0:T(8,128)(2,1)S(1)}, u32[]{:S(2)}, u32[]{:S(2)}) collective-permute-start(bf16[512,1024]{1,0:T(8,128)(2,1)S(1)} %get-tuple-element.172), channel_id=1, source_target_pairs={{0,2},{1,3},{2,0},{3,1},{4,6},{5,7},{6,4},{7,5},{8,10},{9,11},{10,... | collective-permute-start | bytes 3145736 | tf_op jit(solution)/shard_map/ppermute | solution.py:36
  227.4 42.8 %collective-permute-start.33 = (bf16[128,1536]{1,0:T(8,128)(2,1)}, bf16[128,1536]{1,0:T(8,128)(2,1)S(1)}, u32[]{:S(2)}, u32[]{:S(2)}) collective-permute-start(bf16[128,1536]{1,0:T(8,128)(2,1)} %collective-permute-done.29), channel_id=1, source_target_pairs={{0,4},{1,5},{2,6},{3,7},{4,0},{5,1},{6,2},{7,3},{8,12},{9,13},{10,... | collective-permute-start | bytes 1179656 | tf_op jit(solution)/shard_map/ppermute | solution.py:36
  275.4 9.3 %collective-permute-start.45 = (bf16[512,1024]{1,0:T(8,128)(2,1)S(1)}, bf16[512,1024]{1,0:T(8,128)(2,1)S(1)}, u32[]{:S(2)}, u32[]{:S(2)}) collective-permute-start(bf16[512,1024]{1,0:T(8,128)(2,1)S(1)} %get-tuple-element.169), channel_id=1, source_target_pairs={{0,1},{1,0},{2,3},{3,2},{4,5},{5,4},{6,7},{7,6},{8,9},{9,8},{10,11... | collective-permute-start | bytes 3145736 | tf_op jit(solution)/shard_map/ppermute | solution.py:36
  296.9 24.3 %collective-permute-start.81 = (bf16[2,2,96,1024]{3,2,1,0:T(8,128)(2,1)}, bf16[2,2,96,1024]{3,2,1,0:T(8,128)(2,1)S(1)}, u32[]{:S(2)}, u32[]{:S(2)}) collective-permute-start(bf16[2,2,96,1024]{3,2,1,0:T(8,128)(2,1)} %dynamic-slice_bitcast_fusion.2), channel_id=1, source_target_pairs={{0,4},{1,5},{2,6},{3,7},{4,0},{5,1},{6,2},{7,3},{8,12},{9,13},{10,... | collective-permute-start | bytes 2359304 | tf_op jit(solution)/shard_map/ppermute | solution.py:36
  301.4 20.5 %collective-permute-start.56 = (bf16[512,1024]{1,0:T(8,128)(2,1)}, bf16[512,1024]{1,0:T(8,128)(2,1)}, u32[]{:S(2)}, u32[]{:S(2)}) collective-permute-start(bf16[512,1024]{1,0:T(8,128)(2,1)} %fusion.96), channel_id=1, source_target_pairs={{0,1},{1,0},{2,3},{3,2},{4,5},{5,4},{6,7},{7,6},{8,9},{9,8},{10,11... | collective-permute-start | bytes 3145736 | tf_op jit(solution)/shard_map/ppermute | solution.py:36
  304.4 24.9 %collective-permute-start.51 = (bf16[512,1024]{1,0:T(8,128)(2,1)}, bf16[512,1024]{1,0:T(8,128)(2,1)}, u32[]{:S(2)}, u32[]{:S(2)}) collective-permute-start(bf16[512,1024]{1,0:T(8,128)(2,1)} %fusion.95), channel_id=1, source_target_pairs={{0,1},{1,0},{2,3},{3,2},{4,5},{5,4},{6,7},{7,6},{8,9},{9,8},{10,11... | collective-permute-start | bytes 3145736 | tf_op jit(solution)/shard_map/ppermute | solution.py:36
  319.9 36.6 %collective-permute-start.76 = (bf16[2,2,128,1536]{3,2,1,0:T(8,128)(2,1)S(1)}, bf16[2,2,128,1536]{3,2,1,0:T(8,128)(2,1)S(1)}, u32[]{:S(2)}, u32[]{:S(2)}) collective-permute-start(bf16[2,2,128,1536]{3,2,1,0:T(8,128)(2,1)S(1)} %dynamic-slice_bitcast_fusion), channel_id=1, source_target_pairs={{0,4},{1,5},{2,6},{3,7},{4,0},{5,1},{6,2},{7,3},{8,12},{9,13},{10,... | collective-permute-start | bytes 4718600 | tf_op jit(solution)/shard_map/ppermute | solution.py:36
  321.0 13.8 %collective-permute-start.41 = (bf16[512,1024]{1,0:T(8,128)(2,1)S(1)}, bf16[512,1024]{1,0:T(8,128)(2,1)S(1)}, u32[]{:S(2)}, u32[]{:S(2)}) collective-permute-start(bf16[512,1024]{1,0:T(8,128)(2,1)S(1)} %copy-done.63), channel_id=1, source_target_pairs={{0,1},{1,0},{2,3},{3,2},{4,5},{5,4},{6,7},{7,6},{8,9},{9,8},{10,11... | collective-permute-start | bytes 3145736 | tf_op jit(solution)/shard_map/ppermute | solution.py:36
  321.2 22.7 %collective-permute-start.46 = (bf16[512,1024]{1,0:T(8,128)(2,1)S(1)}, bf16[512,1024]{1,0:T(8,128)(2,1)S(1)}, u32[]{:S(2)}, u32[]{:S(2)}) collective-permute-start(bf16[512,1024]{1,0:T(8,128)(2,1)S(1)} %convolution_convert_fusion), channel_id=1, source_target_pairs={{0,1},{1,0},{2,3},{3,2},{4,5},{5,4},{6,7},{7,6},{8,9},{9,8},{10,11... | collective-permute-start | bytes 3145736 | tf_op jit(solution)/shard_map/ppermute | solution.py:36
  321.9 20.9 %collective-permute-start.82 = (bf16[2,96,1024]{2,1,0:T(8,128)(2,1)S(1)}, bf16[2,96,1024]{2,1,0:T(8,128)(2,1)S(1)}, u32[]{:S(2)}, u32[]{:S(2)}) collective-permute-start(bf16[2,96,1024]{2,1,0:T(8,128)(2,1)S(1)} %dynamic-slice_bitcast_fusion.5), channel_id=1, source_target_pairs={{0,16},{1,17},{2,18},{3,19},{4,20},{5,21},{6,22},{7,23},{8,24},{9,... | collective-permute-start | bytes 1179656 | tf_op jit(solution)/shard_map/ppermute | solution.py:36
  329.3 31.4 %collective-permute-start.57 = (bf16[512,1024]{1,0:T(8,128)(2,1)S(1)}, bf16[512,1024]{1,0:T(8,128)(2,1)S(1)}, u32[]{:S(2)}, u32[]{:S(2)}) collective-permute-start(bf16[512,1024]{1,0:T(8,128)(2,1)S(1)} %get-tuple-element.176), channel_id=1, source_target_pairs={{0,2},{1,3},{2,0},{3,1},{4,6},{5,7},{6,4},{7,5},{8,10},{9,11},{10,... | collective-permute-start | bytes 3145736 | tf_op jit(solution)/shard_map/ppermute | solution.py:36
  334.8 43.1 %collective-permute-start.52 = (bf16[512,1024]{1,0:T(8,128)(2,1)S(1)}, bf16[512,1024]{1,0:T(8,128)(2,1)S(1)}, u32[]{:S(2)}, u32[]{:S(2)}) collective-permute-start(bf16[512,1024]{1,0:T(8,128)(2,1)S(1)} %get-tuple-element.174), channel_id=1, source_target_pairs={{0,2},{1,3},{2,0},{3,1},{4,6},{5,7},{6,4},{7,5},{8,10},{9,11},{10,... | collective-permute-start | bytes 3145736 | tf_op jit(solution)/shard_map/ppermute | solution.py:36
  342.8 56.8 %collective-permute-start.42 = (bf16[256,1024]{1,0:T(8,128)(2,1)}, bf16[256,1024]{1,0:T(8,128)(2,1)}, u32[]{:S(2)}, u32[]{:S(2)}) collective-permute-start(bf16[256,1024]{1,0:T(8,128)(2,1)} %slice.703), channel_id=1, source_target_pairs={{0,2},{1,3},{2,0},{3,1},{4,6},{5,7},{6,4},{7,5},{8,10},{9,11},{10,... | collective-permute-start | bytes 1572872 | tf_op jit(solution)/shard_map/ppermute | solution.py:36
  350.0 56.8 %collective-permute-start.47 = (bf16[256,1024]{1,0:T(8,128)(2,1)}, bf16[256,1024]{1,0:T(8,128)(2,1)}, u32[]{:S(2)}, u32[]{:S(2)}) collective-permute-start(bf16[256,1024]{1,0:T(8,128)(2,1)} %slice.702), channel_id=1, source_target_pairs={{0,2},{1,3},{2,0},{3,1},{4,6},{5,7},{6,4},{7,5},{8,10},{9,11},{10,... | collective-permute-start | bytes 1572872 | tf_op jit(solution)/shard_map/ppermute | solution.py:36
  357.8 37.1 %collective-permute-start.77 = (bf16[2,128,1536]{2,1,0:T(8,128)(2,1)}, bf16[2,128,1536]{2,1,0:T(8,128)(2,1)}, u32[]{:S(2)}, u32[]{:S(2)}) collective-permute-start(bf16[2,128,1536]{2,1,0:T(8,128)(2,1)} %dynamic-slice_bitcast_fusion.3), channel_id=1, source_target_pairs={{0,16},{1,17},{2,18},{3,19},{4,20},{5,21},{6,22},{7,23},{8,24},{9,... | collective-permute-start | bytes 2359304 | tf_op jit(solution)/shard_map/ppermute | solution.py:36
  396.3 10.2 %collective-permute-start.78 = (bf16[128,1536]{1,0:T(8,128)(2,1)S(1)}, bf16[128,1536]{1,0:T(8,128)(2,1)S(1)}, u32[]{:S(2)}, u32[]{:S(2)}) collective-permute-start(bf16[128,1536]{1,0:T(8,128)(2,1)S(1)} %dynamic-slice_bitcast_fusion.6), channel_id=1, source_target_pairs={{0,8},{1,9},{2,10},{3,11},{4,12},{5,13},{6,14},{7,15},{8,0},{9,1},... | collective-permute-start | bytes 1179656 | tf_op jit(solution)/shard_map/ppermute | solution.py:36
  399.0 14.2 %collective-permute-start.53 = (bf16[512,1024]{1,0:T(8,128)(2,1)S(1)}, bf16[512,1024]{1,0:T(8,128)(2,1)S(1)}, u32[]{:S(2)}, u32[]{:S(2)}) collective-permute-start(bf16[512,1024]{1,0:T(8,128)(2,1)S(1)} %get-tuple-element.57), channel_id=1, source_target_pairs={{0,1},{1,0},{2,3},{3,2},{4,5},{5,4},{6,7},{7,6},{8,9},{9,8},{10,11... | collective-permute-start | bytes 3145736 | tf_op jit(solution)/shard_map/ppermute | solution.py:36
  399.1 14.1 %collective-permute-start.58 = (bf16[512,1024]{1,0:T(8,128)(2,1)S(1)}, bf16[512,1024]{1,0:T(8,128)(2,1)S(1)}, u32[]{:S(2)}, u32[]{:S(2)}) collective-permute-start(bf16[512,1024]{1,0:T(8,128)(2,1)S(1)} %get-tuple-element.166), channel_id=1, source_target_pairs={{0,1},{1,0},{2,3},{3,2},{4,5},{5,4},{6,7},{7,6},{8,9},{9,8},{10,11... | collective-permute-start | bytes 3145736 | tf_op jit(solution)/shard_map/ppermute | solution.py:36
  413.1 63.5 %collective-permute-start.80 = (bf16[2,1,32,1536]{3,2,0,1:T(8,128)(2,1)}, bf16[2,1,32,1536]{3,2,0,1:T(8,128)(2,1)}, u32[]{:S(2)}, u32[]{:S(2)}) collective-permute-start(bf16[2,1,32,1536]{3,2,0,1:T(8,128)(2,1)} %fusion.138), channel_id=1, source_target_pairs={{0,1},{1,0},{2,3},{3,2},{4,5},{5,4},{6,7},{7,6},{8,9},{9,8},{10,11... | collective-permute-start | bytes 589832 | tf_op jit(solution)/shard_map/ppermute | solution.py:36
  416.5 64.9 %collective-permute-start.71 = (bf16[256,1024]{1,0:T(8,128)(2,1)}, bf16[256,1024]{1,0:T(8,128)(2,1)}, u32[]{:S(2)}, u32[]{:S(2)}) collective-permute-start(bf16[256,1024]{1,0:T(8,128)(2,1)} %constant_dynamic-slice_fusion.2), channel_id=1, source_target_pairs={{0,16},{1,17},{2,18},{3,19},{4,20},{5,21},{6,22},{7,23},{8,24},{9,... | collective-permute-start | bytes 1572872 | tf_op jit(solution)/shard_map/ppermute | solution.py:36
  470.0 25.9 %collective-permute-start.66 = (bf16[2,2,128,1024]{3,2,1,0:T(8,128)(2,1)}, bf16[2,2,128,1024]{3,2,1,0:T(8,128)(2,1)}, u32[]{:S(2)}, u32[]{:S(2)}) collective-permute-start(bf16[2,2,128,1024]{3,2,1,0:T(8,128)(2,1)} %dynamic-slice_bitcast_fusion.1), channel_id=1, source_target_pairs={{0,4},{1,5},{2,6},{3,7},{4,0},{5,1},{6,2},{7,3},{8,12},{9,13},{10,... | collective-permute-start | bytes 3145736 | tf_op jit(solution)/shard_map/ppermute | solution.py:36
  473.9 26.7 %collective-permute-start.59 = (bf16[512,1024]{1,0:T(8,128)(2,1)}, bf16[512,1024]{1,0:T(8,128)(2,1)}, u32[]{:S(2)}, u32[]{:S(2)}) collective-permute-start(bf16[512,1024]{1,0:T(8,128)(2,1)} %convolution_convert_fusion.2), channel_id=1, source_target_pairs={{0,1},{1,0},{2,3},{3,2},{4,5},{5,4},{6,7},{7,6},{8,9},{9,8},{10,11... | collective-permute-start | bytes 3145736 | tf_op jit(solution)/shard_map/ppermute | solution.py:36
  476.7 27.0 %collective-permute-start.54 = (bf16[512,1024]{1,0:T(8,128)(2,1)}, bf16[512,1024]{1,0:T(8,128)(2,1)}, u32[]{:S(2)}, u32[]{:S(2)}) collective-permute-start(bf16[512,1024]{1,0:T(8,128)(2,1)} %convolution_convert_fusion.3), channel_id=1, source_target_pairs={{0,1},{1,0},{2,3},{3,2},{4,5},{5,4},{6,7},{7,6},{8,9},{9,8},{10,11... | collective-permute-start | bytes 3145736 | tf_op jit(solution)/shard_map/ppermute | solution.py:36
  482.9 25.2 %collective-permute-start.72 = (bf16[256,1024]{1,0:T(8,128)(2,1)S(1)}, bf16[256,1024]{1,0:T(8,128)(2,1)S(1)}, u32[]{:S(2)}, u32[]{:S(2)}) collective-permute-start(bf16[256,1024]{1,0:T(8,128)(2,1)S(1)} %add_convert_fusion.2), channel_id=1, source_target_pairs={{1,9},{3,11},{5,13},{7,15},{8,0},{10,2},{12,4},{14,6},{17,25},{19,... | collective-permute-start | bytes 1572872 | tf_op jit(solution)/shard_map/ppermute | solution.py:36
  497.9 25.7 %collective-permute-start.67 = (bf16[2,128,1024]{2,1,0:T(8,128)(2,1)S(1)}, bf16[2,128,1024]{2,1,0:T(8,128)(2,1)S(1)}, u32[]{:S(2)}, u32[]{:S(2)}) collective-permute-start(bf16[2,128,1024]{2,1,0:T(8,128)(2,1)S(1)} %dynamic-slice_bitcast_fusion.4), channel_id=1, source_target_pairs={{0,16},{1,17},{2,18},{3,19},{4,20},{5,21},{6,22},{7,23},{8,24},{9,... | collective-permute-start | bytes 1572872 | tf_op jit(solution)/shard_map/ppermute | solution.py:36
  503.3 20.6 %collective-permute-start.60 = (bf16[256,1024]{1,0:T(8,128)(2,1)S(1)}, bf16[256,1024]{1,0:T(8,128)(2,1)S(1)}, u32[]{:S(2)}, u32[]{:S(2)}) collective-permute-start(bf16[256,1024]{1,0:T(8,128)(2,1)S(1)} %slice.700), channel_id=1, source_target_pairs={{0,2},{1,3},{2,0},{3,1},{4,6},{5,7},{6,4},{7,5},{8,10},{9,11},{10,... | collective-permute-start | bytes 1572872 | tf_op jit(solution)/shard_map/ppermute | solution.py:36
  506.3 21.2 %collective-permute-start.55 = (bf16[256,1024]{1,0:T(8,128)(2,1)S(1)}, bf16[256,1024]{1,0:T(8,128)(2,1)S(1)}, u32[]{:S(2)}, u32[]{:S(2)}) collective-permute-start(bf16[256,1024]{1,0:T(8,128)(2,1)S(1)} %slice.701), channel_id=1, source_target_pairs={{0,2},{1,3},{2,0},{3,1},{4,6},{5,7},{6,4},{7,5},{8,10},{9,11},{10,... | collective-permute-start | bytes 1572872 | tf_op jit(solution)/shard_map/ppermute | solution.py:36
  508.3 29.1 %collective-permute-start.73 = (bf16[256,1024]{1,0:T(8,128)(2,1)S(1)}, bf16[256,1024]{1,0:T(8,128)(2,1)S(1)}, u32[]{:S(2)}, u32[]{:S(2)}) collective-permute-start(bf16[256,1024]{1,0:T(8,128)(2,1)S(1)} %add_convert_fusion.1), channel_id=1, source_target_pairs={{2,6},{4,0},{11,15},{13,9},{18,22},{20,16},{27,31},{29,25}} | collective-permute-start | bytes 1572872 | tf_op jit(solution)/shard_map/ppermute | solution.py:36
  523.8 22.8 %collective-permute-start.68 = (bf16[128,1024]{1,0:T(8,128)(2,1)S(1)}, bf16[128,1024]{1,0:T(8,128)(2,1)S(1)}, u32[]{:S(2)}, u32[]{:S(2)}) collective-permute-start(bf16[128,1024]{1,0:T(8,128)(2,1)S(1)} %dynamic-slice_bitcast_fusion.7), channel_id=1, source_target_pairs={{0,8},{1,9},{2,10},{3,11},{4,12},{5,13},{6,14},{7,15},{8,0},{9,1},... | collective-permute-start | bytes 786440 | tf_op jit(solution)/shard_map/ppermute | solution.py:36
  541.5 6.3 %collective-permute-start.74 = (bf16[128,1024]{1,0:T(8,128)(2,1)S(1)}, bf16[128,1024]{1,0:T(8,128)(2,1)S(1)}, u32[]{:S(2)}, u32[]{:S(2)}) collective-permute-start(bf16[128,1024]{1,0:T(8,128)(2,1)S(1)} %constant_dynamic-slice_fusion.1), channel_id=1, source_target_pairs={{0,2},{6,4},{9,11},{15,13},{16,18},{22,20},{25,27},{31,29}} | collective-permute-start | bytes 786440 | tf_op jit(solution)/shard_map/ppermute | solution.py:36
  (101 other events, 925.1 us)

commit v2 on v1

--- a/solution.py
+++ b/solution.py
@@ -448,6 +448,393 @@
     )(s, qkv, qkv, qkv, grad_mixed, log_total, pre, pre, query_gain, key_gain, cosine, sine)
 
 
+MESH = pl.DeviceIdType.MESH
+
+
+def flip(index, bit):
+    step = 1 << bit
+    return index + step - 2 * step * lax.rem(lax.div(index, step), 2)
+
+
+def bit_of(index, bit):
+    return lax.rem(lax.div(index, 1 << bit), 2)
+
+
+class Links:
+    def __init__(self, send, recv):
+        self.send, self.recv = send, recv
+        self.d, self.s = lax.axis_index("dp"), lax.axis_index("seq")
+        self.used = 0
+        self.started = []
+
+    def slots(self, n):
+        self.used += n
+        return self.used - n
+
+    def copy(self, src, dst, slot, **to):
+        return pltpu.make_async_remote_copy(
+            src_ref=src,
+            dst_ref=dst,
+            send_sem=self.send.at[slot],
+            recv_sem=self.recv.at[slot],
+            device_id=to,
+            device_id_type=MESH,
+        )
+
+    def start(self, src, dst, slot, when=None, **to):
+        copy = self.copy(src, dst, slot, **to)
+        self.started.append((copy, when))
+        if when is None:
+            copy.start()
+        else:
+            pl.when(when)(copy.start)
+        return copy
+
+    def finish(self):
+        for copy, when in self.started:
+            if when is None:
+                copy.wait_send()
+            else:
+                pl.when(when)(copy.wait_send)
+
+    def greet(self, dp_bits, seq_masks):
+        barrier = pltpu.get_barrier_semaphore()
+        for bit in dp_bits:
+            pl.semaphore_signal(
+                barrier, inc=1, device_id={"dp": flip(self.d, bit)}, device_id_type=MESH
+            )
+        for mask in seq_masks:
+            pl.semaphore_signal(
+                barrier, inc=1, device_id={"seq": self.seq_at(mask)}, device_id_type=MESH
+            )
+        pl.semaphore_wait(barrier, len(dp_bits) + len(seq_masks))
+
+    def seq_at(self, mask):
+        s = self.s
+        for bit in range(2):
+            if mask >> bit & 1:
+                s = flip(s, bit)
+        return s
+
+    def dp_at(self, mask):
+        d = self.d
+        for bit in range(3):
+            if mask >> bit & 1:
+                d = flip(d, bit)
+        return d
+
+
+class Gather:
+    def __init__(self, links, block, order):
+        self.links, self.block, self.order = links, block, order
+        self.base = links.slots(8)
+        self.copies = {}
+
+    def send(self, r, bit):
+        src = self.block(self.links.dp_at(r))
+        self.copies[r | 1 << bit] = self.links.start(
+            src, src, self.base + (r | 1 << bit), dp=flip(self.links.d, bit)
+        )
+
+    def got(self, r):
+        self.copies[r].wait_recv()
+
+    def first(self):
+        for bit in self.order:
+            self.send(0, bit)
+
+    def second(self):
+        a, b, c = self.order
+        self.got(1 << a)
+        self.send(1 << a, b)
+        self.send(1 << a, c)
+
+    def third(self):
+        a, b, c = self.order
+        self.got(1 << b)
+        self.send(1 << b, c)
+        self.got(1 << a | 1 << b)
+        self.send(1 << a | 1 << b, c)
+
+    def last(self):
+        a, b, c = self.order
+        for r in (0, 1 << a, 1 << b, 1 << a | 1 << b):
+            self.got(r | 1 << c)
+
+
+def first_kernel(
+    heads,
+    a_ref, c_ref, out_ref, down_ref, x_ref, g_ref, gains_ref, qg_ref, kg_ref, cos_ref, sin_ref,
+    xr_ref, gr_ref, wa_ref, wc_ref, wo_ref, wd_ref, n_ref, qkv_ref, pre_ref, o_ref, log_ref, gain_ref,
+    w_v, x_v, n_v, qkv_v, pre_v, o_v, sum_v, got_v, send, recv, local,
+):
+    links = Links(send, recv)
+    d, s = links.d, links.s
+    sequences, piece, width = x_ref.shape
+    blocks = xr_ref.shape[1]
+    length = blocks * piece
+    x_bit, core = bit_of(s, 1), bit_of(s, 0)
+    z1, z0, y = bit_of(d, 2), bit_of(d, 1), bit_of(d, 0)
+    place_of = lambda i: lax.rem((i & 1) + core, 2) * 2 + lax.rem((i >> 1) + x_bit, 2)
+    local_used = [0]
+    locals_ = {}
+
+    def near(name, src, dst):
+        copy = pltpu.make_async_copy(src, dst, local.at[local_used[0]])
+        local_used[0] += 1
+        copy.start()
+        locals_[name] = copy
+
+    links.greet((0, 1, 2), (1, 2, 3))
+
+    def exchange(src, dst):
+        base = links.slots(4)
+        return [
+            links.start(src.at[links.seq_at(k)], dst.at[d, s], base + k, seq=links.seq_at(k))
+            for k in (2, 3, 1)
+        ]
+
+    a_own = exchange(a_ref, wa_ref)
+    near("a", a_ref.at[s], wa_ref.at[d, s])
+
+    gain_slots = links.slots(5)
+    gain_to = [dict(seq=links.seq_at(1)), dict(seq=links.seq_at(2))] + [dict(dp=flip(d, b)) for b in range(3)]
+    gain_copy = links.start(gains_ref, got_v.at[0], gain_slots, **gain_to[0])
+
+    x_slots = links.slots(3 * sequences)
+    x_far = [
+        links.start(x_ref.at[n], xr_ref.at[n, 1], x_slots + 3 * n, seq=links.seq_at(2))
+        for n in range(sequences)
+    ]
+    x_near = [
+        links.start(x_ref.at[n], xr_ref.at[n, 2], x_slots + 3 * n + 1, seq=links.seq_at(1))
+        for n in range(sequences)
+    ]
+    c_own = exchange(c_ref, wc_ref)
+    near("c", c_ref.at[s], wc_ref.at[d, s])
+    for n in range(sequences):
+        near(f"x{n}", x_ref.at[n], xr_ref.at[n, 0])
+    near("d", down_ref, wd_ref.at[d])
+
+    across, beside = lax.rem(x_bit + y, 2), lax.rem(core + z0, 2)
+    out_slots = links.slots(7)
+    holder = (across == 0) & (beside == 0)
+    out_first = [
+        links.start(
+            out_ref, wo_ref.at[z1, s], out_slots + k,
+            when=(across == k >> 1) & (beside == (k & 1)), seq=links.seq_at(k),
+        )
+        for k in (1, 2, 3)
+    ]
+
+    for copy in a_own:
+        copy.wait_recv()
+    locals_["a"].wait()
+    half = blocks // 2
+    gathers_a = [
+        Gather(links, lambda at, h=h: wa_ref.at[at, pl.ds(h * half, half)], order)
+        for h, order in ((0, (1, 2, 0)), (1, (0, 2, 1)))
+    ]
+    for gather in gathers_a:
+        gather.first()
+    gather_d = Gather(links, lambda at: wd_ref.at[at], (1, 2, 0))
+    gather_c = Gather(links, lambda at: wc_ref.at[at], (1, 2, 0))
+
+    for stage in range(5):
+        gain_copy.wait_recv()
+        before = gains_ref[...] if stage == 0 else sum_v[stage - 1]
+        if stage == 4:
+            gain_ref[...] = before + got_v[4]
+        else:
+            sum_v[stage] = before + got_v[stage]
+            gain_copy = links.start(
+                sum_v.at[stage], got_v.at[stage + 1], gain_slots + stage + 1, **gain_to[stage + 1]
+            )
+
+    for gather in gathers_a:
+        gather.second()
+
+    for copy in c_own:
+        copy.wait_recv()
+    locals_["c"].wait()
+    gather_c.first()
+
+    x_on = []
+    x_far[0].wait_recv()
+    x_on.append(links.start(xr_ref.at[0, 1], xr_ref.at[0, 3], x_slots + 2, seq=links.seq_at(1)))
+
+    @pl.when(holder)
+    def _():
+        own = pltpu.make_async_copy(out_ref, wo_ref.at[z1, s], local.at[local_used[0]])
+        own.start()
+        for copy in out_first:
+            copy.wait_recv()
+        own.wait()
+
+    local_used[0] += 1
+    out_y = links.start(wo_ref.at[z1], wo_ref.at[z1], out_slots + 4, when=holder, dp=flip(d, 0))
+
+    for gather in gathers_a:
+        gather.third()
+    locals_["d"].wait()
+    gather_d.first()
+
+    g_slots = links.slots(3 * sequences)
+    g_far = [
+        links.start(g_ref.at[n], gr_ref.at[n, 1], g_slots + 3 * n, seq=links.seq_at(2))
+        for n in range(sequences)
+    ]
+    g_near = [
+        links.start(g_ref.at[n], gr_ref.at[n, 2], g_slots + 3 * n + 1, seq=links.seq_at(1))
+        for n in range(sequences)
+    ]
+    for n in range(sequences):
+        near(f"g{n}", g_ref.at[n], gr_ref.at[n, 0])
+    g_on = []
+
+    for gather in gathers_a:
+        gather.last()
+    near("w", wa_ref, w_v)
+
+    def wait_x(n):
+        if n:
+            x_far[n].wait_recv()
+            x_on.append(
+                links.start(xr_ref.at[n, 1], xr_ref.at[n, 3], x_slots + 3 * n + 2, seq=links.seq_at(1))
+            )
+        locals_[f"x{n}"].wait()
+        x_near[n].wait_recv()
+        x_on[n].wait_recv()
+        near(f"xv{n}", xr_ref.at[n], x_v)
+        locals_[f"xv{n}"].wait()
+
+    def project_part(n):
+        def step(i, carry):
+            at = place_of(i)
+            x = x_v[at].astype(F32)
+            normed = (x * rms_scale(x) * gain_ref[0:1, :]).astype(BF16)
+            n_v[n, at] = normed
+            y_rows = dot(normed, w_v[...].reshape(width, -1))
+            rows = pl.ds(pl.multiple_of(i * piece, piece), piece)
+            cosine, sine = cos_ref[rows, :], sin_ref[rows, :]
+            for j in range(heads // 2):
+                for part in range(4):
+                    cut = slice((4 * j + part) * HEAD_SIZE, (4 * j + part + 1) * HEAD_SIZE)
+                    head = y_rows[:, cut]
+                    if part < 3:
+                        pre_v[n, rows, (3 * j + part) * HEAD_SIZE : (3 * j + part + 1) * HEAD_SIZE] = head
+                        gain = qg_ref[...] if part < 2 else kg_ref[...]
+                        head = head * rms_scale(head) * gain
+                        head = head * cosine + pltpu.roll(head, HEAD_SIZE // 2, 1) * sine
+                    qkv_v[n, rows, cut] = head.astype(BF16)
+            return carry
+
+        lax.fori_loop(0, blocks, step, 0)
+        near(f"n{n}", n_v.at[n], n_ref.at[n])
+        near(f"qkv{n}", qkv_v.at[n], qkv_ref.at[n])
+        near(f"pre{n}", pre_v.at[n], pre_ref.at[n])
+
+    def attend_part(n, start, stop):
+        def step(h, carry):
+            j, g = lax.div(h, 2), lax.rem(h, 2)
+            lanes = lambda at: pl.ds(pl.multiple_of(at * HEAD_SIZE, HEAD_SIZE), HEAD_SIZE)
+            values_t = qkv_v[n, :, lanes(4 * j + 3)].T
+            keys = qkv_v.at[n, :, lanes(4 * j + 2)]
+            for i in range(blocks):
+                query = qkv_v[n, i * piece : (i + 1) * piece, lanes(4 * j + g)]
+                exponent, highest = masked_exp(keys, query, i, piece, None)
+                total = jnp.sum(exponent, axis=0, keepdims=True)
+                probs = (exponent * (1.0 / total)).astype(BF16)
+                mixed = dot(values_t[:, : (i + 1) * piece], probs)
+                o_v[n, place_of(i), :, lanes(h)] = mixed.T.astype(BF16)
+                log_ref[n, h, :, i * piece : (i + 1) * piece] = highest + jnp.log(total)
+            return carry
+
+        lax.fori_loop(start, stop, step, 0)
+
+    wait_x(0)
+    locals_["w"].wait()
+    project_part(0)
+    gather_c.second()
+    pl.when((across == 1) & (beside == 0))(out_y.wait_recv)
+    out_z0 = links.start(wo_ref.at[z1], wo_ref.at[z1], out_slots + 5, when=beside == 0, dp=flip(d, 1))
+    gather_d.second()
+    attend_part(0, 0, heads // 2)
+    gather_c.third()
+    pl.when(beside == 1)(out_z0.wait_recv)
+    out_z1 = links.start(wo_ref.at[z1], wo_ref.at[z1], out_slots + 6, dp=flip(d, 2))
+    attend_part(0, heads // 2, heads)
+    near("o0", o_v.at[0], o_ref.at[0])
+    for n in range(1, sequences):
+        wait_x(n)
+        project_part(n)
+        if n == 1:
+            gather_d.third()
+            for m in range(sequences):
+                g_far[m].wait_recv()
+                g_on.append(
+                    links.start(gr_ref.at[m, 1], gr_ref.at[m, 3], g_slots + 3 * m + 2, seq=links.seq_at(1))
+                )
+        attend_part(n, 0, heads)
+        near(f"o{n}", o_v.at[n], o_ref.at[n])
+    gather_c.last()
+    gather_d.last()
+    out_z1.wait_recv()
+    for copy in g_near + g_on:
+        copy.wait_recv()
+    for n in range(sequences):
+        for name in ("g", "n", "qkv", "pre", "o"):
+            locals_[f"{name}{n}"].wait()
+    links.finish()
+
+
+def first(a, c, w_out, w_down, x, g, gains, query_gain, key_gain, cosine, sine, dp, heads):
+    blocks, rows, columns = a.shape
+    sequences, piece, width = x.shape
+    length = blocks * piece
+    hbm = pl.BlockSpec(memory_space=pl.ANY)
+    vmem = pl.BlockSpec(memory_space=pltpu.VMEM)
+    shape = jax.ShapeDtypeStruct
+    pre_columns = columns // 4 * 3
+    slots = 96
+    return pl.pallas_call(
+        functools.partial(first_kernel, heads),
+        name="first",
+        out_shape=(
+            shape((sequences, blocks, piece, width), BF16),
+            shape((sequences, blocks, piece, width), BF16),
+            shape((dp, blocks, rows, columns), BF16),
+            shape((dp, blocks, rows, c.shape[2]), BF16),
+            shape((2, blocks) + w_out.shape, BF16),
+            shape((dp,) + w_down.shape, BF16),
+            shape((sequences, blocks, piece, width), BF16),
+            shape((sequences, length, columns), BF16),
+            shape((sequences, length, pre_columns), F32),
+            shape((sequences, blocks, piece, heads * HEAD_SIZE), BF16),
+            shape((sequences, heads, 1, length), F32),
+            shape((8, width), F32),
+        ),
+        in_specs=[hbm] * 6 + [vmem] * 5,
+        out_specs=[hbm] * 10 + [vmem] * 2,
+        scratch_shapes=[
+            pltpu.VMEM((dp, blocks, rows, columns), BF16),
+            pltpu.VMEM((blocks, piece, width), BF16),
+            pltpu.VMEM((sequences, blocks, piece, width), BF16),
+            pltpu.VMEM((sequences, length, columns), BF16),
+            pltpu.VMEM((sequences, length, pre_columns), F32),
+            pltpu.VMEM((sequences, blocks, piece, heads * HEAD_SIZE), BF16),
+            pltpu.VMEM((4, 8, width), F32),
+            pltpu.VMEM((5, 8, width), F32),
+            pltpu.SemaphoreType.DMA((slots,)),
+            pltpu.SemaphoreType.DMA((slots,)),
+            pltpu.SemaphoreType.DMA((24,)),
+        ],
+        compiler_params=pltpu.CompilerParams(
+            collective_id=0, has_side_effects=True, vmem_limit_bytes=60 * 1024 * 1024
+        ),
+    )(a, c, w_out, w_down, x, g, gains, query_gain, key_gain, cosine, sine)
+
+
 def body(
     hidden_in,
     attn_gain,
@@ -475,13 +862,8 @@
     query_gain_row = query_gain.astype(F32).reshape(1, -1)
     key_gain_row = key_gain.astype(F32).reshape(1, -1)
 
-    gains = jnp.zeros((2, count, width // count), BF16)
-    own_gains = jnp.stack([attn_gain, mlp_gain]).reshape(2, 1, -1)
     index = wires.d * seq + wires.s
-    gains = lax.dynamic_update_slice(gains, own_gains, (0, index, 0))
-    gains = wires.sum_all(gains.reshape(2, width)).astype(F32)
-    attn_gain_row, mlp_gain_row = gains[:1], gains[1:]
-
+    own_gains = jnp.stack([attn_gain, mlp_gain])
     rows = w_query.shape[0]
     by_head = jnp.concatenate(
         [
@@ -492,37 +874,55 @@
         axis=2,
     )
     order = [wires.heads_of(t, heads_kv) for t in range(seq)]
-    package = jnp.stack([jnp.concatenate([by_head[:, j] for j in order[t]], axis=1) for t in range(seq)])
-    package = wires.exchange_seq(package).reshape(seq * rows, -1)
-    w_in = wires.gather_dp(package).reshape(width, -1)
-
-    x_pieces = wires.gather_seq_relative(hidden_in)
-    x_rel = jnp.stack(x_pieces, axis=1)
-
-    w_o = wires.gather_out(w_out, heads_kv)
-
+    package_in = jnp.stack(
+        [jnp.concatenate([by_head[:, j] for j in order[t]], axis=1) for t in range(seq)]
+    )
     down_rows = w_down.shape[0]
 
     def by_unit(w):
         return w.reshape(rows, dp, seq, down_rows).transpose(2, 0, 1, 3).reshape(seq, rows, -1)
 
     units = dp * down_rows
-    package = jnp.concatenate([by_unit(w_gate), by_unit(w_up)], axis=2)
-    package = wires.exchange_seq(package).reshape(seq * rows, -1)
-    w_mlp = wires.gather_dp(package).reshape(width, -1)
-
-    g_pieces = wires.gather_seq_relative(cotangent)
-    g_rel = jnp.stack(g_pieces, axis=1)
-
-    w_d = wires.gather_dp(w_down).reshape(units, width)
+    package_mlp = jnp.concatenate([by_unit(w_gate), by_unit(w_up)], axis=2)
+
+    fused = (dp, seq) == (8, 4) and rows % 16 == 0 and down_rows % 16 == 0
+    if fused:
+        gains = jnp.zeros((8, count, width // count), F32)
+        gains = lax.dynamic_update_slice(gains, own_gains.astype(F32)[:, None], (0, index, 0))
+        (
+            x_rel, g_rel, w_in, w_mlp, w_o, w_d, all_normed, all_qkv, all_pre, all_mixed, all_log, gains
+        ) = first(
+            package_in, package_mlp, w_out, w_down, hidden_in, cotangent, gains.reshape(8, width),
+            query_gain_row, key_gain_row, cosine, sine, dp, 2 * heads_kv // seq,
+        )
+        w_in, w_mlp = w_in.reshape(width, -1), w_mlp.reshape(width, -1)
+        w_o, w_d = w_o.reshape(-1, width), w_d.reshape(units, width)
+        attn_gain_row, mlp_gain_row = gains[:1], gains[1:2]
+    else:
+        gains = jnp.zeros((2, count, width // count), BF16)
+        gains = lax.dynamic_update_slice(gains, own_gains[:, None], (0, index, 0))
+        gains = wires.sum_all(gains.reshape(2, width)).astype(F32)
+        attn_gain_row, mlp_gain_row = gains[:1], gains[1:]
+        package = wires.exchange_seq(package_in).reshape(seq * rows, -1)
+        w_in = wires.gather_dp(package).reshape(width, -1)
+        x_rel = jnp.stack(wires.gather_seq_relative(hidden_in), axis=1)
+        w_o = wires.gather_out(w_out, heads_kv)
+        package = wires.exchange_seq(package_mlp).reshape(seq * rows, -1)
+        w_mlp = wires.gather_dp(package).reshape(width, -1)
+        g_rel = jnp.stack(wires.gather_seq_relative(cotangent), axis=1)
+        w_d = wires.gather_dp(w_down).reshape(units, width)
 
     kept = []
     outs = []
     for n in range(sequences):
-        normed, qkv, pre = project(
-            s_index, x_rel[n], w_in, attn_gain_row, query_gain_row, key_gain_row, cosine, sine, x_count
-        )
-        mixed, log_total = attend(s_index, qkv, seq, x_count)
+        if fused:
+            normed, qkv, pre = all_normed[n], all_qkv[n], all_pre[n]
+            mixed, log_total = all_mixed[n], all_log[n]
+        else:
+            normed, qkv, pre = project(
+                s_index, x_rel[n], w_in, attn_gain_row, query_gain_row, key_gain_row, cosine, sine, x_count
+            )
+            mixed, log_total = attend(s_index, qkv, seq, x_count)
         mixed_rows = mixed.reshape(length, -1)
         other = wires.swap(dot(mixed_rows[part:], w_o).astype(BF16), 1)
         total = wires.sum_x(dot(mixed_rows[:part], w_o) + other.astype(F32))

time: 563 us -> 529 us (0.940)
  Pallas kernels: 71.6 us -> 180 us
  waiting for transfers between devices: 217 us -> 133 us
  starting transfers between devices: 90.3 us -> 31.5 us
  other arithmetic: 41.9 us -> 31.7 us
  local copies, waits for them, and re-layouts: 49.8 us -> 57.4 us
  matrix products: 80.4 us -> 87.9 us
    pallas_call x4 -> x1, Pallas kernels: 36.9 us -> 145 us  [first(): pl.pallas_call(functools.partial(first_kernel, heads), name='first', out_...]
    ppermute x84 -> x43, waiting for transfers between devices: 217 us -> 133 us  [swap(): return lax.ppermute(value, AXES, pairs)]
    ppermute x84 -> x43, starting transfers between devices: 90.3 us -> 31.5 us  [swap(): return lax.ppermute(value, AXES, pairs)]
    dynamic_update_slice x25 -> x1, local copies, waits for them, and re-layouts: 12.9 us -> 0.04 us  [body(): lax.dynamic_update_slice(gains, own_gains.astype(F32)[:, None], (0, index...]
    another operation x4 -> x0, other arithmetic: 7.7 us -> none  [the longest x2 4.13 us: body(): g_rel = jnp.stack(g_pieces, axis=1)]
    dot_general x12, matrix products: 36.1 us -> 43.4 us  [dot_t(): lax.dot_general(a, b, (((1,), (1,)), ((), ())), preferred_element_type=F32)]
    slice x6 -> x8, local copies, waits for them, and re-layouts: 9.65 us -> 16.2 us  [the longest x2 5.71 us: body(): other = wires.swap(dot_t(grad_rows[part:], w_in).astype(BF16), 1)]
  transfers between devices with their start and end apart: 84 -> 43, of which waited for: 40 -> 18; matrix products, arithmetic and copies ran while one was open for 28% -> 25% of each run, Pallas kernels for 13% -> 7%
where the time goes in v2:
time: 529 us; the launch traced here: 524 us
  Pallas kernels  180 us (34%)
  waiting for transfers between devices  133 us (25%)
  matrix products  87.9 us (17%)
  local copies, waits for them, and re-layouts  57.4 us (11%)
  other arithmetic  31.7 us (6%)
  starting transfers between devices  31.5 us (6%)
    pallas_call x1, Pallas kernels, first(): pl.pallas_call(functools.partial(first_kernel, heads), name='first', out_...  145 us
    ppermute x43, waiting for transfers between devices, swap(): return lax.ppermute(value, AXES, pairs)  133 us
    dot_general x12, matrix products, dot_t(): lax.dot_general(a, b, (((1,), (1,)), ((), ())), preferred_element_type=F32)  43.4 us
    pallas_call x2, Pallas kernels, attend_back(): pl.pallas_call(functools.partial(backward_kernel, blocks, x_count), name=...  34.7 us
    ppermute x43, starting transfers between devices, swap(): return lax.ppermute(value, AXES, pairs)  31.5 us
    dot_general x4, matrix products, t_dot(): lax.dot_general(a, b, (((0,), (0,)), ((), ())), preferred_element_type=F32)  22.6 us
    dot_general x10, matrix products, dot(): lax.dot_general(a, b, (((1,), (0,)), ((), ())), preferred_element_type=F32)  21.9 us
  transfers between devices with their start and end apart: 43, of which 18 were waited for; matrix products, arithmetic and copies ran while one was open for 25% of the time, Pallas kernels for 7%

profile of v2, /device:TPU:0, one launch (start us, length us, event | category | flops | bytes accessed | tf_op | source)
XLA Modules:
  0.0 523.8 jit_solution(7167340398494013645)
XLA Ops:
  6.1 1.9 fusion.149
  11.5 145.2 %first.1 = (bf16[2,4,256,1024]{3,2,1,0:T(8,128)(2,1)}, bf16[2,4,256,1024]{3,2,1,0:T(8,128)(2,1)}, bf16[8,4,32,1024]{3,2,1,0:T(8,128)(2,1)}, bf16[8,4,32,1536]{3,...) custom-call(bf16[4,32,1024]{2,1,0:T(8,128)(2,1)} %pad_maximum_fusion, ...), custom_call_target="tpu_custom_call" | custom-call | tf_op jit(solution)/shard_map/first/pallas_call | solution.py:800
  156.7 2.7 fusion.185
  159.4 1.7 convolution_convert_fusion.4
  162.1 1.7 convolution_convert_fusion.5
  163.8 1.5 fusion.182
  170.5 2.4 fusion.180
  173.6 2.6 fusion.104
  177.7 2.5 slice_bitcast_fusion.2
  180.9 2.1 collective-permute-start.1
  183.3 19.0 %collective-permute-done.6 = bf16[512,1024]{1,0:T(8,128)(2,1)S(1)} collective-permute-done((bf16[512,1024]{1,0:T(8,128)(2,1)S(1)}, bf16[512,1024]{1,0:T(8,128)(2,1)S(1)}, u32[]{:S(2)}, u32[]{:S(2)}) %collective-permute-start.6) | collective-permute-done | bytes 1048608 | tf_op jit(solution)/shard_map/ppermute | solution.py:36
  202.5 1.9 multiply_reduce_fusion.2
  204.4 19.3 %collective-permute-done.1 = bf16[512,1024]{1,0:T(8,128)(2,1)S(1)} collective-permute-done((bf16[512,1024]{1,0:T(8,128)(2,1)S(1)}, bf16[512,1024]{1,0:T(8,128)(2,1)S(1)}, u32[]{:S(2)}, u32[]{:S(2)}) %collective-permute-start.1) | collective-permute-done | bytes 1048608 | tf_op jit(solution)/shard_map/ppermute | solution.py:36
  225.8 1.8 copy-done.8
  227.6 2.5 fusion.178
  230.7 3.1 slice_bitcast_fusion
  233.9 3.4 fusion.43
  237.3 3.1 multiply_convert_fusion.3
  240.5 2.4 convolution_convert_fusion.1
  242.9 3.4 fusion.48
  246.3 12.5 %multiply_convert_fusion.1 = (bf16[1024,768]{1,0:T(8,128)(2,1)S(1)}, bf16[1024,768]{1,0:T(8,128)(2,1)}, bf16[1024,768]{1,0:T(8,128)(2,1)S(1)}) fusion(f32[1024,1536]{1,0:T(8,128)S(1)} %fusion.48, bf16[1024,1024]{1,0:T(8,128)(2,1)S(1)} %bitcast.319, bf16[768,1024]{1,0:T(8,128)(2,1)S(1)} %bitcast.366), kind=kOutput, calls=%fused_computation.43 | convolution fusion | flops 1622409216 | bytes 14680064 | tf_op jit(solution)/shard_map/dot_general | solution.py:199
  258.9 3.5 fusion.71
  264.9 2.8 fusion.96
  267.9 2.8 fusion.95
  271.0 10.8 %fusion.30 = bf16[1024,1536]{1,0:T(8,128)(2,1)S(1)} fusion(bf16[1024,768]{1,0:T(8,128)(2,1)} %get-tuple-element.70, bf16[1024,768]{1,0:T(8,128)(2,1)} %copy-done.81, bf16[1024,768]{1,0:T(8,128)(2,1)} %copy-done.79, bf16[1024,768]{1,0:T(8,128)(2,1)} %copy-done.77, bf16[512,1024]{1,0:T(8,128)(2,1)} %copy-done.72, bf16[512,1024]{1,0:T(8,128)(2,1)} %copy-done.41, ...), kind=kOutput, calls=%fused_computation.30 | convolution fusion | flops 6485966848 | bytes 13631488 | tf_op jit(solution)/shard_map/dot_general | solution.py:203
  281.8 4.0 convolution_convert_fusion
  288.5 3.3 fusion.195
  292.3 4.5 fusion.194
  296.8 1.6 collective-permute-start.11
  300.2 1.6 collective-permute-done.41
  304.4 4.5 collective-permute-done.42
  308.9 1.7 collective-permute-start.9
  311.5 11.1 %collective-permute-done.35 = bf16[2,2,128,1536]{3,2,1,0:T(8,128)(2,1)S(1)} collective-permute-done((bf16[2,2,128,1536]{3,2,1,0:T(8,128)(2,1)S(1)}, bf16[2,2,128,1536]{3,2,1,0:T(8,128)(2,1)S(1)}, u32[]{:S(2)}, u32[]{:S(2)}) %collective-permute-start.35) | collective-permute-done | bytes 1572896 | tf_op jit(solution)/shard_map/ppermute | solution.py:36
  324.2 16.3 %collective-permute-done.11 = bf16[512,1024]{1,0:T(8,128)(2,1)S(1)} collective-permute-done((bf16[512,1024]{1,0:T(8,128)(2,1)S(1)}, bf16[512,1024]{1,0:T(8,128)(2,1)S(1)}, u32[]{:S(2)}, u32[]{:S(2)}) %collective-permute-start.11) | collective-permute-done | bytes 1048608 | tf_op jit(solution)/shard_map/ppermute | solution.py:36
  340.7 2.7 multiply_reduce_fusion.1
  343.4 10.6 %collective-permute-done.36 = bf16[2,128,1536]{2,1,0:T(8,128)(2,1)} collective-permute-done((bf16[2,128,1536]{2,1,0:T(8,128)(2,1)}, bf16[2,128,1536]{2,1,0:T(8,128)(2,1)}, u32[]{:S(2)}, u32[]{:S(2)}) %collective-permute-start.36) | collective-permute-done | bytes 786464 | tf_op jit(solution)/shard_map/ppermute | solution.py:36
  355.5 2.8 fusion.174
  358.9 1.8 fusion.120
  360.7 5.8 %collective-permute-done.37 = bf16[128,1536]{1,0:T(8,128)(2,1)S(1)} collective-permute-done((bf16[128,1536]{1,0:T(8,128)(2,1)S(1)}, bf16[128,1536]{1,0:T(8,128)(2,1)S(1)}, u32[]{:S(2)}, u32[]{:S(2)}) %collective-permute-start.37) | collective-permute-done | bytes 393248 | tf_op jit(solution)/shard_map/ppermute | solution.py:36
  369.4 3.3 collective-permute-done.38
  373.5 2.4 fusion.90
  376.8 2.2 fusion.97
  379.1 17.2 %attend_back.3 = (bf16[4,256,1024]{2,1,0:T(8,128)(2,1)}, f32[1,128]{1,0:T(1,128)}, f32[1,128]{1,0:T(1,128)}) custom-call(s32[1]{0:T(128)} %bitcast.33.s_ref, bf16[1024,1024]{1,0:T(8,128)(2,1)} %get-tuple-element.79.q_ref.k_ref.v_ref, bf16[1024,1024]{1,0:T(8,128)(2,1)} %get-tuple-element.79.q_ref.k_ref.v_ref, ...), custom_call_target="tpu_custom_call" | custom-call | flops 2684354560 | bytes 12582912 | tf_op jit(solution)/shard_map/attend_back/pallas_call | solution.py:412
  396.3 2.8 fusion.183
  399.1 2.3 convolution_convert_fusion.2
  401.9 2.3 fusion.100
  404.2 17.5 %attend_back.2 = (bf16[4,256,1024]{2,1,0:T(8,128)(2,1)}, f32[1,128]{1,0:T(1,128)}, f32[1,128]{1,0:T(1,128)}) custom-call(s32[1]{0:T(128)} %bitcast.33.s_ref, bf16[1024,1024]{1,0:T(8,128)(2,1)} %get-tuple-element.80.q_ref.k_ref.v_ref, bf16[1024,1024]{1,0:T(8,128)(2,1)} %get-tuple-element.80.q_ref.k_ref.v_ref, ...), custom_call_target="tpu_custom_call" | custom-call | flops 2684354560 | bytes 12582912 | tf_op jit(solution)/shard_map/attend_back/pallas_call | solution.py:412
  421.7 2.9 fusion.184
  424.6 2.3 convolution_convert_fusion.3
  428.4 5.8 %fusion.66 = bf16[1024,1024]{1,0:T(8,128)(2,1)} fusion(bf16[1024,1024]{1,0:T(8,128)(2,1)S(1)} %bitcast.315, bf16[1024,1024]{1,0:T(8,128)(2,1)S(1)} %bitcast.316, bf16[1024,1024]{1,0:T(8,128)(2,1)S(1)} %bitcast.318, bf16[1024,1024]{1,0:T(8,128)(2,1)S(1)} %bitcast.317), kind=kOutput, calls=%fused_computation.101 | convolution fusion | flops 4312793088 | bytes 10485760 | tf_op jit(solution)/shard_map/dot_general | solution.py:203
  441.5 2.2 reshape.323
  446.1 2.2 reshape.325
  453.3 2.6 convert_add_fusion.4
  456.0 2.4 collective-permute-start.19
  458.4 2.7 convert_add_fusion.6
  461.3 13.9 %collective-permute-done.25 = bf16[2,2,128,1024]{3,2,1,0:T(8,128)(2,1)S(1)} collective-permute-done((bf16[2,2,128,1024]{3,2,1,0:T(8,128)(2,1)S(1)}, bf16[2,2,128,1024]{3,2,1,0:T(8,128)(2,1)S(1)}, u32[]{:S(2)}, u32[]{:S(2)}) %collective-permute-start.25) | collective-permute-done | bytes 1048608 | tf_op jit(solution)/shard_map/ppermute | solution.py:36
  475.7 2.4 collective-permute-start.26
  478.1 3.4 collective-permute-done.32
  484.2 14.1 %collective-permute-done.26 = bf16[2,128,1024]{2,1,0:T(8,128)(2,1)S(1)} collective-permute-done((bf16[2,128,1024]{2,1,0:T(8,128)(2,1)S(1)}, bf16[2,128,1024]{2,1,0:T(8,128)(2,1)S(1)}, u32[]{:S(2)}, u32[]{:S(2)}) %collective-permute-start.26) | collective-permute-done | bytes 524320 | tf_op jit(solution)/shard_map/ppermute | solution.py:36
  500.1 2.3 collective-permute-done.21
  503.1 3.0 collective-permute-done.22
  506.1 1.9 collective-permute-start.23
  509.8 3.2 collective-permute-start.24
  518.5 2.5 collective-permute-done.28
  (361 shorter events, 72.1 us)
Async XLA Ops:
  161.1 12.5 %collective-permute-start.5 = (bf16[512,1024]{1,0:T(8,128)(2,1)}, bf16[512,1024]{1,0:T(8,128)(2,1)}, u32[]{:S(2)}, u32[]{:S(2)}) collective-permute-start(bf16[512,1024]{1,0:T(8,128)(2,1)} %convolution_convert_fusion.4), channel_id=1, source_target_pairs={{0,1},{1,0},{2,3},{3,2},{4,5},{5,4},{6,7},{7,6},{8,9},{9,8},{10,11... | collective-permute-start | bytes 3145736 | tf_op jit(solution)/shard_map/ppermute | solution.py:36
  163.8 16.4 %collective-permute-start = (bf16[512,1024]{1,0:T(8,128)(2,1)}, bf16[512,1024]{1,0:T(8,128)(2,1)S(1)}, u32[]{:S(2)}, u32[]{:S(2)}) collective-permute-start(bf16[512,1024]{1,0:T(8,128)(2,1)} %convolution_convert_fusion.5), channel_id=1, source_target_pairs={{0,1},{1,0},{2,3},{3,2},{4,5},{5,4},{6,7},{7,6},{8,9},{9,8},{10,11... | collective-permute-start | bytes 3145736 | tf_op jit(solution)/shard_map/ppermute | solution.py:36
  176.2 26.1 %collective-permute-start.6 = (bf16[512,1024]{1,0:T(8,128)(2,1)S(1)}, bf16[512,1024]{1,0:T(8,128)(2,1)S(1)}, u32[]{:S(2)}, u32[]{:S(2)}) collective-permute-start(bf16[512,1024]{1,0:T(8,128)(2,1)S(1)} %get-tuple-element.170), channel_id=1, source_target_pairs={{0,2},{1,3},{2,0},{3,1},{4,6},{5,7},{6,4},{7,5},{8,10},{9,11},{10,... | collective-permute-start | bytes 3145736 | tf_op jit(solution)/shard_map/ppermute | solution.py:36
  180.9 42.8 %collective-permute-start.1 = (bf16[512,1024]{1,0:T(8,128)(2,1)S(1)}, bf16[512,1024]{1,0:T(8,128)(2,1)S(1)}, u32[]{:S(2)}, u32[]{:S(2)}) collective-permute-start(bf16[512,1024]{1,0:T(8,128)(2,1)S(1)} %get-tuple-element.168), channel_id=1, source_target_pairs={{0,2},{1,3},{2,0},{3,1},{4,6},{5,7},{6,4},{7,5},{8,10},{9,11},{10,... | collective-permute-start | bytes 3145736 | tf_op jit(solution)/shard_map/ppermute | solution.py:36
  183.3 41.9 %copy-start.46 = (f32[256]{0:T(256)}, f32[256]{0:T(256)S(1)}, u32[]{:S(2)}) copy-start(f32[256]{0:T(256)S(1)} %get-tuple-element.55) | copy-start | bytes 3076
  183.3 41.9 %copy-start.48 = (f32[256]{0:T(256)}, f32[256]{0:T(256)S(1)}, u32[]{:S(2)}) copy-start(f32[256]{0:T(256)S(1)} %get-tuple-element.56) | copy-start | bytes 3076
  183.3 19.2 %copy-start.11 = (bf16[1,2,256,1024]{3,2,1,0:T(8,128)(2,1)S(1)}, bf16[1,2,256,1024]{3,2,1,0:T(8,128)(2,1)}, u32[]{:S(2)}) copy-start(bf16[1,2,256,1024]{3,2,1,0:T(8,128)(2,1)} %get-tuple-element.86) | copy-start | bytes 3145732
  204.4 151.0 %copy-start.45 = (f32[512]{0:T(512)}, f32[512]{0:T(512)S(1)}, u32[]{:S(2)}) copy-start(f32[512]{0:T(512)S(1)} %add_rsqrt_fusion) | copy-start | bytes 6148
  225.1 8.7 %copy-start.40 = (bf16[512,1024]{1,0:T(8,128)(2,1)}, bf16[512,1024]{1,0:T(8,128)(2,1)S(1)}, u32[]{:S(2)}) copy-start(bf16[512,1024]{1,0:T(8,128)(2,1)S(1)} %get-tuple-element.166) | copy-start | bytes 3145732
  225.1 17.8 %copy-start.41 = (bf16[512,1024]{1,0:T(8,128)(2,1)}, bf16[512,1024]{1,0:T(8,128)(2,1)S(1)}, u32[]{:S(2)}) copy-start(bf16[512,1024]{1,0:T(8,128)(2,1)S(1)} %get-tuple-element.167) | copy-start | bytes 3145732
  225.1 8.7 %collective-permute-start.2 = (bf16[512,1024]{1,0:T(8,128)(2,1)S(1)}, bf16[512,1024]{1,0:T(8,128)(2,1)S(1)}, u32[]{:S(2)}, u32[]{:S(2)}) collective-permute-start(bf16[512,1024]{1,0:T(8,128)(2,1)S(1)} %get-tuple-element.166), channel_id=1, source_target_pairs={{0,1},{1,0},{2,3},{3,2},{4,5},{5,4},{6,7},{7,6},{8,9},{9,8},{10,11... | collective-permute-start | bytes 3145736 | tf_op jit(solution)/shard_map/ppermute | solution.py:36
  233.8 9.1 %collective-permute-start.7 = (bf16[512,1024]{1,0:T(8,128)(2,1)S(1)}, bf16[512,1024]{1,0:T(8,128)(2,1)S(1)}, u32[]{:S(2)}, u32[]{:S(2)}) collective-permute-start(bf16[512,1024]{1,0:T(8,128)(2,1)S(1)} %get-tuple-element.167), channel_id=1, source_target_pairs={{0,1},{1,0},{2,3},{3,2},{4,5},{5,4},{6,7},{7,6},{8,9},{9,8},{10,11... | collective-permute-start | bytes 3145736 | tf_op jit(solution)/shard_map/ppermute | solution.py:36
  240.5 18.4 %copy-start.75 = (bf16[1024,768]{1,0:T(8,128)(2,1)}, bf16[1024,768]{1,0:T(8,128)(2,1)S(1)}, u32[]{:S(2)}) copy-start(bf16[1024,768]{1,0:T(8,128)(2,1)S(1)} %get-tuple-element.76) | copy-start | bytes 4718596
  240.5 27.4 %copy-start.77 = (bf16[1024,768]{1,0:T(8,128)(2,1)}, bf16[1024,768]{1,0:T(8,128)(2,1)S(1)}, u32[]{:S(2)}) copy-start(bf16[1024,768]{1,0:T(8,128)(2,1)S(1)} %get-tuple-element.71) | copy-start | bytes 4718596
  240.5 27.4 %copy-start.79 = (bf16[1024,768]{1,0:T(8,128)(2,1)}, bf16[1024,768]{1,0:T(8,128)(2,1)S(1)}, u32[]{:S(2)}) copy-start(bf16[1024,768]{1,0:T(8,128)(2,1)S(1)} %get-tuple-element.72) | copy-start | bytes 4718596
  246.3 12.6 %copy-start.5 = (bf16[2,4,256,1024]{3,2,1,0:T(8,128)(2,1)S(1)}, bf16[2,4,256,1024]{3,2,1,0:T(8,128)(2,1)}, u32[]{:S(2)}) copy-start(bf16[2,4,256,1024]{3,2,1,0:T(8,128)(2,1)} %get-tuple-element.37) | copy-start | bytes 12582916
  263.4 23.9 %collective-permute-start.40 = (bf16[2,2,96,1024]{3,2,1,0:T(8,128)(2,1)}, bf16[2,2,96,1024]{3,2,1,0:T(8,128)(2,1)S(1)}, u32[]{:S(2)}, u32[]{:S(2)}) collective-permute-start(bf16[2,2,96,1024]{3,2,1,0:T(8,128)(2,1)} %dynamic-slice_bitcast_fusion.2), channel_id=1, source_target_pairs={{0,4},{1,5},{2,6},{3,7},{4,0},{5,1},{6,2},{7,3},{8,12},{9,13},{10,... | collective-permute-start | bytes 2359304 | tf_op jit(solution)/shard_map/ppermute | solution.py:36
  267.7 20.3 %collective-permute-start.15 = (bf16[512,1024]{1,0:T(8,128)(2,1)}, bf16[512,1024]{1,0:T(8,128)(2,1)}, u32[]{:S(2)}, u32[]{:S(2)}) collective-permute-start(bf16[512,1024]{1,0:T(8,128)(2,1)} %fusion.96), channel_id=1, source_target_pairs={{0,1},{1,0},{2,3},{3,2},{4,5},{5,4},{6,7},{7,6},{8,9},{9,8},{10,11... | collective-permute-start | bytes 3145736 | tf_op jit(solution)/shard_map/ppermute | solution.py:36
  270.7 21.2 %collective-permute-start.10 = (bf16[512,1024]{1,0:T(8,128)(2,1)}, bf16[512,1024]{1,0:T(8,128)(2,1)}, u32[]{:S(2)}, u32[]{:S(2)}) collective-permute-start(bf16[512,1024]{1,0:T(8,128)(2,1)} %fusion.95), channel_id=1, source_target_pairs={{0,1},{1,0},{2,3},{3,2},{4,5},{5,4},{6,7},{7,6},{8,9},{9,8},{10,11... | collective-permute-start | bytes 3145736 | tf_op jit(solution)/shard_map/ppermute | solution.py:36
  286.0 36.6 %collective-permute-start.35 = (bf16[2,2,128,1536]{3,2,1,0:T(8,128)(2,1)S(1)}, bf16[2,2,128,1536]{3,2,1,0:T(8,128)(2,1)S(1)}, u32[]{:S(2)}, u32[]{:S(2)}) collective-permute-start(bf16[2,2,128,1536]{3,2,1,0:T(8,128)(2,1)S(1)} %dynamic-slice_bitcast_fusion), channel_id=1, source_target_pairs={{0,4},{1,5},{2,6},{3,7},{4,0},{5,1},{6,2},{7,3},{8,12},{9,13},{10,... | collective-permute-start | bytes 4718600 | tf_op jit(solution)/shard_map/ppermute | solution.py:36
  287.1 9.7 %collective-permute-start.3 = (bf16[512,1024]{1,0:T(8,128)(2,1)S(1)}, bf16[512,1024]{1,0:T(8,128)(2,1)S(1)}, u32[]{:S(2)}, u32[]{:S(2)}) collective-permute-start(bf16[512,1024]{1,0:T(8,128)(2,1)S(1)} %copy-done.70), channel_id=1, source_target_pairs={{0,1},{1,0},{2,3},{3,2},{4,5},{5,4},{6,7},{7,6},{8,9},{9,8},{10,11... | collective-permute-start | bytes 3145736 | tf_op jit(solution)/shard_map/ppermute | solution.py:36
  287.3 15.0 %collective-permute-start.8 = (bf16[512,1024]{1,0:T(8,128)(2,1)S(1)}, bf16[512,1024]{1,0:T(8,128)(2,1)S(1)}, u32[]{:S(2)}, u32[]{:S(2)}) collective-permute-start(bf16[512,1024]{1,0:T(8,128)(2,1)S(1)} %convolution_convert_fusion), channel_id=1, source_target_pairs={{0,1},{1,0},{2,3},{3,2},{4,5},{5,4},{6,7},{7,6},{8,9},{9,8},{10,11... | collective-permute-start | bytes 3145736 | tf_op jit(solution)/shard_map/ppermute | solution.py:36
  288.0 13.8 %collective-permute-start.41 = (bf16[2,96,1024]{2,1,0:T(8,128)(2,1)S(1)}, bf16[2,96,1024]{2,1,0:T(8,128)(2,1)S(1)}, u32[]{:S(2)}, u32[]{:S(2)}) collective-permute-start(bf16[2,96,1024]{2,1,0:T(8,128)(2,1)S(1)} %dynamic-slice_bitcast_fusion.5), channel_id=1, source_target_pairs={{0,16},{1,17},{2,18},{3,19},{4,20},{5,21},{6,22},{7,23},{8,24},{9,... | collective-permute-start | bytes 1179656 | tf_op jit(solution)/shard_map/ppermute | solution.py:36
  291.9 32.0 %collective-permute-start.16 = (bf16[512,1024]{1,0:T(8,128)(2,1)S(1)}, bf16[512,1024]{1,0:T(8,128)(2,1)S(1)}, u32[]{:S(2)}, u32[]{:S(2)}) collective-permute-start(bf16[512,1024]{1,0:T(8,128)(2,1)S(1)} %get-tuple-element.174), channel_id=1, source_target_pairs={{0,2},{1,3},{2,0},{3,1},{4,6},{5,7},{6,4},{7,5},{8,10},{9,11},{10,... | collective-permute-start | bytes 3145736 | tf_op jit(solution)/shard_map/ppermute | solution.py:36
  296.8 43.7 %collective-permute-start.11 = (bf16[512,1024]{1,0:T(8,128)(2,1)S(1)}, bf16[512,1024]{1,0:T(8,128)(2,1)S(1)}, u32[]{:S(2)}, u32[]{:S(2)}) collective-permute-start(bf16[512,1024]{1,0:T(8,128)(2,1)S(1)} %get-tuple-element.172), channel_id=1, source_target_pairs={{0,2},{1,3},{2,0},{3,1},{4,6},{5,7},{6,4},{7,5},{8,10},{9,11},{10,... | collective-permute-start | bytes 3145736 | tf_op jit(solution)/shard_map/ppermute | solution.py:36
  301.8 57.0 %collective-permute-start.4 = (bf16[256,1024]{1,0:T(8,128)(2,1)}, bf16[256,1024]{1,0:T(8,128)(2,1)}, u32[]{:S(2)}, u32[]{:S(2)}) collective-permute-start(bf16[256,1024]{1,0:T(8,128)(2,1)} %slice.729), channel_id=1, source_target_pairs={{0,2},{1,3},{2,0},{3,1},{4,6},{5,7},{6,4},{7,5},{8,10},{9,11},{10,... | collective-permute-start | bytes 1572872 | tf_op jit(solution)/shard_map/ppermute | solution.py:36
  302.3 6.6 %collective-permute-start.42 = (bf16[96,1024]{1,0:T(8,128)(2,1)S(1)}, bf16[96,1024]{1,0:T(8,128)(2,1)S(1)}, u32[]{:S(2)}, u32[]{:S(2)}) collective-permute-start(bf16[96,1024]{1,0:T(8,128)(2,1)S(1)} %dynamic-slice_bitcast_fusion.8), channel_id=1, source_target_pairs={{0,8},{1,9},{2,10},{3,11},{4,12},{5,13},{6,14},{7,15},{8,0},{9,1},... | collective-permute-start | bytes 589832 | tf_op jit(solution)/shard_map/ppermute | solution.py:36
  302.4 20.2 %copy-start.16 = (bf16[1024,1536]{1,0:T(8,128)(2,1)S(1)}, bf16[1024,1536]{1,0:T(8,128)(2,1)}, u32[]{:S(2)}) copy-start(bf16[1024,1536]{1,0:T(8,128)(2,1)} %copy-done.15) | copy-start | bytes 9437188
  303.4 8.1 %copy-start.29 = (f32[512,1024]{1,0:T(8,128)}, f32[512,1024]{1,0:T(8,128)S(1)}, u32[]{:S(2)}) copy-start(f32[512,1024]{1,0:T(8,128)S(1)} %convert_add_fusion.8) | copy-start | bytes 6291460
  308.9 58.0 %collective-permute-start.9 = (bf16[256,1024]{1,0:T(8,128)(2,1)}, bf16[256,1024]{1,0:T(8,128)(2,1)}, u32[]{:S(2)}, u32[]{:S(2)}) collective-permute-start(bf16[256,1024]{1,0:T(8,128)(2,1)} %slice.728), channel_id=1, source_target_pairs={{0,2},{1,3},{2,0},{3,1},{4,6},{5,7},{6,4},{7,5},{8,10},{9,11},{10,... | collective-permute-start | bytes 1572872 | tf_op jit(solution)/shard_map/ppermute | solution.py:36
  323.9 30.1 %collective-permute-start.36 = (bf16[2,128,1536]{2,1,0:T(8,128)(2,1)}, bf16[2,128,1536]{2,1,0:T(8,128)(2,1)}, u32[]{:S(2)}, u32[]{:S(2)}) collective-permute-start(bf16[2,128,1536]{2,1,0:T(8,128)(2,1)} %dynamic-slice_bitcast_fusion.3), channel_id=1, source_target_pairs={{0,16},{1,17},{2,18},{3,19},{4,20},{5,21},{6,22},{7,23},{8,24},{9,... | collective-permute-start | bytes 2359304 | tf_op jit(solution)/shard_map/ppermute | solution.py:36
  343.4 12.1 %copy-start.10 = (bf16[1,2,256,1024]{3,2,1,0:T(8,128)(2,1)S(1)}, bf16[1,2,256,1024]{3,2,1,0:T(8,128)(2,1)}, u32[]{:S(2)}) copy-start(bf16[1,2,256,1024]{3,2,1,0:T(8,128)(2,1)} %get-tuple-element.82) | copy-start | bytes 3145732
  355.4 11.1 %collective-permute-start.37 = (bf16[128,1536]{1,0:T(8,128)(2,1)S(1)}, bf16[128,1536]{1,0:T(8,128)(2,1)S(1)}, u32[]{:S(2)}, u32[]{:S(2)}) collective-permute-start(bf16[128,1536]{1,0:T(8,128)(2,1)S(1)} %dynamic-slice_bitcast_fusion.6), channel_id=1, source_target_pairs={{0,8},{1,9},{2,10},{3,11},{4,12},{5,13},{6,14},{7,15},{8,0},{9,1},... | collective-permute-start | bytes 1179656 | tf_op jit(solution)/shard_map/ppermute | solution.py:36
  358.3 15.2 %copy-start.31 = (bf16[512,1024]{1,0:T(8,128)(2,1)}, bf16[512,1024]{1,0:T(8,128)(2,1)S(1)}, u32[]{:S(2)}) copy-start(bf16[512,1024]{1,0:T(8,128)(2,1)S(1)} %get-tuple-element.61) | copy-start | bytes 3145732
  358.3 15.2 %collective-permute-start.12 = (bf16[512,1024]{1,0:T(8,128)(2,1)S(1)}, bf16[512,1024]{1,0:T(8,128)(2,1)S(1)}, u32[]{:S(2)}, u32[]{:S(2)}) collective-permute-start(bf16[512,1024]{1,0:T(8,128)(2,1)S(1)} %get-tuple-element.61), channel_id=1, source_target_pairs={{0,1},{1,0},{2,3},{3,2},{4,5},{5,4},{6,7},{7,6},{8,9},{9,8},{10,11... | collective-permute-start | bytes 3145736 | tf_op jit(solution)/shard_map/ppermute | solution.py:36
  358.4 8.6 %copy-start.30 = (f32[512,1024]{1,0:T(8,128)S(1)}, f32[512,1024]{1,0:T(8,128)}, u32[]{:S(2)}) copy-start(f32[512,1024]{1,0:T(8,128)} %copy-done.29) | copy-start | bytes 6291460
  358.4 8.6 %slice-start.2 = ((f32[512]{0:T(512)}), f32[256]{0:T(256)S(1)}, s32[]{:S(2)}) async-start(f32[512]{0:T(512)} %copy-done.45), calls=%async_computation.2 | async-start | bytes 2048 | tf_op jit(solution)/shard_map/slice | solution.py:955
  358.4 15.1 %collective-permute-start.17 = (bf16[512,1024]{1,0:T(8,128)(2,1)S(1)}, bf16[512,1024]{1,0:T(8,128)(2,1)S(1)}, u32[]{:S(2)}, u32[]{:S(2)}) collective-permute-start(bf16[512,1024]{1,0:T(8,128)(2,1)S(1)} %get-tuple-element.164), channel_id=1, source_target_pairs={{0,1},{1,0},{2,3},{3,2},{4,5},{5,4},{6,7},{7,6},{8,9},{9,8},{10,11... | collective-permute-start | bytes 3145736 | tf_op jit(solution)/shard_map/ppermute | solution.py:36
  366.6 6.0 %collective-permute-start.38 = (bf16[1,2,32,1536]{3,2,1,0:T(8,128)(2,1)S(1)}, bf16[1,2,32,1536]{3,2,1,0:T(8,128)(2,1)S(1)}, u32[]{:S(2)}, u32[]{:S(2)}) collective-permute-start(bf16[1,2,32,1536]{3,2,1,0:T(8,128)(2,1)S(1)} %dynamic-slice_bitcast_fusion.9), channel_id=1, source_target_pairs={{0,2},{1,3},{2,0},{3,1},{4,6},{5,7},{6,4},{7,5},{8,10},{9,11},{10,... | collective-permute-start | bytes 589832 | tf_op jit(solution)/shard_map/ppermute | solution.py:36
  373.4 60.8 %collective-permute-start.39 = (bf16[2,1,32,1536]{3,2,0,1:T(8,128)(2,1)}, bf16[2,1,32,1536]{3,2,0,1:T(8,128)(2,1)}, u32[]{:S(2)}, u32[]{:S(2)}) collective-permute-start(bf16[2,1,32,1536]{3,2,0,1:T(8,128)(2,1)} %fusion.144), channel_id=1, source_target_pairs={{0,1},{1,0},{2,3},{3,2},{4,5},{5,4},{6,7},{7,6},{8,9},{9,8},{10,11... | collective-permute-start | bytes 589832 | tf_op jit(solution)/shard_map/ppermute | solution.py:36
  376.8 58.5 %collective-permute-start.30 = (bf16[256,1024]{1,0:T(8,128)(2,1)}, bf16[256,1024]{1,0:T(8,128)(2,1)}, u32[]{:S(2)}, u32[]{:S(2)}) collective-permute-start(bf16[256,1024]{1,0:T(8,128)(2,1)} %constant_dynamic-slice_fusion.2), channel_id=1, source_target_pairs={{0,16},{1,17},{2,18},{3,19},{4,20},{5,21},{6,22},{7,23},{8,24},{9,... | collective-permute-start | bytes 1572872 | tf_op jit(solution)/shard_map/ppermute | solution.py:36
  401.4 51.9 %collective-permute-start.18 = (bf16[512,1024]{1,0:T(8,128)(2,1)}, bf16[512,1024]{1,0:T(8,128)(2,1)}, u32[]{:S(2)}, u32[]{:S(2)}) collective-permute-start(bf16[512,1024]{1,0:T(8,128)(2,1)} %convolution_convert_fusion.2), channel_id=1, source_target_pairs={{0,1},{1,0},{2,3},{3,2},{4,5},{5,4},{6,7},{7,6},{8,9},{9,8},{10,11... | collective-permute-start | bytes 3145736 | tf_op jit(solution)/shard_map/ppermute | solution.py:36
  426.8 31.6 %collective-permute-start.13 = (bf16[512,1024]{1,0:T(8,128)(2,1)}, bf16[512,1024]{1,0:T(8,128)(2,1)}, u32[]{:S(2)}, u32[]{:S(2)}) collective-permute-start(bf16[512,1024]{1,0:T(8,128)(2,1)} %convolution_convert_fusion.3), channel_id=1, source_target_pairs={{0,1},{1,0},{2,3},{3,2},{4,5},{5,4},{6,7},{7,6},{8,9},{9,8},{10,11... | collective-permute-start | bytes 3145736 | tf_op jit(solution)/shard_map/ppermute | solution.py:36
  436.8 13.7 %collective-permute-start.31 = (bf16[256,1024]{1,0:T(8,128)(2,1)S(1)}, bf16[256,1024]{1,0:T(8,128)(2,1)}, u32[]{:S(2)}, u32[]{:S(2)}) collective-permute-start(bf16[256,1024]{1,0:T(8,128)(2,1)S(1)} %add_convert_fusion.2), channel_id=1, source_target_pairs={{1,9},{3,11},{5,13},{7,15},{8,0},{10,2},{12,4},{14,6},{17,25},{19,... | collective-permute-start | bytes 1572872 | tf_op jit(solution)/shard_map/ppermute | solution.py:36
  449.8 25.4 %collective-permute-start.25 = (bf16[2,2,128,1024]{3,2,1,0:T(8,128)(2,1)S(1)}, bf16[2,2,128,1024]{3,2,1,0:T(8,128)(2,1)S(1)}, u32[]{:S(2)}, u32[]{:S(2)}) collective-permute-start(bf16[2,2,128,1024]{3,2,1,0:T(8,128)(2,1)S(1)} %dynamic-slice_bitcast_fusion.1), channel_id=1, source_target_pairs={{0,4},{1,5},{2,6},{3,7},{4,0},{5,1},{6,2},{7,3},{8,12},{9,13},{10,... | collective-permute-start | bytes 3145736 | tf_op jit(solution)/shard_map/ppermute | solution.py:36
  451.7 29.8 %collective-permute-start.32 = (bf16[256,1024]{1,0:T(8,128)(2,1)S(1)}, bf16[256,1024]{1,0:T(8,128)(2,1)S(1)}, u32[]{:S(2)}, u32[]{:S(2)}) collective-permute-start(bf16[256,1024]{1,0:T(8,128)(2,1)S(1)} %add_convert_fusion.1), channel_id=1, source_target_pairs={{2,6},{4,0},{11,15},{13,9},{18,22},{20,16},{27,31},{29,25}} | collective-permute-start | bytes 1572872 | tf_op jit(solution)/shard_map/ppermute | solution.py:36
  456.0 27.1 %collective-permute-start.19 = (bf16[256,1024]{1,0:T(8,128)(2,1)S(1)}, bf16[256,1024]{1,0:T(8,128)(2,1)S(1)}, u32[]{:S(2)}, u32[]{:S(2)}) collective-permute-start(bf16[256,1024]{1,0:T(8,128)(2,1)S(1)} %slice.726), channel_id=1, source_target_pairs={{0,2},{1,3},{2,0},{3,1},{4,6},{5,7},{6,4},{7,5},{8,10},{9,11},{10,... | collective-permute-start | bytes 1572872 | tf_op jit(solution)/shard_map/ppermute | solution.py:36
  458.4 16.8 %copy-start.17 = (bf16[1024,1024]{1,0:T(8,128)(2,1)S(1)}, bf16[1024,1024]{1,0:T(8,128)(2,1)}, u32[]{:S(2)}) copy-start(bf16[1024,1024]{1,0:T(8,128)(2,1)} %fusion.66) | copy-start | bytes 6291460
  461.2 22.0 %collective-permute-start.14 = (bf16[256,1024]{1,0:T(8,128)(2,1)S(1)}, bf16[256,1024]{1,0:T(8,128)(2,1)S(1)}, u32[]{:S(2)}, u32[]{:S(2)}) collective-permute-start(bf16[256,1024]{1,0:T(8,128)(2,1)S(1)} %slice.727), channel_id=1, source_target_pairs={{0,2},{1,3},{2,0},{3,1},{4,6},{5,7},{6,4},{7,5},{8,10},{9,11},{10,... | collective-permute-start | bytes 1572872 | tf_op jit(solution)/shard_map/ppermute | solution.py:36
  475.6 7.5 %copy-start.3 = (bf16[2,256,1024]{2,1,0:T(8,128)(2,1)S(1)}, bf16[2,256,1024]{2,1,0:T(8,128)(2,1)}, u32[]{:S(2)}) copy-start(bf16[2,256,1024]{2,1,0:T(8,128)(2,1)} %x_ref.1) | copy-start | bytes 3145732
  475.7 22.6 %collective-permute-start.26 = (bf16[2,128,1024]{2,1,0:T(8,128)(2,1)S(1)}, bf16[2,128,1024]{2,1,0:T(8,128)(2,1)S(1)}, u32[]{:S(2)}, u32[]{:S(2)}) collective-permute-start(bf16[2,128,1024]{2,1,0:T(8,128)(2,1)S(1)} %dynamic-slice_bitcast_fusion.4), channel_id=1, source_target_pairs={{0,16},{1,17},{2,18},{3,19},{4,20},{5,21},{6,22},{7,23},{8,24},{9,... | collective-permute-start | bytes 1572872 | tf_op jit(solution)/shard_map/ppermute | solution.py:36
  481.8 35.3 %collective-permute-start.33 = (bf16[128,1024]{1,0:T(8,128)(2,1)S(1)}, bf16[128,1024]{1,0:T(8,128)(2,1)S(1)}, u32[]{:S(2)}, u32[]{:S(2)}) collective-permute-start(bf16[128,1024]{1,0:T(8,128)(2,1)S(1)} %constant_dynamic-slice_fusion.1), channel_id=1, source_target_pairs={{0,2},{6,4},{9,11},{15,13},{16,18},{22,20},{25,27},{31,29}} | collective-permute-start | bytes 786440 | tf_op jit(solution)/shard_map/ppermute | solution.py:36
  484.0 16.0 %copy-start.49 = (f32[256]{0:T(256)S(1)}, f32[256]{0:T(256)}, u32[]{:S(2)}) copy-start(f32[256]{0:T(256)} %copy-done.48) | copy-start | bytes 3076
  484.0 19.0 %copy-start.47 = (f32[256]{0:T(256)S(1)}, f32[256]{0:T(256)}, u32[]{:S(2)}) copy-start(f32[256]{0:T(256)} %copy-done.46) | copy-start | bytes 3076
  484.1 24.0 %copy-start.7 = (f32[512,1024]{1,0:T(8,128)S(1)}, f32[512,1024]{1,0:T(8,128)}, u32[]{:S(2)}) copy-start(f32[512,1024]{1,0:T(8,128)} %get-tuple-element.165) | copy-start | bytes 6291460
  484.1 14.5 %collective-permute-start.20 = (f32[2304]{0:T(1024)S(1)}, f32[2304]{0:T(1024)S(1)}, u32[]{:S(2)}, u32[]{:S(2)}) collective-permute-start(f32[2304]{0:T(1024)S(1)} %maximum_add_fusion.4), channel_id=1, source_target_pairs={{0,1},{1,0},{2,3},{3,2},{4,5},{5,4},{6,7},{7,6},{8,9},{9,8},{10,11... | collective-permute-start | bytes 27656 | tf_op jit(solution)/shard_map/ppermute | solution.py:36
  498.6 17.3 %collective-permute-start.27 = (bf16[128,1024]{1,0:T(8,128)(2,1)S(1)}, bf16[128,1024]{1,0:T(8,128)(2,1)S(1)}, u32[]{:S(2)}, u32[]{:S(2)}) collective-permute-start(bf16[128,1024]{1,0:T(8,128)(2,1)S(1)} %dynamic-slice_bitcast_fusion.7), channel_id=1, source_target_pairs={{0,8},{1,9},{2,10},{3,11},{4,12},{5,13},{6,14},{7,15},{8,0},{9,1},... | collective-permute-start | bytes 786440 | tf_op jit(solution)/shard_map/ppermute | solution.py:36
  498.7 3.8 collective-permute-start.21
  502.4 3.7 collective-permute-start.22
  506.1 3.7 collective-permute-start.23
  509.8 4.9 collective-permute-start.24
  515.9 5.0 collective-permute-start.28
  517.2 3.9 collective-permute-start.34
  521.0 1.4 collective-permute-start.29
  (67 other events, 228.1 us)

commit v3 on v2

--- a/solution.py
+++ b/solution.py
@@ -481,9 +481,13 @@
             device_id_type=MESH,
         )
 
-    def start(self, src, dst, slot, when=None, **to):
+    def plan(self, src, dst, slot, when=None, **to):
         copy = self.copy(src, dst, slot, **to)
         self.started.append((copy, when))
+        return copy
+
+    def start(self, src, dst, slot, when=None, **to):
+        copy = self.plan(src, dst, slot, when, **to)
         if when is None:
             copy.start()
         else:
@@ -497,17 +501,17 @@
             else:
                 pl.when(when)(copy.wait_send)
 
-    def greet(self, dp_bits, seq_masks):
+    def greet(self, dp_masks, seq_masks):
         barrier = pltpu.get_barrier_semaphore()
-        for bit in dp_bits:
+        for mask in dp_masks:
             pl.semaphore_signal(
-                barrier, inc=1, device_id={"dp": flip(self.d, bit)}, device_id_type=MESH
+                barrier, inc=1, device_id={"dp": self.dp_at(mask)}, device_id_type=MESH
             )
         for mask in seq_masks:
             pl.semaphore_signal(
                 barrier, inc=1, device_id={"seq": self.seq_at(mask)}, device_id_type=MESH
             )
-        pl.semaphore_wait(barrier, len(dp_bits) + len(seq_masks))
+        pl.semaphore_wait(barrier, len(dp_masks) + len(seq_masks))
 
     def seq_at(self, mask):
         s = self.s
@@ -525,48 +529,36 @@
 
 
 class Gather:
-    def __init__(self, links, block, order):
-        self.links, self.block, self.order = links, block, order
-        self.base = links.slots(8)
+    def __init__(self, links, block):
+        base = links.slots(8)
         self.copies = {}
-
-    def send(self, r, bit):
-        src = self.block(self.links.dp_at(r))
-        self.copies[r | 1 << bit] = self.links.start(
-            src, src, self.base + (r | 1 << bit), dp=flip(self.links.d, bit)
-        )
+        for r, mask in ((0, 1), (0, 2), (0, 4), (2, 1), (4, 2), (4, 1), (6, 1)):
+            src = block(links.dp_at(r))
+            self.copies[r | mask] = links.plan(src, src, base + (r | mask), dp=links.dp_at(mask))
 
     def got(self, r):
         self.copies[r].wait_recv()
 
     def first(self):
-        for bit in self.order:
-            self.send(0, bit)
-
-    def second(self):
-        a, b, c = self.order
-        self.got(1 << a)
-        self.send(1 << a, b)
-        self.send(1 << a, c)
-
-    def third(self):
-        a, b, c = self.order
-        self.got(1 << b)
-        self.send(1 << b, c)
-        self.got(1 << a | 1 << b)
-        self.send(1 << a | 1 << b, c)
+        for mask in (4, 2, 1):
+            self.copies[mask].start()
+
+    def relay(self, r):
+        self.got(r)
+        if r == 4:
+            self.copies[6].start()
+        self.copies[r | 1].start()
 
     def last(self):
-        a, b, c = self.order
-        for r in (0, 1 << a, 1 << b, 1 << a | 1 << b):
-            self.got(r | 1 << c)
+        for r in (1, 3, 5, 7):
+            self.got(r)
 
 
 def first_kernel(
     heads,
     a_ref, c_ref, out_ref, down_ref, x_ref, g_ref, gains_ref, qg_ref, kg_ref, cos_ref, sin_ref,
     xr_ref, gr_ref, wa_ref, wc_ref, wo_ref, wd_ref, n_ref, qkv_ref, pre_ref, o_ref, log_ref, gain_ref,
-    w_v, x_v, n_v, qkv_v, pre_v, o_v, sum_v, got_v, send, recv, local,
+    w_v, x_v, n_v, qkv_v, pre_v, o_v, got_v, send, recv, local,
 ):
     links = Links(send, recv)
     d, s = links.d, links.s
@@ -585,7 +577,7 @@
         copy.start()
         locals_[name] = copy
 
-    links.greet((0, 1, 2), (1, 2, 3))
+    links.greet((1, 2, 4), (1, 2, 3))
 
     def exchange(src, dst):
         base = links.slots(4)
@@ -594,22 +586,29 @@
             for k in (2, 3, 1)
         ]
 
+    gain_slots = links.slots(4)
+    gain_own = [
+        links.start(gains_ref, got_v.at[d, s], gain_slots + k, seq=links.seq_at(k)) for k in (2, 3, 1)
+    ]
+    got_v[d, s] = gains_ref[...]
     a_own = exchange(a_ref, wa_ref)
     near("a", a_ref.at[s], wa_ref.at[d, s])
 
-    gain_slots = links.slots(5)
-    gain_to = [dict(seq=links.seq_at(1)), dict(seq=links.seq_at(2))] + [dict(dp=flip(d, b)) for b in range(3)]
-    gain_copy = links.start(gains_ref, got_v.at[0], gain_slots, **gain_to[0])
-
-    x_slots = links.slots(3 * sequences)
-    x_far = [
-        links.start(x_ref.at[n], xr_ref.at[n, 1], x_slots + 3 * n, seq=links.seq_at(2))
-        for n in range(sequences)
-    ]
-    x_near = [
-        links.start(x_ref.at[n], xr_ref.at[n, 2], x_slots + 3 * n + 1, seq=links.seq_at(1))
-        for n in range(sequences)
-    ]
+    x_slots, g_slots = links.slots(3 * sequences), links.slots(3 * sequences)
+
+    def spread(own, everywhere, base, n):
+        copies = [
+            links.start(own.at[n], everywhere.at[n, k], base + 3 * n + k - 1, seq=links.seq_at(3 - k))
+            for k in (1, 2)
+        ]
+        onward = links.plan(everywhere.at[n, 1], everywhere.at[n, 3], base + 3 * n + 2, seq=links.seq_at(1))
+        return copies + [onward]
+
+    def pass_on(copies):
+        copies[0].wait_recv()
+        copies[2].start()
+
+    x_copies = [spread(x_ref, xr_ref, x_slots, 0)]
     c_own = exchange(c_ref, wc_ref)
     near("c", c_ref.at[s], wc_ref.at[d, s])
     for n in range(sequences):
@@ -626,42 +625,20 @@
         )
         for k in (1, 2, 3)
     ]
-
-    for copy in a_own:
+    x_copies += [spread(x_ref, xr_ref, x_slots, n) for n in range(1, sequences)]
+
+    for copy in gain_own + a_own:
         copy.wait_recv()
     locals_["a"].wait()
-    half = blocks // 2
-    gathers_a = [
-        Gather(links, lambda at, h=h: wa_ref.at[at, pl.ds(h * half, half)], order)
-        for h, order in ((0, (1, 2, 0)), (1, (0, 2, 1)))
-    ]
-    for gather in gathers_a:
-        gather.first()
-    gather_d = Gather(links, lambda at: wd_ref.at[at], (1, 2, 0))
-    gather_c = Gather(links, lambda at: wc_ref.at[at], (1, 2, 0))
-
-    for stage in range(5):
-        gain_copy.wait_recv()
-        before = gains_ref[...] if stage == 0 else sum_v[stage - 1]
-        if stage == 4:
-            gain_ref[...] = before + got_v[4]
-        else:
-            sum_v[stage] = before + got_v[stage]
-            gain_copy = links.start(
-                sum_v.at[stage], got_v.at[stage + 1], gain_slots + stage + 1, **gain_to[stage + 1]
-            )
-
-    for gather in gathers_a:
-        gather.second()
-
-    for copy in c_own:
-        copy.wait_recv()
-    locals_["c"].wait()
-    gather_c.first()
-
-    x_on = []
-    x_far[0].wait_recv()
-    x_on.append(links.start(xr_ref.at[0, 1], xr_ref.at[0, 3], x_slots + 2, seq=links.seq_at(1)))
+    gather_a, gather_c, gather_d, gather_gain = (
+        Gather(links, lambda at, ref=ref: ref.at[at]) for ref in (wa_ref, wc_ref, wd_ref, got_v)
+    )
+    gather_gain.first()
+    gather_a.first()
+    for r in (2, 4, 6):
+        gather_gain.relay(r)
+
+    pass_on(x_copies[0])
 
     @pl.when(holder)
     def _():
@@ -672,44 +649,31 @@
         own.wait()
 
     local_used[0] += 1
+    gather_a.relay(2)
+    gather_a.relay(4)
+    gather_a.relay(6)
     out_y = links.start(wo_ref.at[z1], wo_ref.at[z1], out_slots + 4, when=holder, dp=flip(d, 0))
-
-    for gather in gathers_a:
-        gather.third()
+    for copy in c_own:
+        copy.wait_recv()
+    locals_["c"].wait()
+    gather_c.first()
+    g_copies = [spread(g_ref, gr_ref, g_slots, n) for n in range(sequences)]
+    for n in range(sequences):
+        near(f"g{n}", g_ref.at[n], gr_ref.at[n, 0])
     locals_["d"].wait()
     gather_d.first()
 
-    g_slots = links.slots(3 * sequences)
-    g_far = [
-        links.start(g_ref.at[n], gr_ref.at[n, 1], g_slots + 3 * n, seq=links.seq_at(2))
-        for n in range(sequences)
-    ]
-    g_near = [
-        links.start(g_ref.at[n], gr_ref.at[n, 2], g_slots + 3 * n + 1, seq=links.seq_at(1))
-        for n in range(sequences)
-    ]
-    for n in range(sequences):
-        near(f"g{n}", g_ref.at[n], gr_ref.at[n, 0])
-    g_on = []
-
-    for gather in gathers_a:
-        gather.last()
-    near("w", wa_ref, w_v)
-
     def wait_x(n):
-        if n:
-            x_far[n].wait_recv()
-            x_on.append(
-                links.start(xr_ref.at[n, 1], xr_ref.at[n, 3], x_slots + 3 * n + 2, seq=links.seq_at(1))
-            )
         locals_[f"x{n}"].wait()
-        x_near[n].wait_recv()
-        x_on[n].wait_recv()
+        for copy in x_copies[n][1:]:
+            copy.wait_recv()
         near(f"xv{n}", xr_ref.at[n], x_v)
         locals_[f"xv{n}"].wait()
 
-    def project_part(n):
+    def project_part(n, meanwhile=()):
         def step(i, carry):
+            for k, action in enumerate(meanwhile):
+                pl.when(i == k)(action)
             at = place_of(i)
             x = x_v[at].astype(F32)
             normed = (x * rms_scale(x) * gain_ref[0:1, :]).astype(BF16)
@@ -734,8 +698,10 @@
         near(f"qkv{n}", qkv_v.at[n], qkv_ref.at[n])
         near(f"pre{n}", pre_v.at[n], pre_ref.at[n])
 
-    def attend_part(n, start, stop):
+    def attend_part(n, meanwhile=()):
         def step(h, carry):
+            for k, action in enumerate(meanwhile):
+                pl.when(h == k)(action)
             j, g = lax.div(h, 2), lax.rem(h, 2)
             lanes = lambda at: pl.ds(pl.multiple_of(at * HEAD_SIZE, HEAD_SIZE), HEAD_SIZE)
             values_t = qkv_v[n, :, lanes(4 * j + 3)].T
@@ -750,38 +716,45 @@
                 log_ref[n, h, :, i * piece : (i + 1) * piece] = highest + jnp.log(total)
             return carry
 
-        lax.fori_loop(start, stop, step, 0)
+        lax.fori_loop(0, heads, step, 0)
 
     wait_x(0)
+    gather_a.last()
+    near("w", wa_ref, w_v)
     locals_["w"].wait()
-    project_part(0)
-    gather_c.second()
-    pl.when((across == 1) & (beside == 0))(out_y.wait_recv)
-    out_z0 = links.start(wo_ref.at[z1], wo_ref.at[z1], out_slots + 5, when=beside == 0, dp=flip(d, 1))
-    gather_d.second()
-    attend_part(0, 0, heads // 2)
-    gather_c.third()
-    pl.when(beside == 1)(out_z0.wait_recv)
-    out_z1 = links.start(wo_ref.at[z1], wo_ref.at[z1], out_slots + 6, dp=flip(d, 2))
-    attend_part(0, heads // 2, heads)
+
+    gather_gain.last()
+    for at in range(got_v.shape[0]):
+        gain_ref[:, at * 128 : (at + 1) * 128] = jnp.sum(got_v[at], axis=0)
+
+    out_z1 = links.plan(wo_ref.at[z1], wo_ref.at[z1], out_slots + 5, when=beside == 0, dp=flip(d, 2))
+    out_z0 = links.plan(wo_ref, wo_ref, out_slots + 6, when=beside == 0, dp=flip(d, 1))
+
+    def out_next():
+        pl.when((across == 1) & (beside == 0))(out_y.wait_recv)
+        pl.when(beside == 0)(out_z1.start)
+
+    def out_last():
+        @pl.when(beside == 0)
+        def _():
+            out_z1.wait_recv()
+            out_z0.start()
+
+    nothing = lambda: None
+    project_part(0, [out_next, lambda: gather_c.relay(2), lambda: pass_on(x_copies[1]), lambda: gather_c.relay(4)])
+    attend_part(0, [nothing, out_last, lambda: gather_c.relay(6), lambda: gather_d.relay(2)])
     near("o0", o_v.at[0], o_ref.at[0])
     for n in range(1, sequences):
         wait_x(n)
-        project_part(n)
-        if n == 1:
-            gather_d.third()
-            for m in range(sequences):
-                g_far[m].wait_recv()
-                g_on.append(
-                    links.start(gr_ref.at[m, 1], gr_ref.at[m, 3], g_slots + 3 * m + 2, seq=links.seq_at(1))
-                )
-        attend_part(n, 0, heads)
+        project_part(n, [lambda: gather_d.relay(4), nothing, lambda: pass_on(g_copies[0])])
+        attend_part(n, [lambda: gather_d.relay(6), lambda: pass_on(g_copies[1])])
         near(f"o{n}", o_v.at[n], o_ref.at[n])
     gather_c.last()
     gather_d.last()
-    out_z1.wait_recv()
-    for copy in g_near + g_on:
-        copy.wait_recv()
+    pl.when(beside == 1)(out_z0.wait_recv)
+    for pair in g_copies:
+        for copy in pair[1:]:
+            copy.wait_recv()
     for n in range(sequences):
         for name in ("g", "n", "qkv", "pre", "o"):
             locals_[f"{name}{n}"].wait()
@@ -814,7 +787,7 @@
             shape((sequences, heads, 1, length), F32),
             shape((8, width), F32),
         ),
-        in_specs=[hbm] * 6 + [vmem] * 5,
+        in_specs=[vmem] * 11,
         out_specs=[hbm] * 10 + [vmem] * 2,
         scratch_shapes=[
             pltpu.VMEM((dp, blocks, rows, columns), BF16),
@@ -823,8 +796,7 @@
             pltpu.VMEM((sequences, length, columns), BF16),
             pltpu.VMEM((sequences, length, pre_columns), F32),
             pltpu.VMEM((sequences, blocks, piece, heads * HEAD_SIZE), BF16),
-            pltpu.VMEM((4, 8, width), F32),
-            pltpu.VMEM((5, 8, width), F32),
+            pltpu.VMEM((dp, blocks, 8, width // dp), F32),
             pltpu.SemaphoreType.DMA((slots,)),
             pltpu.SemaphoreType.DMA((slots,)),
             pltpu.SemaphoreType.DMA((24,)),
@@ -885,14 +857,14 @@
     units = dp * down_rows
     package_mlp = jnp.concatenate([by_unit(w_gate), by_unit(w_up)], axis=2)
 
-    fused = (dp, seq) == (8, 4) and rows % 16 == 0 and down_rows % 16 == 0
+    fused = (dp, seq) == (8, 4) and width == 128 * dp and rows % 16 == 0 and down_rows % 16 == 0
     if fused:
-        gains = jnp.zeros((8, count, width // count), F32)
-        gains = lax.dynamic_update_slice(gains, own_gains.astype(F32)[:, None], (0, index, 0))
+        gains = jnp.zeros((8, seq, width // count), F32)
+        gains = lax.dynamic_update_slice(gains, own_gains.astype(F32)[:, None], (0, wires.s, 0))
         (
             x_rel, g_rel, w_in, w_mlp, w_o, w_d, all_normed, all_qkv, all_pre, all_mixed, all_log, gains
         ) = first(
-            package_in, package_mlp, w_out, w_down, hidden_in, cotangent, gains.reshape(8, width),
+            package_in, package_mlp, w_out, w_down, hidden_in, cotangent, gains.reshape(8, -1),
             query_gain_row, key_gain_row, cosine, sine, dp, 2 * heads_kv // seq,
         )
         w_in, w_mlp = w_in.reshape(width, -1), w_mlp.reshape(width, -1)

time: 529 us -> 493 us (0.932)
  Pallas kernels: 180 us -> 138 us
  waiting for transfers between devices: 133 us -> 140 us
    pallas_call x1, Pallas kernels: 145 us -> 103 us  [first(): pl.pallas_call(functools.partial(first_kernel, heads), name='first', out_...]
    ppermute x43, waiting for transfers between devices: 133 us -> 140 us  [swap(): return lax.ppermute(value, AXES, pairs)]
  transfers between devices with their start and end apart: 43 -> 43, of which waited for: 18 -> 18; matrix products, arithmetic and copies ran while one was open for 25% -> 27% of each run, Pallas kernels for 7% -> 7%
where the time goes in v3:
time: 493 us; the launch traced here: 489 us
  waiting for transfers between devices  140 us (28%)
  Pallas kernels  138 us (28%)
  matrix products  87.4 us (18%)
  local copies, waits for them, and re-layouts  57.6 us (12%)
  starting transfers between devices  32.2 us (7%)
  other arithmetic  31.7 us (6%)
    ppermute x43, waiting for transfers between devices, swap(): return lax.ppermute(value, AXES, pairs)  140 us
    pallas_call x1, Pallas kernels, first(): pl.pallas_call(functools.partial(first_kernel, heads), name='first', out_...  103 us
    dot_general x12, matrix products, dot_t(): lax.dot_general(a, b, (((1,), (1,)), ((), ())), preferred_element_type=F32)  43 us
    pallas_call x2, Pallas kernels, attend_back(): pl.pallas_call(functools.partial(backward_kernel, blocks, x_count), name=...  34.7 us
    ppermute x43, starting transfers between devices, swap(): return lax.ppermute(value, AXES, pairs)  32.2 us
    dot_general x4, matrix products, t_dot(): lax.dot_general(a, b, (((0,), (0,)), ((), ())), preferred_element_type=F32)  22.6 us
    dot_general x10, matrix products, dot(): lax.dot_general(a, b, (((1,), (0,)), ((), ())), preferred_element_type=F32)  21.9 us
    unnamed x190, local copies, waits for them, and re-layouts  10.3 us
  transfers between devices with their start and end apart: 43, of which 18 were waited for; matrix products, arithmetic and copies ran while one was open for 27% of the time, Pallas kernels for 7%

profile of v3, /device:TPU:0, one launch (start us, length us, event | category | flops | bytes accessed | tf_op | source)
XLA Modules:
  0.0 489.0 jit_solution(13893825325011148757)
XLA Ops:
  6.1 1.9 fusion.149
  11.4 103.1 %first.1 = (bf16[2,4,256,1024]{3,2,1,0:T(8,128)(2,1)}, bf16[2,4,256,1024]{3,2,1,0:T(8,128)(2,1)}, bf16[8,4,32,1024]{3,2,1,0:T(8,128)(2,1)}, bf16[8,4,32,1536]{3,...) custom-call(bf16[4,32,1024]{2,1,0:T(8,128)(2,1)} %pad_maximum_fusion, ...), custom_call_target="tpu_custom_call" | custom-call | tf_op jit(solution)/shard_map/first/pallas_call | solution.py:773
  114.5 2.7 fusion.185
  117.2 1.7 convolution_convert_fusion.4
  119.4 1.7 convolution_convert_fusion.5
  121.2 1.5 fusion.182
  127.8 2.4 fusion.180
  130.8 2.6 fusion.104
  133.4 2.1 collective-permute-start.6
  136.9 2.5 slice_bitcast_fusion.2
  140.9 18.6 %collective-permute-done.6 = bf16[512,1024]{1,0:T(8,128)(2,1)S(1)} collective-permute-done((bf16[512,1024]{1,0:T(8,128)(2,1)S(1)}, bf16[512,1024]{1,0:T(8,128)(2,1)S(1)}, u32[]{:S(2)}, u32[]{:S(2)}) %collective-permute-start.6) | collective-permute-done | bytes 1048608 | tf_op jit(solution)/shard_map/ppermute | solution.py:36
  159.8 1.9 multiply_reduce_fusion.2
  161.7 20.1 %collective-permute-done.1 = bf16[512,1024]{1,0:T(8,128)(2,1)S(1)} collective-permute-done((bf16[512,1024]{1,0:T(8,128)(2,1)S(1)}, bf16[512,1024]{1,0:T(8,128)(2,1)S(1)}, u32[]{:S(2)}, u32[]{:S(2)}) %collective-permute-start.1) | collective-permute-done | bytes 1048608 | tf_op jit(solution)/shard_map/ppermute | solution.py:36
  183.8 1.8 copy-done.8
  185.6 2.5 fusion.178
  188.7 3.1 slice_bitcast_fusion
  191.9 3.4 fusion.43
  195.3 3.1 multiply_convert_fusion.3
  198.5 2.4 convolution_convert_fusion.1
  200.9 3.4 fusion.48
  204.3 12.5 %multiply_convert_fusion.1 = (bf16[1024,768]{1,0:T(8,128)(2,1)S(1)}, bf16[1024,768]{1,0:T(8,128)(2,1)}, bf16[1024,768]{1,0:T(8,128)(2,1)S(1)}) fusion(f32[1024,1536]{1,0:T(8,128)S(1)} %fusion.48, bf16[1024,1024]{1,0:T(8,128)(2,1)S(1)} %bitcast.319, bf16[768,1024]{1,0:T(8,128)(2,1)S(1)} %bitcast.366), kind=kOutput, calls=%fused_computation.43 | convolution fusion | flops 1622409216 | bytes 14680064 | tf_op jit(solution)/shard_map/dot_general | solution.py:199
  216.9 3.5 fusion.71
  221.4 1.9 collective-permute-start.40
  223.3 2.8 fusion.96
  226.4 2.8 fusion.95
  229.5 10.8 %fusion.30 = bf16[1024,1536]{1,0:T(8,128)(2,1)S(1)} fusion(bf16[1024,768]{1,0:T(8,128)(2,1)} %get-tuple-element.70, bf16[1024,768]{1,0:T(8,128)(2,1)} %copy-done.81, bf16[1024,768]{1,0:T(8,128)(2,1)} %copy-done.79, bf16[1024,768]{1,0:T(8,128)(2,1)} %copy-done.77, bf16[512,1024]{1,0:T(8,128)(2,1)} %copy-done.72, bf16[512,1024]{1,0:T(8,128)(2,1)} %copy-done.41, ...), kind=kOutput, calls=%fused_computation.30 | convolution fusion | flops 6485966848 | bytes 13631488 | tf_op jit(solution)/shard_map/dot_general | solution.py:203
  240.3 4.0 convolution_convert_fusion
  247.9 3.0 fusion.195
  252.5 4.4 fusion.194
  259.6 7.5 %collective-permute-done.41 = bf16[2,96,1024]{2,1,0:T(8,128)(2,1)S(1)} collective-permute-done((bf16[2,96,1024]{2,1,0:T(8,128)(2,1)S(1)}, bf16[2,96,1024]{2,1,0:T(8,128)(2,1)S(1)}, u32[]{:S(2)}, u32[]{:S(2)}) %collective-permute-start.41) | collective-permute-done | bytes 393248 | tf_op jit(solution)/shard_map/ppermute | solution.py:36
  270.0 4.5 collective-permute-done.42
  276.7 4.4 collective-permute-done.35
  284.1 15.5 %collective-permute-done.11 = bf16[512,1024]{1,0:T(8,128)(2,1)S(1)} collective-permute-done((bf16[512,1024]{1,0:T(8,128)(2,1)S(1)}, bf16[512,1024]{1,0:T(8,128)(2,1)S(1)}, u32[]{:S(2)}, u32[]{:S(2)}) %collective-permute-start.11) | collective-permute-done | bytes 1048608 | tf_op jit(solution)/shard_map/ppermute | solution.py:36
  299.8 2.7 multiply_reduce_fusion.1
  302.5 16.7 %collective-permute-done.36 = bf16[2,128,1536]{2,1,0:T(8,128)(2,1)} collective-permute-done((bf16[2,128,1536]{2,1,0:T(8,128)(2,1)}, bf16[2,128,1536]{2,1,0:T(8,128)(2,1)}, u32[]{:S(2)}, u32[]{:S(2)}) %collective-permute-start.36) | collective-permute-done | bytes 786464 | tf_op jit(solution)/shard_map/ppermute | solution.py:36
  320.7 2.8 fusion.174
  324.1 1.8 fusion.120
  325.9 5.8 %collective-permute-done.37 = bf16[128,1536]{1,0:T(8,128)(2,1)S(1)} collective-permute-done((bf16[128,1536]{1,0:T(8,128)(2,1)S(1)}, bf16[128,1536]{1,0:T(8,128)(2,1)S(1)}, u32[]{:S(2)}, u32[]{:S(2)}) %collective-permute-start.37) | collective-permute-done | bytes 393248 | tf_op jit(solution)/shard_map/ppermute | solution.py:36
  334.6 3.3 collective-permute-done.38
  338.7 2.4 fusion.90
  342.0 2.2 fusion.97
  344.2 17.2 %attend_back.3 = (bf16[4,256,1024]{2,1,0:T(8,128)(2,1)}, f32[1,128]{1,0:T(1,128)}, f32[1,128]{1,0:T(1,128)}) custom-call(s32[1]{0:T(128)} %bitcast.33.s_ref, bf16[1024,1024]{1,0:T(8,128)(2,1)} %get-tuple-element.79.q_ref.k_ref.v_ref, bf16[1024,1024]{1,0:T(8,128)(2,1)} %get-tuple-element.79.q_ref.k_ref.v_ref, ...), custom_call_target="tpu_custom_call" | custom-call | flops 2684354560 | bytes 12582912 | tf_op jit(solution)/shard_map/attend_back/pallas_call | solution.py:412
  361.5 2.8 fusion.183
  364.3 2.3 convolution_convert_fusion.2
  367.1 2.3 fusion.100
  369.4 17.5 %attend_back.2 = (bf16[4,256,1024]{2,1,0:T(8,128)(2,1)}, f32[1,128]{1,0:T(1,128)}, f32[1,128]{1,0:T(1,128)}) custom-call(s32[1]{0:T(128)} %bitcast.33.s_ref, bf16[1024,1024]{1,0:T(8,128)(2,1)} %get-tuple-element.80.q_ref.k_ref.v_ref, bf16[1024,1024]{1,0:T(8,128)(2,1)} %get-tuple-element.80.q_ref.k_ref.v_ref, ...), custom_call_target="tpu_custom_call" | custom-call | flops 2684354560 | bytes 12582912 | tf_op jit(solution)/shard_map/attend_back/pallas_call | solution.py:412
  386.9 2.9 fusion.184
  389.7 2.3 convolution_convert_fusion.3
  393.6 5.8 %fusion.66 = bf16[1024,1024]{1,0:T(8,128)(2,1)} fusion(bf16[1024,1024]{1,0:T(8,128)(2,1)S(1)} %bitcast.315, bf16[1024,1024]{1,0:T(8,128)(2,1)S(1)} %bitcast.316, bf16[1024,1024]{1,0:T(8,128)(2,1)S(1)} %bitcast.318, bf16[1024,1024]{1,0:T(8,128)(2,1)S(1)} %bitcast.317), kind=kOutput, calls=%fused_computation.101 | convolution fusion | flops 4312793088 | bytes 10485760 | tf_op jit(solution)/shard_map/dot_general | solution.py:203
  406.7 2.2 reshape.323
  411.3 2.2 reshape.325
  416.7 1.5 collective-permute-start.32
  418.3 2.6 convert_add_fusion.4
  421.0 2.6 collective-permute-start.19
  423.6 2.7 convert_add_fusion.6
  426.4 13.9 %collective-permute-done.25 = bf16[2,2,128,1024]{3,2,1,0:T(8,128)(2,1)S(1)} collective-permute-done((bf16[2,2,128,1024]{3,2,1,0:T(8,128)(2,1)S(1)}, bf16[2,2,128,1024]{3,2,1,0:T(8,128)(2,1)S(1)}, u32[]{:S(2)}, u32[]{:S(2)}) %collective-permute-start.25) | collective-permute-done | bytes 1048608 | tf_op jit(solution)/shard_map/ppermute | solution.py:36
  440.9 2.4 collective-permute-start.26
  443.3 3.4 collective-permute-done.32
  449.4 14.1 %collective-permute-done.26 = bf16[2,128,1024]{2,1,0:T(8,128)(2,1)S(1)} collective-permute-done((bf16[2,128,1024]{2,1,0:T(8,128)(2,1)S(1)}, bf16[2,128,1024]{2,1,0:T(8,128)(2,1)S(1)}, u32[]{:S(2)}, u32[]{:S(2)}) %collective-permute-start.26) | collective-permute-done | bytes 524320 | tf_op jit(solution)/shard_map/ppermute | solution.py:36
  464.3 3.3 collective-permute-done.21
  468.1 3.2 collective-permute-done.22
  471.3 1.9 collective-permute-start.23
  475.0 3.2 collective-permute-start.24
  482.9 3.3 collective-permute-done.28
  (361 shorter events, 72.8 us)
Async XLA Ops:
  119.0 11.9 %collective-permute-start.5 = (bf16[512,1024]{1,0:T(8,128)(2,1)}, bf16[512,1024]{1,0:T(8,128)(2,1)}, u32[]{:S(2)}, u32[]{:S(2)}) collective-permute-start(bf16[512,1024]{1,0:T(8,128)(2,1)} %convolution_convert_fusion.4), channel_id=1, source_target_pairs={{0,1},{1,0},{2,3},{3,2},{4,5},{5,4},{6,7},{7,6},{8,9},{9,8},{10,11... | collective-permute-start | bytes 3145736 | tf_op jit(solution)/shard_map/ppermute | solution.py:36
  121.1 18.3 %collective-permute-start = (bf16[512,1024]{1,0:T(8,128)(2,1)}, bf16[512,1024]{1,0:T(8,128)(2,1)S(1)}, u32[]{:S(2)}, u32[]{:S(2)}) collective-permute-start(bf16[512,1024]{1,0:T(8,128)(2,1)} %convolution_convert_fusion.5), channel_id=1, source_target_pairs={{0,1},{1,0},{2,3},{3,2},{4,5},{5,4},{6,7},{7,6},{8,9},{9,8},{10,11... | collective-permute-start | bytes 3145736 | tf_op jit(solution)/shard_map/ppermute | solution.py:36
  133.4 26.1 %collective-permute-start.6 = (bf16[512,1024]{1,0:T(8,128)(2,1)S(1)}, bf16[512,1024]{1,0:T(8,128)(2,1)S(1)}, u32[]{:S(2)}, u32[]{:S(2)}) collective-permute-start(bf16[512,1024]{1,0:T(8,128)(2,1)S(1)} %get-tuple-element.170), channel_id=1, source_target_pairs={{0,2},{1,3},{2,0},{3,1},{4,6},{5,7},{6,4},{7,5},{8,10},{9,11},{10,... | collective-permute-start | bytes 3145736 | tf_op jit(solution)/shard_map/ppermute | solution.py:36
  140.2 41.6 %collective-permute-start.1 = (bf16[512,1024]{1,0:T(8,128)(2,1)S(1)}, bf16[512,1024]{1,0:T(8,128)(2,1)S(1)}, u32[]{:S(2)}, u32[]{:S(2)}) collective-permute-start(bf16[512,1024]{1,0:T(8,128)(2,1)S(1)} %get-tuple-element.168), channel_id=1, source_target_pairs={{0,2},{1,3},{2,0},{3,1},{4,6},{5,7},{6,4},{7,5},{8,10},{9,11},{10,... | collective-permute-start | bytes 3145736 | tf_op jit(solution)/shard_map/ppermute | solution.py:36
  140.9 42.3 %copy-start.46 = (f32[256]{0:T(256)}, f32[256]{0:T(256)S(1)}, u32[]{:S(2)}) copy-start(f32[256]{0:T(256)S(1)} %get-tuple-element.55) | copy-start | bytes 3076
  140.9 42.3 %copy-start.48 = (f32[256]{0:T(256)}, f32[256]{0:T(256)S(1)}, u32[]{:S(2)}) copy-start(f32[256]{0:T(256)S(1)} %get-tuple-element.56) | copy-start | bytes 3076
  140.9 18.8 %copy-start.11 = (bf16[1,2,256,1024]{3,2,1,0:T(8,128)(2,1)S(1)}, bf16[1,2,256,1024]{3,2,1,0:T(8,128)(2,1)}, u32[]{:S(2)}) copy-start(bf16[1,2,256,1024]{3,2,1,0:T(8,128)(2,1)} %get-tuple-element.86) | copy-start | bytes 3145732
  161.7 159.0 %copy-start.45 = (f32[512]{0:T(512)}, f32[512]{0:T(512)S(1)}, u32[]{:S(2)}) copy-start(f32[512]{0:T(512)S(1)} %add_rsqrt_fusion) | copy-start | bytes 6148
  183.1 8.7 %copy-start.40 = (bf16[512,1024]{1,0:T(8,128)(2,1)}, bf16[512,1024]{1,0:T(8,128)(2,1)S(1)}, u32[]{:S(2)}) copy-start(bf16[512,1024]{1,0:T(8,128)(2,1)S(1)} %get-tuple-element.166) | copy-start | bytes 3145732
  183.1 17.8 %copy-start.41 = (bf16[512,1024]{1,0:T(8,128)(2,1)}, bf16[512,1024]{1,0:T(8,128)(2,1)S(1)}, u32[]{:S(2)}) copy-start(bf16[512,1024]{1,0:T(8,128)(2,1)S(1)} %get-tuple-element.167) | copy-start | bytes 3145732
  183.1 8.7 %collective-permute-start.2 = (bf16[512,1024]{1,0:T(8,128)(2,1)S(1)}, bf16[512,1024]{1,0:T(8,128)(2,1)S(1)}, u32[]{:S(2)}, u32[]{:S(2)}) collective-permute-start(bf16[512,1024]{1,0:T(8,128)(2,1)S(1)} %get-tuple-element.166), channel_id=1, source_target_pairs={{0,1},{1,0},{2,3},{3,2},{4,5},{5,4},{6,7},{7,6},{8,9},{9,8},{10,11... | collective-permute-start | bytes 3145736 | tf_op jit(solution)/shard_map/ppermute | solution.py:36
  191.8 9.1 %collective-permute-start.7 = (bf16[512,1024]{1,0:T(8,128)(2,1)S(1)}, bf16[512,1024]{1,0:T(8,128)(2,1)S(1)}, u32[]{:S(2)}, u32[]{:S(2)}) collective-permute-start(bf16[512,1024]{1,0:T(8,128)(2,1)S(1)} %get-tuple-element.167), channel_id=1, source_target_pairs={{0,1},{1,0},{2,3},{3,2},{4,5},{5,4},{6,7},{7,6},{8,9},{9,8},{10,11... | collective-permute-start | bytes 3145736 | tf_op jit(solution)/shard_map/ppermute | solution.py:36
  198.5 18.4 %copy-start.75 = (bf16[1024,768]{1,0:T(8,128)(2,1)}, bf16[1024,768]{1,0:T(8,128)(2,1)S(1)}, u32[]{:S(2)}) copy-start(bf16[1024,768]{1,0:T(8,128)(2,1)S(1)} %get-tuple-element.76) | copy-start | bytes 4718596
  198.5 27.9 %copy-start.77 = (bf16[1024,768]{1,0:T(8,128)(2,1)}, bf16[1024,768]{1,0:T(8,128)(2,1)S(1)}, u32[]{:S(2)}) copy-start(bf16[1024,768]{1,0:T(8,128)(2,1)S(1)} %get-tuple-element.71) | copy-start | bytes 4718596
  198.5 27.9 %copy-start.79 = (bf16[1024,768]{1,0:T(8,128)(2,1)}, bf16[1024,768]{1,0:T(8,128)(2,1)S(1)}, u32[]{:S(2)}) copy-start(bf16[1024,768]{1,0:T(8,128)(2,1)S(1)} %get-tuple-element.72) | copy-start | bytes 4718596
  204.3 12.6 %copy-start.5 = (bf16[2,4,256,1024]{3,2,1,0:T(8,128)(2,1)S(1)}, bf16[2,4,256,1024]{3,2,1,0:T(8,128)(2,1)}, u32[]{:S(2)}) copy-start(bf16[2,4,256,1024]{3,2,1,0:T(8,128)(2,1)} %get-tuple-element.37) | copy-start | bytes 12582916
  221.4 24.3 %collective-permute-start.40 = (bf16[2,2,96,1024]{3,2,1,0:T(8,128)(2,1)}, bf16[2,2,96,1024]{3,2,1,0:T(8,128)(2,1)S(1)}, u32[]{:S(2)}, u32[]{:S(2)}) collective-permute-start(bf16[2,2,96,1024]{3,2,1,0:T(8,128)(2,1)} %dynamic-slice_bitcast_fusion.2), channel_id=1, source_target_pairs={{0,4},{1,5},{2,6},{3,7},{4,0},{5,1},{6,2},{7,3},{8,12},{9,13},{10,... | collective-permute-start | bytes 2359304 | tf_op jit(solution)/shard_map/ppermute | solution.py:36
  226.2 20.3 %collective-permute-start.15 = (bf16[512,1024]{1,0:T(8,128)(2,1)}, bf16[512,1024]{1,0:T(8,128)(2,1)}, u32[]{:S(2)}, u32[]{:S(2)}) collective-permute-start(bf16[512,1024]{1,0:T(8,128)(2,1)} %fusion.96), channel_id=1, source_target_pairs={{0,1},{1,0},{2,3},{3,2},{4,5},{5,4},{6,7},{7,6},{8,9},{9,8},{10,11... | collective-permute-start | bytes 3145736 | tf_op jit(solution)/shard_map/ppermute | solution.py:36
  229.2 21.8 %collective-permute-start.10 = (bf16[512,1024]{1,0:T(8,128)(2,1)}, bf16[512,1024]{1,0:T(8,128)(2,1)}, u32[]{:S(2)}, u32[]{:S(2)}) collective-permute-start(bf16[512,1024]{1,0:T(8,128)(2,1)} %fusion.95), channel_id=1, source_target_pairs={{0,1},{1,0},{2,3},{3,2},{4,5},{5,4},{6,7},{7,6},{8,9},{9,8},{10,11... | collective-permute-start | bytes 3145736 | tf_op jit(solution)/shard_map/ppermute | solution.py:36
  244.5 36.6 %collective-permute-start.35 = (bf16[2,2,128,1536]{3,2,1,0:T(8,128)(2,1)S(1)}, bf16[2,2,128,1536]{3,2,1,0:T(8,128)(2,1)S(1)}, u32[]{:S(2)}, u32[]{:S(2)}) collective-permute-start(bf16[2,2,128,1536]{3,2,1,0:T(8,128)(2,1)S(1)} %dynamic-slice_bitcast_fusion), channel_id=1, source_target_pairs={{0,4},{1,5},{2,6},{3,7},{4,0},{5,1},{6,2},{7,3},{8,12},{9,13},{10,... | collective-permute-start | bytes 4718600 | tf_op jit(solution)/shard_map/ppermute | solution.py:36
  245.6 11.3 %collective-permute-start.3 = (bf16[512,1024]{1,0:T(8,128)(2,1)S(1)}, bf16[512,1024]{1,0:T(8,128)(2,1)S(1)}, u32[]{:S(2)}, u32[]{:S(2)}) collective-permute-start(bf16[512,1024]{1,0:T(8,128)(2,1)S(1)} %copy-done.70), channel_id=1, source_target_pairs={{0,1},{1,0},{2,3},{3,2},{4,5},{5,4},{6,7},{7,6},{8,9},{9,8},{10,11... | collective-permute-start | bytes 3145736 | tf_op jit(solution)/shard_map/ppermute | solution.py:36
  245.8 22.2 %collective-permute-start.8 = (bf16[512,1024]{1,0:T(8,128)(2,1)S(1)}, bf16[512,1024]{1,0:T(8,128)(2,1)S(1)}, u32[]{:S(2)}, u32[]{:S(2)}) collective-permute-start(bf16[512,1024]{1,0:T(8,128)(2,1)S(1)} %convolution_convert_fusion), channel_id=1, source_target_pairs={{0,1},{1,0},{2,3},{3,2},{4,5},{5,4},{6,7},{7,6},{8,9},{9,8},{10,11... | collective-permute-start | bytes 3145736 | tf_op jit(solution)/shard_map/ppermute | solution.py:36
  246.5 20.6 %collective-permute-start.41 = (bf16[2,96,1024]{2,1,0:T(8,128)(2,1)S(1)}, bf16[2,96,1024]{2,1,0:T(8,128)(2,1)S(1)}, u32[]{:S(2)}, u32[]{:S(2)}) collective-permute-start(bf16[2,96,1024]{2,1,0:T(8,128)(2,1)S(1)} %dynamic-slice_bitcast_fusion.5), channel_id=1, source_target_pairs={{0,16},{1,17},{2,18},{3,19},{4,20},{5,21},{6,22},{7,23},{8,24},{9,... | collective-permute-start | bytes 1179656 | tf_op jit(solution)/shard_map/ppermute | solution.py:36
  251.0 32.8 %collective-permute-start.16 = (bf16[512,1024]{1,0:T(8,128)(2,1)S(1)}, bf16[512,1024]{1,0:T(8,128)(2,1)S(1)}, u32[]{:S(2)}, u32[]{:S(2)}) collective-permute-start(bf16[512,1024]{1,0:T(8,128)(2,1)S(1)} %get-tuple-element.174), channel_id=1, source_target_pairs={{0,2},{1,3},{2,0},{3,1},{4,6},{5,7},{6,4},{7,5},{8,10},{9,11},{10,... | collective-permute-start | bytes 3145736 | tf_op jit(solution)/shard_map/ppermute | solution.py:36
  256.8 42.8 %collective-permute-start.11 = (bf16[512,1024]{1,0:T(8,128)(2,1)S(1)}, bf16[512,1024]{1,0:T(8,128)(2,1)S(1)}, u32[]{:S(2)}, u32[]{:S(2)}) collective-permute-start(bf16[512,1024]{1,0:T(8,128)(2,1)S(1)} %get-tuple-element.172), channel_id=1, source_target_pairs={{0,2},{1,3},{2,0},{3,1},{4,6},{5,7},{6,4},{7,5},{8,10},{9,11},{10,... | collective-permute-start | bytes 3145736 | tf_op jit(solution)/shard_map/ppermute | solution.py:36
  258.7 10.4 %copy-start.27 = (f32[512,1024]{1,0:T(8,128)}, f32[512,1024]{1,0:T(8,128)S(1)}, u32[]{:S(2)}) copy-start(f32[512,1024]{1,0:T(8,128)S(1)} %convert_add_fusion.10) | copy-start | bytes 6291460
  258.7 9.3 %copy-start.74 = (bf16[1024,768]{1,0:T(8,128)(2,1)S(1)}, bf16[1024,768]{1,0:T(8,128)(2,1)}, u32[]{:S(2)}) copy-start(bf16[1024,768]{1,0:T(8,128)(2,1)} %copy-done.73) | copy-start | bytes 4718596
  267.1 57.0 %collective-permute-start.4 = (bf16[256,1024]{1,0:T(8,128)(2,1)}, bf16[256,1024]{1,0:T(8,128)(2,1)}, u32[]{:S(2)}, u32[]{:S(2)}) collective-permute-start(bf16[256,1024]{1,0:T(8,128)(2,1)} %slice.729), channel_id=1, source_target_pairs={{0,2},{1,3},{2,0},{3,1},{4,6},{5,7},{6,4},{7,5},{8,10},{9,11},{10,... | collective-permute-start | bytes 1572872 | tf_op jit(solution)/shard_map/ppermute | solution.py:36
  267.9 6.6 %collective-permute-start.42 = (bf16[96,1024]{1,0:T(8,128)(2,1)S(1)}, bf16[96,1024]{1,0:T(8,128)(2,1)S(1)}, u32[]{:S(2)}, u32[]{:S(2)}) collective-permute-start(bf16[96,1024]{1,0:T(8,128)(2,1)S(1)} %dynamic-slice_bitcast_fusion.8), channel_id=1, source_target_pairs={{0,8},{1,9},{2,10},{3,11},{4,12},{5,13},{6,14},{7,15},{8,0},{9,1},... | collective-permute-start | bytes 589832 | tf_op jit(solution)/shard_map/ppermute | solution.py:36
  268.0 13.0 %copy-start.16 = (bf16[1024,1536]{1,0:T(8,128)(2,1)S(1)}, bf16[1024,1536]{1,0:T(8,128)(2,1)}, u32[]{:S(2)}) copy-start(bf16[1024,1536]{1,0:T(8,128)(2,1)} %copy-done.15) | copy-start | bytes 9437188
  274.6 57.6 %collective-permute-start.9 = (bf16[256,1024]{1,0:T(8,128)(2,1)}, bf16[256,1024]{1,0:T(8,128)(2,1)}, u32[]{:S(2)}, u32[]{:S(2)}) collective-permute-start(bf16[256,1024]{1,0:T(8,128)(2,1)} %slice.728), channel_id=1, source_target_pairs={{0,2},{1,3},{2,0},{3,1},{4,6},{5,7},{6,4},{7,5},{8,10},{9,11},{10,... | collective-permute-start | bytes 1572872 | tf_op jit(solution)/shard_map/ppermute | solution.py:36
  282.4 36.9 %collective-permute-start.36 = (bf16[2,128,1536]{2,1,0:T(8,128)(2,1)}, bf16[2,128,1536]{2,1,0:T(8,128)(2,1)}, u32[]{:S(2)}, u32[]{:S(2)}) collective-permute-start(bf16[2,128,1536]{2,1,0:T(8,128)(2,1)} %dynamic-slice_bitcast_fusion.3), channel_id=1, source_target_pairs={{0,16},{1,17},{2,18},{3,19},{4,20},{5,21},{6,22},{7,23},{8,24},{9,... | collective-permute-start | bytes 2359304 | tf_op jit(solution)/shard_map/ppermute | solution.py:36
  302.5 18.2 %copy-start.10 = (bf16[1,2,256,1024]{3,2,1,0:T(8,128)(2,1)S(1)}, bf16[1,2,256,1024]{3,2,1,0:T(8,128)(2,1)}, u32[]{:S(2)}) copy-start(bf16[1,2,256,1024]{3,2,1,0:T(8,128)(2,1)} %get-tuple-element.82) | copy-start | bytes 3145732
  320.6 11.1 %collective-permute-start.37 = (bf16[128,1536]{1,0:T(8,128)(2,1)S(1)}, bf16[128,1536]{1,0:T(8,128)(2,1)S(1)}, u32[]{:S(2)}, u32[]{:S(2)}) collective-permute-start(bf16[128,1536]{1,0:T(8,128)(2,1)S(1)} %dynamic-slice_bitcast_fusion.6), channel_id=1, source_target_pairs={{0,8},{1,9},{2,10},{3,11},{4,12},{5,13},{6,14},{7,15},{8,0},{9,1},... | collective-permute-start | bytes 1179656 | tf_op jit(solution)/shard_map/ppermute | solution.py:36
  323.5 15.1 %copy-start.31 = (bf16[512,1024]{1,0:T(8,128)(2,1)}, bf16[512,1024]{1,0:T(8,128)(2,1)S(1)}, u32[]{:S(2)}) copy-start(bf16[512,1024]{1,0:T(8,128)(2,1)S(1)} %get-tuple-element.61) | copy-start | bytes 3145732
  323.5 15.1 %collective-permute-start.12 = (bf16[512,1024]{1,0:T(8,128)(2,1)S(1)}, bf16[512,1024]{1,0:T(8,128)(2,1)S(1)}, u32[]{:S(2)}, u32[]{:S(2)}) collective-permute-start(bf16[512,1024]{1,0:T(8,128)(2,1)S(1)} %get-tuple-element.61), channel_id=1, source_target_pairs={{0,1},{1,0},{2,3},{3,2},{4,5},{5,4},{6,7},{7,6},{8,9},{9,8},{10,11... | collective-permute-start | bytes 3145736 | tf_op jit(solution)/shard_map/ppermute | solution.py:36
  323.6 8.5 %copy-start.30 = (f32[512,1024]{1,0:T(8,128)S(1)}, f32[512,1024]{1,0:T(8,128)}, u32[]{:S(2)}) copy-start(f32[512,1024]{1,0:T(8,128)} %copy-done.29) | copy-start | bytes 6291460
  323.6 8.5 %slice-start.2 = ((f32[512]{0:T(512)}), f32[256]{0:T(256)S(1)}, s32[]{:S(2)}) async-start(f32[512]{0:T(512)} %copy-done.45), calls=%async_computation.2 | async-start | bytes 2048 | tf_op jit(solution)/shard_map/slice | solution.py:927
  323.6 15.0 %collective-permute-start.17 = (bf16[512,1024]{1,0:T(8,128)(2,1)S(1)}, bf16[512,1024]{1,0:T(8,128)(2,1)S(1)}, u32[]{:S(2)}, u32[]{:S(2)}) collective-permute-start(bf16[512,1024]{1,0:T(8,128)(2,1)S(1)} %get-tuple-element.164), channel_id=1, source_target_pairs={{0,1},{1,0},{2,3},{3,2},{4,5},{5,4},{6,7},{7,6},{8,9},{9,8},{10,11... | collective-permute-start | bytes 3145736 | tf_op jit(solution)/shard_map/ppermute | solution.py:36
  331.8 6.0 %collective-permute-start.38 = (bf16[1,2,32,1536]{3,2,1,0:T(8,128)(2,1)S(1)}, bf16[1,2,32,1536]{3,2,1,0:T(8,128)(2,1)S(1)}, u32[]{:S(2)}, u32[]{:S(2)}) collective-permute-start(bf16[1,2,32,1536]{3,2,1,0:T(8,128)(2,1)S(1)} %dynamic-slice_bitcast_fusion.9), channel_id=1, source_target_pairs={{0,2},{1,3},{2,0},{3,1},{4,6},{5,7},{6,4},{7,5},{8,10},{9,11},{10,... | collective-permute-start | bytes 589832 | tf_op jit(solution)/shard_map/ppermute | solution.py:36
  338.6 60.8 %collective-permute-start.39 = (bf16[2,1,32,1536]{3,2,0,1:T(8,128)(2,1)}, bf16[2,1,32,1536]{3,2,0,1:T(8,128)(2,1)}, u32[]{:S(2)}, u32[]{:S(2)}) collective-permute-start(bf16[2,1,32,1536]{3,2,0,1:T(8,128)(2,1)} %fusion.144), channel_id=1, source_target_pairs={{0,1},{1,0},{2,3},{3,2},{4,5},{5,4},{6,7},{7,6},{8,9},{9,8},{10,11... | collective-permute-start | bytes 589832 | tf_op jit(solution)/shard_map/ppermute | solution.py:36
  342.0 58.5 %collective-permute-start.30 = (bf16[256,1024]{1,0:T(8,128)(2,1)}, bf16[256,1024]{1,0:T(8,128)(2,1)}, u32[]{:S(2)}, u32[]{:S(2)}) collective-permute-start(bf16[256,1024]{1,0:T(8,128)(2,1)} %constant_dynamic-slice_fusion.2), channel_id=1, source_target_pairs={{0,16},{1,17},{2,18},{3,19},{4,20},{5,21},{6,22},{7,23},{8,24},{9,... | collective-permute-start | bytes 1572872 | tf_op jit(solution)/shard_map/ppermute | solution.py:36
  366.6 51.7 %collective-permute-start.18 = (bf16[512,1024]{1,0:T(8,128)(2,1)}, bf16[512,1024]{1,0:T(8,128)(2,1)}, u32[]{:S(2)}, u32[]{:S(2)}) collective-permute-start(bf16[512,1024]{1,0:T(8,128)(2,1)} %convolution_convert_fusion.2), channel_id=1, source_target_pairs={{0,1},{1,0},{2,3},{3,2},{4,5},{5,4},{6,7},{7,6},{8,9},{9,8},{10,11... | collective-permute-start | bytes 3145736 | tf_op jit(solution)/shard_map/ppermute | solution.py:36
  392.0 31.6 %collective-permute-start.13 = (bf16[512,1024]{1,0:T(8,128)(2,1)}, bf16[512,1024]{1,0:T(8,128)(2,1)}, u32[]{:S(2)}, u32[]{:S(2)}) collective-permute-start(bf16[512,1024]{1,0:T(8,128)(2,1)} %convolution_convert_fusion.3), channel_id=1, source_target_pairs={{0,1},{1,0},{2,3},{3,2},{4,5},{5,4},{6,7},{7,6},{8,9},{9,8},{10,11... | collective-permute-start | bytes 3145736 | tf_op jit(solution)/shard_map/ppermute | solution.py:36
  401.9 13.5 %collective-permute-start.31 = (bf16[256,1024]{1,0:T(8,128)(2,1)S(1)}, bf16[256,1024]{1,0:T(8,128)(2,1)}, u32[]{:S(2)}, u32[]{:S(2)}) collective-permute-start(bf16[256,1024]{1,0:T(8,128)(2,1)S(1)} %add_convert_fusion.2), channel_id=1, source_target_pairs={{1,9},{3,11},{5,13},{7,15},{8,0},{10,2},{12,4},{14,6},{17,25},{19,... | collective-permute-start | bytes 1572872 | tf_op jit(solution)/shard_map/ppermute | solution.py:36
  415.0 25.4 %collective-permute-start.25 = (bf16[2,2,128,1024]{3,2,1,0:T(8,128)(2,1)S(1)}, bf16[2,2,128,1024]{3,2,1,0:T(8,128)(2,1)S(1)}, u32[]{:S(2)}, u32[]{:S(2)}) collective-permute-start(bf16[2,2,128,1024]{3,2,1,0:T(8,128)(2,1)S(1)} %dynamic-slice_bitcast_fusion.1), channel_id=1, source_target_pairs={{0,4},{1,5},{2,6},{3,7},{4,0},{5,1},{6,2},{7,3},{8,12},{9,13},{10,... | collective-permute-start | bytes 3145736 | tf_op jit(solution)/shard_map/ppermute | solution.py:36
  416.7 30.0 %collective-permute-start.32 = (bf16[256,1024]{1,0:T(8,128)(2,1)S(1)}, bf16[256,1024]{1,0:T(8,128)(2,1)S(1)}, u32[]{:S(2)}, u32[]{:S(2)}) collective-permute-start(bf16[256,1024]{1,0:T(8,128)(2,1)S(1)} %add_convert_fusion.1), channel_id=1, source_target_pairs={{2,6},{4,0},{11,15},{13,9},{18,22},{20,16},{27,31},{29,25}} | collective-permute-start | bytes 1572872 | tf_op jit(solution)/shard_map/ppermute | solution.py:36
  421.0 27.4 %collective-permute-start.19 = (bf16[256,1024]{1,0:T(8,128)(2,1)S(1)}, bf16[256,1024]{1,0:T(8,128)(2,1)S(1)}, u32[]{:S(2)}, u32[]{:S(2)}) collective-permute-start(bf16[256,1024]{1,0:T(8,128)(2,1)S(1)} %slice.726), channel_id=1, source_target_pairs={{0,2},{1,3},{2,0},{3,1},{4,6},{5,7},{6,4},{7,5},{8,10},{9,11},{10,... | collective-permute-start | bytes 1572872 | tf_op jit(solution)/shard_map/ppermute | solution.py:36
  423.6 16.8 %copy-start.17 = (bf16[1024,1024]{1,0:T(8,128)(2,1)S(1)}, bf16[1024,1024]{1,0:T(8,128)(2,1)}, u32[]{:S(2)}) copy-start(bf16[1024,1024]{1,0:T(8,128)(2,1)} %fusion.66) | copy-start | bytes 6291460
  426.3 22.0 %collective-permute-start.14 = (bf16[256,1024]{1,0:T(8,128)(2,1)S(1)}, bf16[256,1024]{1,0:T(8,128)(2,1)S(1)}, u32[]{:S(2)}, u32[]{:S(2)}) collective-permute-start(bf16[256,1024]{1,0:T(8,128)(2,1)S(1)} %slice.727), channel_id=1, source_target_pairs={{0,2},{1,3},{2,0},{3,1},{4,6},{5,7},{6,4},{7,5},{8,10},{9,11},{10,... | collective-permute-start | bytes 1572872 | tf_op jit(solution)/shard_map/ppermute | solution.py:36
  440.9 22.6 %collective-permute-start.26 = (bf16[2,128,1024]{2,1,0:T(8,128)(2,1)S(1)}, bf16[2,128,1024]{2,1,0:T(8,128)(2,1)S(1)}, u32[]{:S(2)}, u32[]{:S(2)}) collective-permute-start(bf16[2,128,1024]{2,1,0:T(8,128)(2,1)S(1)} %dynamic-slice_bitcast_fusion.4), channel_id=1, source_target_pairs={{0,16},{1,17},{2,18},{3,19},{4,20},{5,21},{6,22},{7,23},{8,24},{9,... | collective-permute-start | bytes 1572872 | tf_op jit(solution)/shard_map/ppermute | solution.py:36
  447.0 34.5 %collective-permute-start.33 = (bf16[128,1024]{1,0:T(8,128)(2,1)S(1)}, bf16[128,1024]{1,0:T(8,128)(2,1)S(1)}, u32[]{:S(2)}, u32[]{:S(2)}) collective-permute-start(bf16[128,1024]{1,0:T(8,128)(2,1)S(1)} %constant_dynamic-slice_fusion.1), channel_id=1, source_target_pairs={{0,2},{6,4},{9,11},{15,13},{16,18},{22,20},{25,27},{31,29}} | collective-permute-start | bytes 786440 | tf_op jit(solution)/shard_map/ppermute | solution.py:36
  449.2 15.0 %copy-start.49 = (f32[256]{0:T(256)S(1)}, f32[256]{0:T(256)}, u32[]{:S(2)}) copy-start(f32[256]{0:T(256)} %copy-done.48) | copy-start | bytes 3076
  449.2 18.8 %copy-start.47 = (f32[256]{0:T(256)S(1)}, f32[256]{0:T(256)}, u32[]{:S(2)}) copy-start(f32[256]{0:T(256)} %copy-done.46) | copy-start | bytes 3076
  449.3 24.0 %copy-start.7 = (f32[512,1024]{1,0:T(8,128)S(1)}, f32[512,1024]{1,0:T(8,128)}, u32[]{:S(2)}) copy-start(f32[512,1024]{1,0:T(8,128)} %get-tuple-element.165) | copy-start | bytes 6291460
  449.3 14.5 %collective-permute-start.20 = (f32[2304]{0:T(1024)S(1)}, f32[2304]{0:T(1024)S(1)}, u32[]{:S(2)}, u32[]{:S(2)}) collective-permute-start(f32[2304]{0:T(1024)S(1)} %maximum_add_fusion.4), channel_id=1, source_target_pairs={{0,1},{1,0},{2,3},{3,2},{4,5},{5,4},{6,7},{7,6},{8,9},{9,8},{10,11... | collective-permute-start | bytes 27656 | tf_op jit(solution)/shard_map/ppermute | solution.py:36
  463.7 17.3 %collective-permute-start.27 = (bf16[128,1024]{1,0:T(8,128)(2,1)S(1)}, bf16[128,1024]{1,0:T(8,128)(2,1)S(1)}, u32[]{:S(2)}, u32[]{:S(2)}) collective-permute-start(bf16[128,1024]{1,0:T(8,128)(2,1)S(1)} %dynamic-slice_bitcast_fusion.7), channel_id=1, source_target_pairs={{0,8},{1,9},{2,10},{3,11},{4,12},{5,13},{6,14},{7,15},{8,0},{9,1},... | collective-permute-start | bytes 786440 | tf_op jit(solution)/shard_map/ppermute | solution.py:36
  463.8 3.8 collective-permute-start.21
  467.6 3.7 collective-permute-start.22
  471.3 3.7 collective-permute-start.23
  475.0 4.9 %collective-permute-start.24 = (f32[2304]{0:T(1024)S(1)}, f32[2304]{0:T(1024)S(1)}, u32[]{:S(2)}, u32[]{:S(2)}) collective-permute-start(f32[2304]{0:T(1024)S(1)} %add.315), channel_id=1, source_target_pairs={{0,16},{1,17},{2,18},{3,19},{4,20},{5,21},{6,22},{7,23},{8,24},{9,... | collective-permute-start | bytes 27656 | tf_op jit(solution)/shard_map/ppermute | solution.py:36
  481.1 5.0 %collective-permute-start.28 = (bf16[1,2,32,1024]{3,2,1,0:T(8,128)(2,1)S(1)}, bf16[1,2,32,1024]{3,2,1,0:T(8,128)(2,1)S(1)}, u32[]{:S(2)}, u32[]{:S(2)}) collective-permute-start(bf16[1,2,32,1024]{3,2,1,0:T(8,128)(2,1)S(1)} %dynamic-slice_bitcast_fusion.10), channel_id=1, source_target_pairs={{0,2},{1,3},{2,0},{3,1},{4,6},{5,7},{6,4},{7,5},{8,10},{9,11},{10,... | collective-permute-start | bytes 393224 | tf_op jit(solution)/shard_map/ppermute | solution.py:36
  481.6 4.7 collective-permute-start.34
  486.2 1.4 collective-permute-start.29
  (67 other events, 244.3 us)

commit v4 on v3

--- a/solution.py
+++ b/solution.py
@@ -807,6 +807,625 @@
     )(a, c, w_out, w_down, x, g, gains, query_gain, key_gain, cosine, sine)
 
 
+def mlp_kernel(
+    mixed_ref, wo_ref, wc_ref, wd_ref, x_ref, g_ref, gain_ref,
+    out_ref, residual_ref, normed_ref, hidden_ref, both_ref, branch_ref, gain_grad_ref,
+    res_v, core_s, oc_v, x_s, og_v, n2_v, hidden_v, both_v, dc_v, dg_v, da_v, us_v, uc_v, ux_v, ug_v, ua_v,
+    send, recv, local, tokens_sem,
+):
+    links = Links(send, recv)
+    sequences, blocks, piece, width = g_ref.shape
+    half = blocks // 2
+    units = wd_ref.shape[0]
+    core, far = dict(seq=links.seq_at(1)), dict(seq=links.seq_at(2))
+    pairs = [(n, k) for n in range(sequences) for k in range(half)]
+    slots = {
+        name: links.slots(half * sequences)
+        for name in ("o_core", "o_far", "normed", "grad_core", "up_core", "grad_far", "branch", "up_far")
+    }
+    ends = {
+        "o_core": lambda n, k: (core_s.at[n, k], oc_v.at[n, k], core),
+        "o_far": lambda n, k: (x_s.at[n, k], og_v.at[n, half - 1 - k], far),
+        "normed": lambda n, k: (n2_v.at[n, k], n2_v.at[n, half + k], core),
+        "grad_core": lambda n, k: (core_s.at[n, k], dc_v.at[n, k], core),
+        "up_core": lambda n, k: (us_v.at[n, k], uc_v.at[n, k], core),
+        "grad_far": lambda n, k: (x_s.at[n, k], dg_v.at[n, half - 1 - k], far),
+        "branch": lambda n, k: (us_v.at[n, k], branch_ref.at[n, half + k], core),
+        "up_far": lambda n, k: (ux_v.at[n], ug_v.at[n], far),
+    }
+
+    def copy(name, n, k):
+        src, dst, to = ends[name](n, k)
+        return links.copy(src, dst, slots[name] + half * n + k, **to)
+
+    def arrived(name, n, k):
+        copy(name, n, half - 1 - k if name in ("o_far", "grad_far") else k).wait_recv()
+
+    near_copies = []
+
+    def near(src, dst):
+        made = pltpu.make_async_copy(src, dst, local.at[len(near_copies)])
+        made.start()
+        near_copies.append(made)
+
+    links.greet((), (1, 2))
+    tokens = [
+        pltpu.make_async_copy(x_ref.at[n, pl.ds(0, half)], uc_v.at[n], tokens_sem.at[n])
+        for n in range(sequences)
+    ]
+    for made in tokens:
+        made.start()
+    gain = gain_ref[...]
+
+    for n in range(sequences):
+
+        def out_part(i, carry):
+            b = lax.rem(i + half, blocks)
+            y = dot(mixed_ref[n, b], wo_ref[...])
+
+            @pl.when(i < half)
+            def _():
+                core_s[n, i] = y.astype(BF16)
+                copy("o_core", n, i).start()
+
+            @pl.when(i >= half)
+            def _():
+                res_v[n, i - half] = y
+
+            return carry
+
+        lax.fori_loop(0, blocks, out_part, 0)
+        for k in range(half):
+            arrived("o_core", n, k)
+            total = res_v[n, k] + oc_v[n, k].astype(F32)
+            res_v[n, k] = total
+            x_s[n, k] = total.astype(BF16)
+            copy("o_far", n, k).start()
+
+    def norm(n):
+        tokens[n].wait()
+        for k in range(half):
+            arrived("o_far", n, k)
+            residual = res_v[n, k] + og_v[n, k].astype(F32) + uc_v[n, k].astype(F32)
+            res_v[n, k] = residual
+            n2_v[n, k] = (residual * rms_scale(residual) * gain).astype(BF16)
+            copy("normed", n, k).start()
+
+    def feed(n):
+        for k in range(half):
+            copy("o_core", n, k).wait_send()
+            copy("o_far", n, k).wait_send()
+            arrived("normed", n, k)
+
+        def step(i, carry):
+            b = lax.rem(i + half, blocks)
+            both = dot(n2_v[n, b], wc_ref[...])
+            gate, upward = both[:, :units], both[:, units:]
+            grad_hidden = dot_t(g_ref[n, b], wd_ref[...])
+            sigmoid = 1.0 / (1.0 + jnp.exp(-gate))
+            silu = gate * sigmoid
+            hidden_v[n, b] = (silu * upward).astype(BF16)
+            both_v[n, b, :, units:] = (grad_hidden * silu).astype(BF16)
+            both_v[n, b, :, :units] = (
+                grad_hidden * upward * sigmoid * (1.0 + gate * (1.0 - sigmoid))
+            ).astype(BF16)
+            grad = dot_t(both_v[n, b], wc_ref[...])
+
+            @pl.when(i < half)
+            def _():
+                core_s[n, i] = grad.astype(BF16)
+                copy("grad_core", n, i).start()
+
+            @pl.when(i >= half)
+            def _():
+                k = i - half
+                arrived_core = copy("grad_core", n, k)
+                arrived_core.wait_recv()
+                total = grad + dc_v[n, k].astype(F32)
+                da_v[n, k] = total
+                x_s[n, k] = total.astype(BF16)
+                copy("grad_far", n, k).start()
+
+            up = dot(hidden_v[n, b], wd_ref[...])
+
+            @pl.when(i < half)
+            def _():
+                us_v[n, i] = up.astype(BF16)
+                copy("up_core", n, i).start()
+
+            @pl.when(i >= half)
+            def _():
+                copy("up_core", n, i - half).wait_recv()
+
+            @pl.when(i == half)
+            def _():
+                ua_v[n] = res_v[n, 0] + (up + uc_v[n, 0].astype(F32))
+
+            @pl.when(i == half + 1)
+            def _():
+                ux_v[n] = (up + uc_v[n, 1].astype(F32)).astype(BF16)
+                copy("up_far", n, 0).start()
+
+            return carry
+
+        lax.fori_loop(0, blocks, step, 0)
+        near(n2_v.at[n], normed_ref.at[n])
+        near(hidden_v.at[n], hidden_ref.at[n])
+        near(both_v.at[n], both_ref.at[n])
+
+    def back(n):
+        for k in range(half):
+            copy("up_core", n, k).wait_send()
+        for k in range(half):
+            arrived("grad_far", n, k)
+            grad = da_v[n, k] + dg_v[n, k].astype(F32)
+            residual = res_v[n, k]
+            scale = rms_scale(residual)
+            scaled = grad * gain
+            grad_residual = (
+                g_ref[n, k].astype(F32)
+                + scale * scaled
+                - residual * (scale * scale * scale * jnp.mean(scaled * residual, axis=-1, keepdims=True))
+            )
+            us_v[n, k] = grad_residual.astype(BF16)
+            copy("branch", n, k).start()
+            near(us_v.at[n, k], branch_ref.at[n, k])
+            if k == 0:
+                part = jnp.sum(grad * residual * scale, axis=0, keepdims=True)
+                gain_grad_ref[...] = part if n == 0 else gain_grad_ref[...] + part
+                da_v[n, 0] = grad_residual
+                near(da_v.at[n, 0], residual_ref.at[n])
+        copy("up_far", n, 0).wait_recv()
+        oc_v[n, 0] = (ua_v[n] + ug_v[n].astype(F32)).astype(BF16)
+        near(oc_v.at[n, 0], out_ref.at[n])
+
+    for n in range(sequences):
+        norm(n)
+        feed(n)
+    for n in range(sequences):
+        back(n)
+    for n, k in pairs:
+        arrived("branch", n, k)
+    for n, k in pairs:
+        for name in ("normed", "grad_core", "grad_far", "branch"):
+            copy(name, n, k).wait_send()
+    for n in range(sequences):
+        copy("up_far", n, 0).wait_send()
+    for made in near_copies:
+        made.wait()
+
+
+def feed_forward(mixed, w_o, w_mlp, w_d, x_rel, g_rel, gain):
+    sequences, blocks, piece, width = g_rel.shape
+    half = blocks // 2
+    units = w_d.shape[0]
+    hbm = pl.BlockSpec(memory_space=pl.ANY)
+    vmem = pl.BlockSpec(memory_space=pltpu.VMEM)
+    shape = jax.ShapeDtypeStruct
+    part = lambda dtype: pltpu.VMEM((sequences, half, piece, width), dtype)
+    one = lambda dtype: pltpu.VMEM((sequences, piece, width), dtype)
+    return pl.pallas_call(
+        mlp_kernel,
+        name="feed_forward",
+        out_shape=(
+            shape((sequences, piece, width), BF16),
+            shape((sequences, piece, width), F32),
+            shape((sequences, blocks, piece, width), BF16),
+            shape((sequences, blocks, piece, units), BF16),
+            shape((sequences, blocks, piece, 2 * units), BF16),
+            shape((sequences, blocks, piece, width), BF16),
+            shape((1, width), F32),
+        ),
+        in_specs=[vmem] * 4 + [hbm, vmem, vmem],
+        out_specs=[hbm] * 6 + [vmem],
+        scratch_shapes=[
+            part(F32),
+            part(BF16),
+            part(BF16),
+            part(BF16),
+            part(BF16),
+            pltpu.VMEM((sequences, blocks, piece, width), BF16),
+            pltpu.VMEM((sequences, blocks, piece, units), BF16),
+            pltpu.VMEM((sequences, blocks, piece, 2 * units), BF16),
+            part(BF16),
+            part(BF16),
+            part(F32),
+            part(BF16),
+            part(BF16),
+            one(BF16),
+            one(BF16),
+            one(F32),
+            pltpu.SemaphoreType.DMA((16 * sequences,)),
+            pltpu.SemaphoreType.DMA((16 * sequences,)),
+            pltpu.SemaphoreType.DMA((16,)),
+            pltpu.SemaphoreType.DMA((sequences,)),
+        ],
+        compiler_params=pltpu.CompilerParams(
+            collective_id=1, has_side_effects=True, vmem_limit_bytes=67043328
+        ),
+    )(mixed, w_o, w_mlp, w_d, x_rel, g_rel, gain)
+
+
+class Scatter:
+    def __init__(self, links, src, first, second, third, done=None):
+        d = links.d
+        self.z1, self.z0, self.y = bit_of(d, 2), bit_of(d, 1), bit_of(d, 0)
+        self.src, self.first, self.second, self.third = src, first, second, third
+        base = links.slots(7)
+        self.over_y = links.plan(src.at[:, :, 1 - self.y], first, base, dp=flip(d, 0))
+        self.over_z0 = links.plan(first.at[:, 1 - self.z0], second, base + 1, dp=flip(d, 1))
+        self.over_z1 = links.plan(second.at[1 - self.z1], third, base + 2, dp=flip(d, 2))
+        self.done, self.s = done, links.s
+        if done is not None:
+            self.share = [
+                links.plan(third.at[links.seq_at(k)], done.at[links.s], base + 3 + k, seq=links.seq_at(k))
+                for k in (2, 3, 1)
+            ]
+
+    def start(self):
+        self.over_y.start()
+
+    def sum_y(self):
+        self.over_y.wait_recv()
+
+        def step(i, carry):
+            a, b = lax.div(i, 2), lax.rem(i, 2)
+            mine = self.src[a, b, self.y].astype(F32)
+            self.first[a, b] = (mine + self.first[a, b].astype(F32)).astype(BF16)
+            return carry
+
+        lax.fori_loop(0, 4, step, 0)
+        self.over_z0.start()
+
+    def sum_z0(self):
+        self.over_z0.wait_recv()
+
+        def step(a, carry):
+            mine = self.first[a, self.z0].astype(F32)
+            self.second[a] = (mine + self.second[a].astype(F32)).astype(BF16)
+            return carry
+
+        lax.fori_loop(0, 2, step, 0)
+        self.over_z1.start()
+
+    def sum_z1(self):
+        self.over_z1.wait_recv()
+        mine = self.second[self.z1].astype(F32)
+        self.third[...] = (mine + self.third[...].astype(F32)).astype(BF16)
+        if self.done is not None:
+            for copy in self.share:
+                copy.start()
+            self.done[self.s] = self.third[self.s]
+
+    def end(self):
+        for copy in self.share:
+            copy.wait_recv()
+
+
+def last_kernel(
+    down_ref, mlp_ref, og_ref, branch_ref, wo_ref, qkv_ref, pre_ref, log_ref, w_ref, normed_ref,
+    x_ref, residual_ref, gain_ref, mlp_gain_ref, qg_ref, kg_ref, cos_ref, sin_ref,
+    tokens_ref, down_out, mlp_out, out_out, in_out, sums_ref,
+    d1, d2, c1, c2, c3, o1, o2, o3, a_v, a1, a2, a3,
+    do_v, gr_v, dk_v, dv_v, core_s, core_r, far_s, far_r, acc_v, total_v, got_v,
+    send, recv, local,
+):
+    links = Links(send, recv)
+    d, s = links.d, links.s
+    sequences, blocks, piece, width = branch_ref.shape
+    half = blocks // 2
+    heads = log_ref.shape[1]
+    heads_kv = heads // 2
+    x_bit, core = bit_of(s, 1), bit_of(s, 0)
+    z1, z0, y = bit_of(d, 2), bit_of(d, 1), bit_of(d, 0)
+    place_of = lambda i: lax.rem((i & 1) + core, 2) * 2 + lax.rem((i >> 1) + x_bit, 2)
+    across, beside = lax.rem(x_bit + y, 2), lax.rem(core + z0, 2)
+    holder = (across == 0) & (beside == 0)
+    lanes = lambda at: pl.ds(pl.multiple_of(at * HEAD_SIZE, HEAD_SIZE), HEAD_SIZE)
+    nothing = lambda: None
+
+    down = Scatter(links, down_ref, d1, d2, down_out)
+    mlp = Scatter(links, mlp_ref, c1, c2, c3, mlp_out)
+    ins = [
+        Scatter(links, a_v.at[j], a1.at[j], a2.at[j], a3.at[j], in_out.at[j]) for j in range(heads_kv)
+    ]
+    base = links.slots(7)
+    out_z0 = links.plan(og_ref, o1, base, when=beside == 1, dp=flip(d, 1))
+    out_z1 = links.plan(o1.at[1 - z1], o2, base + 1, when=beside == 0, dp=flip(d, 2))
+    out_y = links.plan(o2, o3, base + 2, when=(beside == 0) & (across == 1), dp=flip(d, 0))
+    out_share = {
+        k: links.plan(o3.at[links.seq_at(k)], out_out, base + 3 + k, when=holder, seq=links.seq_at(k))
+        for k in (1, 2, 3)
+    }
+
+    def out_sum_z0():
+        @pl.when(beside == 0)
+        def _():
+            out_z0.wait_recv()
+
+            def step(i, carry):
+                a, b = lax.div(i, blocks), lax.rem(i, blocks)
+                o1[a, b] = (og_ref[a, b].astype(F32) + o1[a, b].astype(F32)).astype(BF16)
+                return carry
+
+            lax.fori_loop(0, 2 * blocks, step, 0)
+            out_z1.start()
+
+    def out_sum_z1():
+        @pl.when(beside == 0)
+        def _():
+            out_z1.wait_recv()
+
+            def step(b, carry):
+                o2[b] = (o1[z1, b].astype(F32) + o2[b].astype(F32)).astype(BF16)
+                return carry
+
+            lax.fori_loop(0, blocks, step, 0)
+
+        pl.when((beside == 0) & (across == 1))(out_y.start)
+
+    def out_sum_y():
+        @pl.when(holder)
+        def _():
+            out_y.wait_recv()
+
+            def step(b, carry):
+                o3[b] = (o2[b].astype(F32) + o3[b].astype(F32)).astype(BF16)
+                return carry
+
+            lax.fori_loop(0, blocks, step, 0)
+            for copy in out_share.values():
+                copy.start()
+            out_out[...] = o3[s]
+
+    links.greet((1, 2, 4), (1, 2, 3))
+    upper = pltpu.make_async_copy(residual_ref, tokens_ref, local.at[0])
+    upper.start()
+    mlp.start()
+    down.start()
+    pl.when(beside == 1)(out_z0.start)
+    total_v[0] = jnp.zeros_like(total_v[0])
+    for r in range(width // 128):
+        total_v[0, 8 + r : 9 + r, :] = mlp_gain_ref[:, r * 128 : (r + 1) * 128]
+
+    def mixed_back(i, carry):
+        n, b = lax.div(i, blocks), lax.rem(i, blocks)
+        do_v[n, b] = dot_t(branch_ref[n, b], wo_ref[...]).astype(BF16)
+        return carry
+
+    lax.fori_loop(0, sequences * blocks, mixed_back, 0)
+
+    slots = [links.slots(half * sequences), links.slots(sequences)]
+    core_copies = {
+        (n, k): links.plan(core_s.at[n, k], core_r.at[n, k], slots[0] + half * n + k, seq=links.seq_at(1))
+        for n in range(sequences)
+        for k in range(half)
+    }
+    far_copies = [
+        links.plan(far_s.at[n], far_r.at[n], slots[1] + n, seq=links.seq_at(2)) for n in range(sequences)
+    ]
+
+    def input_part(n):
+        def step(i, carry):
+            b = lax.rem(i + half, blocks)
+            grad = dot_t(gr_v[n, b], w_ref[...])
+            for k in range(half):
+
+                @pl.when(i == k)
+                def _():
+                    core_s[n, k] = grad.astype(BF16)
+                    core_copies[n, k].start()
+
+                @pl.when(i == half + k)
+                def _():
+                    core_copies[n, k].wait_recv()
+                    total = grad + core_r[n, k].astype(F32)
+                    if k == 0:
+                        acc_v[n] = total
+                    else:
+                        far_s[n] = total.astype(BF16)
+                        far_copies[n].start()
+
+            return carry
+
+        lax.fori_loop(0, blocks, step, 0)
+
+    def input_end(n):
+        far_copies[n].wait_recv()
+        grad = acc_v[n] + far_r[n].astype(F32)
+        tokens = x_ref[n].astype(F32)
+        scale = rms_scale(tokens)
+        scaled = grad * gain_ref[...]
+        tokens_ref[n] = (
+            tokens_ref[n]
+            + scale * scaled
+            - tokens * (scale * scale * scale * jnp.mean(scaled * tokens, axis=-1, keepdims=True))
+        )
+        part = jnp.sum(grad * tokens * scale, axis=0, keepdims=True)
+        for r in range(width // 128):
+            total_v[0, r : r + 1, :] += part[:, r * 128 : (r + 1) * 128]
+
+    def attention(j, meanwhile):
+        def step(t, carry):
+            for k, action in enumerate(meanwhile):
+                pl.when(t == k)(action)
+            n, g = lax.div(t, 2), lax.rem(t, 2)
+
+            @pl.when(g == 0)
+            def _():
+                dk_v[...] = jnp.zeros_like(dk_v)
+                dv_v[...] = jnp.zeros_like(dv_v)
+
+            keys, values = qkv_ref.at[n, :, lanes(4 * j + 2)], qkv_ref.at[n, :, lanes(4 * j + 3)]
+            keys_t = keys[...].T
+            for i in range(blocks):
+                rows = slice(i * piece, (i + 1) * piece)
+                end = (i + 1) * piece
+                at = place_of(i)
+                query = qkv_ref[n, rows, lanes(4 * j + g)]
+                grad_out = do_v[n, at, :, lanes(2 * j + g)]
+                probs, _ = masked_exp(keys, query, i, piece, log_ref[n, 2 * j + g, :, rows])
+                dv_v[:end, :] += dot(probs.astype(BF16), grad_out)
+                grad_probs = dot_t(values[:end, :], grad_out)
+                inner = jnp.sum(probs * grad_probs, axis=0, keepdims=True)
+                grad_scores = (probs * (grad_probs - inner)).astype(BF16)
+                dk_v[:end, :] += dot(grad_scores, query)
+                grad_query = dot(keys_t[:, :end], grad_scores).T * SCALE
+                result, gain = head_back(
+                    grad_query, pre_ref[n, rows, lanes(3 * j + g)], qg_ref[...], cos_ref[rows, :], sin_ref[rows, :]
+                )
+                gr_v[n, at, :, lanes(4 * j + g)] = result.astype(BF16)
+                total_v[0, 16:17, :] += gain
+
+            @pl.when(g == 1)
+            def _():
+                for i in range(blocks):
+                    rows = slice(i * piece, (i + 1) * piece)
+                    at = place_of(i)
+                    result, gain = head_back(
+                        dk_v[rows, :] * SCALE, pre_ref[n, rows, lanes(3 * j + 2)], kg_ref[...],
+                        cos_ref[rows, :], sin_ref[rows, :],
+                    )
+                    gr_v[n, at, :, lanes(4 * j + 2)] = result.astype(BF16)
+                    gr_v[n, at, :, lanes(4 * j + 3)] = dv_v[rows, :].astype(BF16)
+                    total_v[0, 17:18, :] += gain
+
+            return carry
+
+        lax.fori_loop(0, 2 * sequences, step, 0)
+
+    def weight_in(j):
+        wide = 4 * HEAD_SIZE
+        chunk = 2 * width // 8
+
+        def step(m, carry):
+            cut = pl.ds(pl.multiple_of(m * chunk, chunk), chunk)
+            total = None
+            for n in range(sequences):
+                left = normed_ref[n, :, :, cut].reshape(blocks * piece, chunk)
+                right = gr_v[n, :, :, j * wide : (j + 1) * wide].reshape(blocks * piece, wide)
+                term = t_dot(left, right)
+                total = term if total is None else total + term
+            a_v[j, lax.div(m, 2), lax.rem(m, 2)] = total.astype(BF16).reshape(a_v.shape[3:])
+            return carry
+
+        lax.fori_loop(0, width // chunk, step, 0)
+        ins[j].start()
+
+    attention(0, [nothing, nothing, out_sum_z0])
+    weight_in(0)
+    attention(1, [out_sum_z1, mlp.sum_y, lambda: input_part(0)])
+    input_part(1)
+    weight_in(1)
+    down.sum_y()
+    mlp.sum_z0()
+    upper.wait()
+    for n in range(sequences):
+        input_end(n)
+
+    gain_slots = links.slots(5)
+    gain_to = [dict(seq=links.seq_at(1)), dict(seq=links.seq_at(2))] + [dict(dp=flip(d, b)) for b in range(3)]
+    gain_copies = [
+        links.plan(total_v.at[k], got_v.at[k], gain_slots + k, **gain_to[k]) for k in range(5)
+    ]
+
+    def gain_stage(k):
+        gain_copies[k].wait_recv()
+        if k == 4:
+            sums_ref[...] = total_v[4] + got_v[4]
+        else:
+            total_v[k + 1] = total_v[k] + got_v[k]
+            gain_copies[k + 1].start()
+
+    gain_copies[0].start()
+    ins[0].sum_y()
+    gain_stage(0)
+    down.sum_z0()
+    gain_stage(1)
+    out_sum_y()
+    mlp.sum_z1()
+    gain_stage(2)
+    ins[0].sum_z0()
+    down.sum_z1()
+    gain_stage(3)
+    ins[0].sum_z1()
+    ins[1].sum_y()
+    gain_stage(4)
+    ins[1].sum_z0()
+    ins[1].sum_z1()
+    for k, copy in out_share.items():
+        pl.when((across == k >> 1) & (beside == (k & 1)))(copy.wait_recv)
+    mlp.end()
+    for scatter in ins:
+        scatter.end()
+    links.finish()
+
+
+def last(
+    down, mlp, out, branch, w_o, qkv, pre, log_total, w_in, normed, x, residual,
+    gain, mlp_gain_grad, query_gain, key_gain, cosine, sine,
+):
+    sequences, blocks, piece, width = branch.shape
+    length = blocks * piece
+    rows, wide = mlp.shape[-2], mlp.shape[-1]
+    down_rows = down.shape[-2]
+    out_rows = out.shape[-2]
+    heads_kv = qkv.shape[-1] // (4 * HEAD_SIZE)
+    vmem = pl.BlockSpec(memory_space=pltpu.VMEM)
+    shape = jax.ShapeDtypeStruct
+    b16 = lambda *dims: pltpu.VMEM(dims, BF16)
+    f32 = lambda *dims: pltpu.VMEM(dims, F32)
+    part = (blocks, rows, 4 * HEAD_SIZE)
+    return pl.pallas_call(
+        last_kernel,
+        name="last",
+        out_shape=(
+            shape((sequences, piece, width), F32),
+            shape((down_rows, width), BF16),
+            shape((blocks, rows, wide), BF16),
+            shape((out_rows, width), BF16),
+            shape((heads_kv,) + part, BF16),
+            shape((24, 128), F32),
+        ),
+        in_specs=[vmem] * 11 + [pl.BlockSpec(memory_space=pl.ANY)] + [vmem] * 6,
+        out_specs=[vmem] * 6,
+        scratch_shapes=[
+            b16(2, 2, down_rows, width),
+            b16(2, down_rows, width),
+            b16(2, 2, blocks, rows, wide),
+            b16(2, blocks, rows, wide),
+            b16(blocks, rows, wide),
+            b16(2, blocks, out_rows, width),
+            b16(blocks, out_rows, width),
+            b16(blocks, out_rows, width),
+            b16(heads_kv, 2, 2, 2, *part),
+            b16(heads_kv, 2, 2, *part),
+            b16(heads_kv, 2, *part),
+            b16(heads_kv, *part),
+            b16(sequences, blocks, piece, 2 * heads_kv * HEAD_SIZE),
+            b16(sequences, blocks, piece, width),
+            f32(length, HEAD_SIZE),
+            f32(length, HEAD_SIZE),
+            b16(sequences, blocks // 2, piece, width),
+            b16(sequences, blocks // 2, piece, width),
+            b16(sequences, piece, width),
+            b16(sequences, piece, width),
+            f32(sequences, piece, width),
+            f32(5, 24, 128),
+            f32(5, 24, 128),
+            pltpu.SemaphoreType.DMA((64,)),
+            pltpu.SemaphoreType.DMA((64,)),
+            pltpu.SemaphoreType.DMA((1,)),
+        ],
+        compiler_params=pltpu.CompilerParams(
+            collective_id=2, has_side_effects=True, vmem_limit_bytes=67043328
+        ),
+    )(
+        down, mlp, out, branch, w_o, qkv, pre, log_total, w_in, normed, x, residual,
+        gain, mlp_gain_grad, query_gain, key_gain, cosine, sine,
+    )
+
+
 def body(
     hidden_in,
     attn_gain,
@@ -857,7 +1476,7 @@
     units = dp * down_rows
     package_mlp = jnp.concatenate([by_unit(w_gate), by_unit(w_up)], axis=2)
 
-    fused = (dp, seq) == (8, 4) and width == 128 * dp and rows % 16 == 0 and down_rows % 16 == 0
+    fused = (dp, seq, heads_kv) == (8, 4, 8) and width == 128 * dp and rows % 16 == 0 and down_rows % 16 == 0
     if fused:
         gains = jnp.zeros((8, seq, width // count), F32)
         gains = lax.dynamic_update_slice(gains, own_gains.astype(F32)[:, None], (0, wires.s, 0))
@@ -870,6 +1489,9 @@
         w_in, w_mlp = w_in.reshape(width, -1), w_mlp.reshape(width, -1)
         w_o, w_d = w_o.reshape(-1, width), w_d.reshape(units, width)
         attn_gain_row, mlp_gain_row = gains[:1], gains[1:2]
+        (
+            all_out, all_grad_residual, all_normed_mlp, all_hidden, all_grad_both, all_branch, mlp_gain_grad
+        ) = feed_forward(all_mixed, w_o, w_mlp, w_d, x_rel, g_rel, mlp_gain_row)
     else:
         gains = jnp.zeros((2, count, width // count), BF16)
         gains = lax.dynamic_update_slice(gains, own_gains[:, None], (0, index, 0))
@@ -886,15 +1508,11 @@
 
     kept = []
     outs = []
-    for n in range(sequences):
-        if fused:
-            normed, qkv, pre = all_normed[n], all_qkv[n], all_pre[n]
-            mixed, log_total = all_mixed[n], all_log[n]
-        else:
-            normed, qkv, pre = project(
-                s_index, x_rel[n], w_in, attn_gain_row, query_gain_row, key_gain_row, cosine, sine, x_count
-            )
-            mixed, log_total = attend(s_index, qkv, seq, x_count)
+    for n in range(0 if fused else sequences):
+        normed, qkv, pre = project(
+            s_index, x_rel[n], w_in, attn_gain_row, query_gain_row, key_gain_row, cosine, sine, x_count
+        )
+        mixed, log_total = attend(s_index, qkv, seq, x_count)
         mixed_rows = mixed.reshape(length, -1)
         other = wires.swap(dot(mixed_rows[part:], w_o).astype(BF16), 1)
         total = wires.sum_x(dot(mixed_rows[:part], w_o) + other.astype(F32))
@@ -959,27 +1577,48 @@
             )
         )
 
-    def over(name):
-        return jnp.concatenate([k[name] for k in kept], axis=0)
-
-    grad_down = t_dot(over("hidden"), g_rel.reshape(-1, width)).astype(BF16)
-    grad_down = wires.scatter_dp(grad_down.reshape(dp, down_rows, width)).astype(F32)
-
-    grad_mlp = t_dot(over("normed_mlp"), over("grad_both")).astype(BF16)
-    grad_mlp = wires.scatter_dp(grad_mlp.reshape(dp, seq * rows, -1))
-    grad_mlp = wires.exchange_seq(grad_mlp.reshape(seq, rows, -1)).astype(F32)
-
     def from_unit(g):
         return g.reshape(seq, rows, dp, down_rows).transpose(1, 2, 0, 3).reshape(rows, -1)
 
+    if fused:
+        flat = lambda value: value.reshape(sequences * length, -1)
+        grad_mlp = t_dot(flat(all_normed_mlp), flat(all_grad_both)).astype(BF16)
+        grad_down = t_dot(flat(all_hidden), flat(g_rel)).astype(BF16)
+        grad_out = t_dot(flat(all_mixed), flat(all_branch)).astype(BF16)
+        grad_tokens, grad_down, grad_mlp, grad_out, grad_in, gain_sums = last(
+            grad_down.reshape(2, 2, 2, down_rows, width),
+            grad_mlp.reshape(2, 2, 2, seq, rows, -1),
+            grad_out.reshape(2, seq, -1, width),
+            all_branch, w_o, all_qkv, all_pre, all_log, w_in, all_normed, hidden_in, all_grad_residual,
+            attn_gain_row, mlp_gain_grad, query_gain_row, key_gain_row, cosine, sine,
+        )
+        grad_down, grad_mlp, grad_out = grad_down.astype(F32), grad_mlp.astype(F32), grad_out.astype(F32)
+        grad_in = grad_in.astype(F32).transpose(1, 2, 0, 3).reshape(seq, rows, -1)
+        gain_sums = gain_sums.reshape(-1)[: 2 * width + 2 * HEAD_SIZE]
+        hidden_out = all_out
+    else:
+        def over(name):
+            return jnp.concatenate([k[name] for k in kept], axis=0)
+
+        grad_down = t_dot(over("hidden"), g_rel.reshape(-1, width)).astype(BF16)
+        grad_down = wires.scatter_dp(grad_down.reshape(dp, down_rows, width)).astype(F32)
+
+        grad_mlp = t_dot(over("normed_mlp"), over("grad_both")).astype(BF16)
+        grad_mlp = wires.scatter_dp(grad_mlp.reshape(dp, seq * rows, -1))
+        grad_mlp = wires.exchange_seq(grad_mlp.reshape(seq, rows, -1)).astype(F32)
+
+
+        grad_out = t_dot(over("mixed"), over("branch")).astype(BF16)
+        grad_out = wires.scatter_out(grad_out, heads_kv).astype(F32)
+
+        grad_in = t_dot(over("normed"), over("grad_rows")).astype(BF16)
+        grad_in = wires.scatter_dp(grad_in.reshape(dp, seq * rows, -1))
+        grad_in = wires.exchange_seq(grad_in.reshape(seq, rows, -1)).astype(F32)
+        gain_sums = wires.sum_all(sum(k["gains"] for k in kept))
+        grad_tokens = jnp.stack([k["grad_tokens"] for k in kept])
+        hidden_out = jnp.stack(outs)
+
     grad_gate, grad_up = from_unit(grad_mlp[..., :units]), from_unit(grad_mlp[..., units:])
-
-    grad_out = t_dot(over("mixed"), over("branch")).astype(BF16)
-    grad_out = wires.scatter_out(grad_out, heads_kv).astype(F32)
-
-    grad_in = t_dot(over("normed"), over("grad_rows")).astype(BF16)
-    grad_in = wires.scatter_dp(grad_in.reshape(dp, seq * rows, -1))
-    grad_in = wires.exchange_seq(grad_in.reshape(seq, rows, -1)).astype(F32)
     pieces = [None] * heads_kv
     for t in range(seq):
         for m, j in enumerate(order[t]):
@@ -988,13 +1627,12 @@
     grad_key = jnp.concatenate([p[:, 2 * HEAD_SIZE : 3 * HEAD_SIZE] for p in pieces], axis=1)
     grad_value = jnp.concatenate([p[:, 3 * HEAD_SIZE :] for p in pieces], axis=1)
 
-    gain_sums = wires.sum_all(sum(k["gains"] for k in kept))
     own = width // count
     grad_attn_gain = lax.dynamic_slice_in_dim(gain_sums, index * own, own)
     grad_mlp_gain = lax.dynamic_slice_in_dim(gain_sums, width + index * own, own)
     return (
-        jnp.stack(outs),
-        jnp.stack([k["grad_tokens"] for k in kept]),
+        hidden_out,
+        grad_tokens,
         grad_attn_gain,
         grad_query,
         grad_key,

time: 493 us -> 408 us (0.83)
  Pallas kernels: 138 us -> 354 us
  waiting for transfers between devices: 140 us -> 0 us
  matrix products: 87.4 us -> 19.4 us
  local copies, waits for them, and re-layouts: 57.6 us -> 18.4 us
  starting transfers between devices: 32.2 us -> 0 us
  other arithmetic: 31.7 us -> 11 us
    pallas_call x2, Pallas kernels: 34.7 us -> 251 us  [the longest x1 126 us: last(): pl.pallas_call(last_kernel, name='last', out_shape=(shape((sequences, pie...]
    ppermute x43 -> x0, waiting for transfers between devices: 140 us -> none  [swap(): return lax.ppermute(value, AXES, pairs)]
    dot_general x22 -> x0, matrix products: 64.9 us -> none  [the longest x12 43 us: dot_t(): lax.dot_general(a, b, (((1,), (1,)), ((), ())), preferred_element_type=F32)]
    ppermute x43 -> x0, starting transfers between devices: 32.2 us -> none  [swap(): return lax.ppermute(value, AXES, pairs)]
    slice x19 -> x1, local copies, waits for them, and re-layouts: 20.2 us -> 0.71 us  [body(): gain_sums = gain_sums.reshape(-1)[:2 * width + 2 * HEAD_SIZE]]
    squeeze x14 -> x0, local copies, waits for them, and re-layouts: 9.91 us -> none  [the longest x2 5.61 us: body(): normed, qkv, pre = (all_normed[n], all_qkv[n], all_pre[n])]
    reduce_sum x7 -> x0, other arithmetic: 9.43 us -> none  [the longest x2 3.11 us: body(): grad_mlp_gain = jnp.sum((grad_normed * residual * scale)[:piece], axis=0)]
    convert_element_type x17 -> x2, other arithmetic: 10.5 us -> 3.33 us  [the longest x1 1.7 us: body(): grad_down.astype(F32)]
  transfers between devices with their start and end apart: 43 -> 0, of which waited for: 18 -> 0; matrix products, arithmetic and copies ran while one was open for 27% -> 0% of each run, Pallas kernels for 7% -> 0%
where the time goes in v4:
time: 408 us; the launch traced here: 404 us
  Pallas kernels  354 us (87%)
  matrix products  19.4 us (5%)
  local copies, waits for them, and re-layouts  18.4 us (5%)
  other arithmetic  11 us (3%)
    pallas_call x1, Pallas kernels, last(): pl.pallas_call(last_kernel, name='last', out_shape=(shape((sequences, pie...  126 us
    pallas_call x1, Pallas kernels, feed_forward(): pl.pallas_call(mlp_kernel, name='feed_forward', out_shape=(shape((sequenc...  125 us
    pallas_call x1, Pallas kernels, first(): pl.pallas_call(functools.partial(first_kernel, heads), name='first', out_...  103 us
    dot_general x3, matrix products, t_dot(): lax.dot_general(a, b, (((0,), (0,)), ((), ())), preferred_element_type=F32)  19.4 us

profile of v4, /device:TPU:0, one launch (start us, length us, event | category | flops | bytes accessed | tf_op | source)
XLA Modules:
  0.0 403.7 jit_solution(12161455999731023992)
XLA Ops:
  0.7 0.7 maximum_convert_fusion
  1.3 1.2 bitcast_convert_fusion.3
  2.6 0.7 reshape.159.gains_ref
  3.3 0.9 bitcast_dynamic-update-slice_fusion
  4.2 0.9 bitcast_dynamic-update-slice_fusion.2
  5.0 0.9 bitcast_dynamic-update-slice_fusion.1
  6.0 0.7 pad_maximum_fusion.3.a_ref
  6.7 1.2 reshape.155
  8.0 0.2 reshape.156
  8.2 1.2 reshape.157
  9.4 0.2 reshape.158
  9.6 0.8 pad_maximum_fusion.2.c_ref
  10.4 1.9 fusion
  12.3 1.3 pad_maximum_fusion
  13.6 103.1 %first.1 = (bf16[2,4,256,1024]{3,2,1,0:T(8,128)(2,1)}, bf16[2,4,256,1024]{3,2,1,0:T(8,128)(2,1)}, bf16[8,4,32,1024]{3,2,1,0:T(8,128)(2,1)}, bf16[8,4,32,1536]{3,...) custom-call(bf16[4,32,1024]{2,1,0:T(8,128)(2,1)} %pad_maximum_fusion, ...), custom_call_target="tpu_custom_call" | custom-call | tf_op jit(solution)/shard_map/first/pallas_call | solution.py:773
  116.7 1.4 fusion.2
  118.2 125.0 %feed_forward.1 = (bf16[2,256,1024]{2,1,0:T(8,128)(2,1)}, f32[2,256,1024]{2,1,0:T(8,128)}, bf16[2,4,256,1024]{3,2,1,0:T(8,128)(2,1)}, bf16[2,4,256,768]{3,2,1,0:...) custom-call(bf16[2,4,256,512]{3,2,1,0:T(8,128)(2,1)} %get-tuple-element.38.mi, ...), custom_call_target="tpu_custom_call" | custom-call | tf_op jit(solution)/shard_map/feed_forward/pallas_call | solution.py:1007
  243.2 0.0 copy-start
  243.2 0.0 copy-start.7
  243.2 0.0 slice-start
  243.2 6.3 %bitcast_convert_fusion.2 = bf16[512,1024]{1,0:T(8,128)(2,1)} fusion(bf16[2,4,256,512]{3,2,1,0:T(8,128)(2,1)} %get-tuple-element.38.mixed_ref, bf16[2,4,256,1024]{3,2,1,0:T(8,128)(2,1)} %get-tuple-element.49.branch_ref), kind=kOutput, calls=%fused_computation.2 | convolution fusion | flops 2148007936 | bytes 7340032 | tf_op jit(solution)/shard_map/dot_general | solution.py:203
  249.5 0.0 slice-start.1
  249.5 0.0 copy-done
  249.5 0.0 copy-done.7
  249.5 0.0 copy-start.6
  249.5 4.6 %bitcast_convert_fusion.1 = bf16[768,1024]{1,0:T(8,128)(2,1)} fusion(bf16[2,4,256,768]{3,2,1,0:T(8,128)(2,1)S(1)} %copy-done.7, bf16[2,4,256,1024]{3,2,1,0:T(8,128)(2,1)S(1)} %copy-done), kind=kOutput, calls=%fused_computation.1 | convolution fusion | flops 3222011904 | bytes 8912896 | tf_op jit(solution)/shard_map/dot_general | solution.py:203
  254.1 0.0 slice-done
  254.1 0.0 slice-done.1
  254.1 0.0 copy-done.6
  254.1 8.6 %bitcast_convert_fusion = bf16[1024,1536]{1,0:T(8,128)(2,1)} fusion(bf16[2,4,256,1024]{3,2,1,0:T(8,128)(2,1)S(1)} %copy-done.6, bf16[2,4,256,1536]{3,2,1,0:T(8,128)(2,1)S(1)} %bitcast.125), kind=kOutput, calls=%fused_computation | convolution fusion | flops 6444023808 | bytes 13631488 | tf_op jit(solution)/shard_map/dot_general | solution.py:203
  262.7 125.6 %last.1 = (f32[2,256,1024]{2,1,0:T(8,128)}, bf16[96,1024]{1,0:T(8,128)(2,1)}, bf16[4,32,1536]{2,1,0:T(8,128)(2,1)}, bf16[64,1024]{1,0:T(8,128)(2,1)}, bf16[2,4,3...) custom-call(bf16[2,2,2,96,1024]{4,3,2,1,0:T(8,128)(2,1)} %bitcast.116, bf16[2,2,2,4,32,1536]{5,4,3,2,1,0:T(8,128)(2,1)} %bitcast.111, ...), custom_call_target="tpu_custom_call" | custom-call | tf_op jit(solution)/shard_map/last/pallas_call | solution.py:1379
  388.2 0.0 copy-start.2
  388.2 1.3 slice_bitcast_fusion.17
  389.5 0.7 slice_bitcast_fusion.16
  390.2 0.6 fusion.3
  390.8 1.6 convert_element_type.63
  392.4 1.7 convert_element_type.65
  394.1 1.0 convert_bitcast_fusion
  395.3 0.0 copy-start.3
  395.5 0.0 copy-start.4
  395.5 0.0 copy-start.5
  395.5 0.6 copy-done.3
  396.0 0.1 copy-done.4
  396.1 0.0 copy-done.5
  396.2 0.0 copy-done.2
  396.2 0.1 fusion.1
  396.2 0.0 copy-start.1
  396.2 0.3 reshape.175
  396.5 0.3 copy.43
  396.8 1.2 reshape.176
  398.0 0.3 reshape.173
  398.3 0.3 copy.42
  398.6 1.2 reshape.174
  399.8 2.3 copy.87
  402.1 0.0 copy-done.1
  402.1 1.3 copy.88
  (28 shorter events, 0.3 us)
Async XLA Ops:
  243.2 6.3 %copy-start = (bf16[2,4,256,1024]{3,2,1,0:T(8,128)(2,1)S(1)}, bf16[2,4,256,1024]{3,2,1,0:T(8,128)(2,1)}, u32[]{:S(2)}) copy-start(bf16[2,4,256,1024]{3,2,1,0:T(8,128)(2,1)} %get-tuple-element.43.g_ref) | copy-start | bytes 12582916
  243.2 6.3 %copy-start.7 = (bf16[2,4,256,768]{3,2,1,0:T(8,128)(2,1)S(1)}, bf16[2,4,256,768]{3,2,1,0:T(8,128)(2,1)}, u32[]{:S(2)}) copy-start(bf16[2,4,256,768]{3,2,1,0:T(8,128)(2,1)} %get-tuple-element.46) | copy-start | bytes 9437188
  243.2 10.9 %slice-start = ((s8[6291456]{0:T(1024)(128)(4,1)}), s8[4194304]{0:T(1024)(128)(4,1)S(1)}, s32[]{:S(2)}) async-start(s8[6291456]{0:T(1024)(128)(4,1)} %bitcast.124), calls=%async_computation | async-start | bytes 8388608
  249.5 4.6 %slice-start.1 = ((s8[6291456]{0:T(1024)(128)(4,1)}), s8[2097152]{0:T(1024)(128)(4,1)S(1)}, s32[]{:S(2)}) async-start(s8[6291456]{0:T(1024)(128)(4,1)} %bitcast.124), calls=%async_computation.1 | async-start | bytes 4194304
  249.5 4.6 %copy-start.6 = (bf16[2,4,256,1024]{3,2,1,0:T(8,128)(2,1)S(1)}, bf16[2,4,256,1024]{3,2,1,0:T(8,128)(2,1)}, u32[]{:S(2)}) copy-start(bf16[2,4,256,1024]{3,2,1,0:T(8,128)(2,1)} %get-tuple-element.47) | copy-start | bytes 12582916
  388.2 7.9 %copy-start.2 = (bf16[4,32,1536]{2,1,0:T(8,128)(2,1)S(1)}, bf16[4,32,1536]{2,1,0:T(8,128)(2,1)}, u32[]{:S(2)}) copy-start(bf16[4,32,1536]{2,1,0:T(8,128)(2,1)} %get-tuple-element.61) | copy-start | bytes 1179652
  395.3 0.7 copy-start.3
  395.5 0.7 copy-start.4
  395.5 0.7 copy-start.5
  396.2 5.9 %copy-start.1 = (f32[2,256,1024]{2,1,0:T(8,128)S(1)}, f32[2,256,1024]{2,1,0:T(8,128)}, u32[]{:S(2)}) copy-start(f32[2,256,1024]{2,1,0:T(8,128)} %get-tuple-element.128) | copy-start | bytes 6291460

commit v5 on v4

--- a/solution.py
+++ b/solution.py
@@ -557,13 +557,14 @@
 def first_kernel(
     heads,
     a_ref, c_ref, out_ref, down_ref, x_ref, g_ref, gains_ref, qg_ref, kg_ref, cos_ref, sin_ref,
-    xr_ref, gr_ref, wa_ref, wc_ref, wo_ref, wd_ref, n_ref, qkv_ref, pre_ref, o_ref, log_ref, gain_ref,
-    w_v, x_v, n_v, qkv_v, pre_v, o_v, got_v, send, recv, local,
+    xr_ref, gr_ref, wa_ref, wc_ref, wo_ref, wd_ref, n_ref, qkv_ref, pre_ref, o_ref, residual_ref, log_ref, gain_ref,
+    w_v, x_v, n_v, qkv_v, pre_v, o_v, got_v, wo_v, res_v, core_s, core_r, far_s, far_r, send, recv, local,
 ):
     links = Links(send, recv)
     d, s = links.d, links.s
     sequences, piece, width = x_ref.shape
     blocks = xr_ref.shape[1]
+    half = blocks // 2
     length = blocks * piece
     x_bit, core = bit_of(s, 1), bit_of(s, 0)
     z1, z0, y = bit_of(d, 2), bit_of(d, 1), bit_of(d, 0)
@@ -607,13 +608,6 @@
     def pass_on(copies):
         copies[0].wait_recv()
         copies[2].start()
-
-    x_copies = [spread(x_ref, xr_ref, x_slots, 0)]
-    c_own = exchange(c_ref, wc_ref)
-    near("c", c_ref.at[s], wc_ref.at[d, s])
-    for n in range(sequences):
-        near(f"x{n}", x_ref.at[n], xr_ref.at[n, 0])
-    near("d", down_ref, wd_ref.at[d])
 
     across, beside = lax.rem(x_bit + y, 2), lax.rem(core + z0, 2)
     out_slots = links.slots(7)
@@ -625,6 +619,12 @@
         )
         for k in (1, 2, 3)
     ]
+    x_copies = [spread(x_ref, xr_ref, x_slots, 0)]
+    c_own = exchange(c_ref, wc_ref)
+    near("c", c_ref.at[s], wc_ref.at[d, s])
+    for n in range(sequences):
+        near(f"x{n}", x_ref.at[n], xr_ref.at[n, 0])
+    near("d", down_ref, wd_ref.at[d])
     x_copies += [spread(x_ref, xr_ref, x_slots, n) for n in range(1, sequences)]
 
     for copy in gain_own + a_own:
@@ -633,12 +633,22 @@
     gather_a, gather_c, gather_d, gather_gain = (
         Gather(links, lambda at, ref=ref: ref.at[at]) for ref in (wa_ref, wc_ref, wd_ref, got_v)
     )
+    out_y = links.plan(wo_ref.at[z1], wo_ref.at[z1], out_slots + 4, when=holder, dp=flip(d, 0))
+    out_z1 = links.plan(wo_ref.at[z1], wo_ref.at[z1], out_slots + 5, when=beside == 0, dp=flip(d, 2))
+    out_z0 = links.plan(wo_ref, wo_ref, out_slots + 6, when=beside == 0, dp=flip(d, 1))
+
+    def out_next():
+        pl.when((across == 1) & (beside == 0))(out_y.wait_recv)
+        pl.when(beside == 0)(out_z1.start)
+
+    def out_last():
+        @pl.when(beside == 0)
+        def _():
+            out_z1.wait_recv()
+            out_z0.start()
+
     gather_gain.first()
     gather_a.first()
-    for r in (2, 4, 6):
-        gather_gain.relay(r)
-
-    pass_on(x_copies[0])
 
     @pl.when(holder)
     def _():
@@ -647,16 +657,20 @@
         for copy in out_first:
             copy.wait_recv()
         own.wait()
+        out_y.start()
 
     local_used[0] += 1
+    for r in (2, 4, 6):
+        gather_gain.relay(r)
+    pass_on(x_copies[0])
     gather_a.relay(2)
+    out_next()
     gather_a.relay(4)
-    gather_a.relay(6)
-    out_y = links.start(wo_ref.at[z1], wo_ref.at[z1], out_slots + 4, when=holder, dp=flip(d, 0))
     for copy in c_own:
         copy.wait_recv()
     locals_["c"].wait()
     gather_c.first()
+    gather_a.relay(6)
     g_copies = [spread(g_ref, gr_ref, g_slots, n) for n in range(sequences)]
     for n in range(sequences):
         near(f"g{n}", g_ref.at[n], gr_ref.at[n, 0])
@@ -667,7 +681,7 @@
         locals_[f"x{n}"].wait()
         for copy in x_copies[n][1:]:
             copy.wait_recv()
-        near(f"xv{n}", xr_ref.at[n], x_v)
+        near(f"xv{n}", xr_ref.at[n], x_v.at[n])
         locals_[f"xv{n}"].wait()
 
     def project_part(n, meanwhile=()):
@@ -675,7 +689,7 @@
             for k, action in enumerate(meanwhile):
                 pl.when(i == k)(action)
             at = place_of(i)
-            x = x_v[at].astype(F32)
+            x = x_v[n, at].astype(F32)
             normed = (x * rms_scale(x) * gain_ref[0:1, :]).astype(BF16)
             n_v[n, at] = normed
             y_rows = dot(normed, w_v[...].reshape(width, -1))
@@ -727,36 +741,74 @@
     for at in range(got_v.shape[0]):
         gain_ref[:, at * 128 : (at + 1) * 128] = jnp.sum(got_v[at], axis=0)
 
-    out_z1 = links.plan(wo_ref.at[z1], wo_ref.at[z1], out_slots + 5, when=beside == 0, dp=flip(d, 2))
-    out_z0 = links.plan(wo_ref, wo_ref, out_slots + 6, when=beside == 0, dp=flip(d, 1))
-
-    def out_next():
-        pl.when((across == 1) & (beside == 0))(out_y.wait_recv)
-        pl.when(beside == 0)(out_z1.start)
-
-    def out_last():
-        @pl.when(beside == 0)
-        def _():
-            out_z1.wait_recv()
-            out_z0.start()
+    core_slots, far_slots = links.slots(half * sequences), links.slots(half * sequences)
+    core_copies = {
+        (n, k): links.plan(core_s.at[n, k], core_r.at[n, k], core_slots + half * n + k, seq=links.seq_at(1))
+        for n in range(sequences)
+        for k in range(half)
+    }
+    far_copies = {
+        (n, k): links.plan(far_s.at[n, k], far_r.at[n, half - 1 - k], far_slots + half * n + k, seq=links.seq_at(2))
+        for n in range(sequences)
+        for k in range(half)
+    }
+
+    def out_part(n):
+        if n == 0:
+            pl.when(beside == 1)(out_z0.wait_recv)
+            near("wo", wo_ref, wo_v)
+            locals_["wo"].wait()
+
+        def step(i, carry):
+            b = lax.rem(i + half, blocks)
+            part = dot(o_v[n, b], wo_v[...].reshape(-1, width))
+            for k in range(half):
+
+                @pl.when(i == k)
+                def _():
+                    core_s[n, k] = part.astype(BF16)
+                    core_copies[n, k].start()
+
+                @pl.when(i == half + k)
+                def _():
+                    core_copies[n, k].wait_recv()
+                    total = part + core_r[n, k].astype(F32)
+                    res_v[n, k] = total
+                    far_s[n, k] = total.astype(BF16)
+                    far_copies[n, k].start()
+
+            return carry
+
+        lax.fori_loop(0, blocks, step, 0)
+
+    def residual(n):
+        for k in range(half):
+            far_copies[n, half - 1 - k].wait_recv()
+            res_v[n, k] = res_v[n, k] + far_r[n, k].astype(F32) + x_v[n, k].astype(F32)
+        near(f"res{n}", res_v.at[n], residual_ref.at[n])
 
     nothing = lambda: None
-    project_part(0, [out_next, lambda: gather_c.relay(2), lambda: pass_on(x_copies[1]), lambda: gather_c.relay(4)])
-    attend_part(0, [nothing, out_last, lambda: gather_c.relay(6), lambda: gather_d.relay(2)])
+    project_part(0, [nothing, lambda: gather_c.relay(2), lambda: pass_on(x_copies[1]), out_last])
+    attend_part(0, [lambda: gather_c.relay(4)])
     near("o0", o_v.at[0], o_ref.at[0])
     for n in range(1, sequences):
         wait_x(n)
-        project_part(n, [lambda: gather_d.relay(4), nothing, lambda: pass_on(g_copies[0])])
-        attend_part(n, [lambda: gather_d.relay(6), lambda: pass_on(g_copies[1])])
+        out_part(n - 1)
+        project_part(n, [lambda: gather_c.relay(6), nothing, lambda: pass_on(g_copies[0])])
+        attend_part(n, [nothing, nothing, lambda: pass_on(g_copies[1])])
         near(f"o{n}", o_v.at[n], o_ref.at[n])
+    out_part(sequences - 1)
+    for r in (2, 4, 6):
+        gather_d.relay(r)
+    for n in range(sequences):
+        residual(n)
     gather_c.last()
     gather_d.last()
-    pl.when(beside == 1)(out_z0.wait_recv)
     for pair in g_copies:
         for copy in pair[1:]:
             copy.wait_recv()
     for n in range(sequences):
-        for name in ("g", "n", "qkv", "pre", "o"):
+        for name in ("g", "n", "qkv", "pre", "o", "res"):
             locals_[f"{name}{n}"].wait()
     links.finish()
 
@@ -784,22 +836,29 @@
             shape((sequences, length, columns), BF16),
             shape((sequences, length, pre_columns), F32),
             shape((sequences, blocks, piece, heads * HEAD_SIZE), BF16),
+            shape((sequences, blocks // 2, piece, width), F32),
             shape((sequences, heads, 1, length), F32),
             shape((8, width), F32),
         ),
         in_specs=[vmem] * 11,
-        out_specs=[hbm] * 10 + [vmem] * 2,
+        out_specs=[hbm] * 11 + [vmem] * 2,
         scratch_shapes=[
             pltpu.VMEM((dp, blocks, rows, columns), BF16),
-            pltpu.VMEM((blocks, piece, width), BF16),
+            pltpu.VMEM((sequences, blocks, piece, width), BF16),
             pltpu.VMEM((sequences, blocks, piece, width), BF16),
             pltpu.VMEM((sequences, length, columns), BF16),
             pltpu.VMEM((sequences, length, pre_columns), F32),
             pltpu.VMEM((sequences, blocks, piece, heads * HEAD_SIZE), BF16),
             pltpu.VMEM((dp, blocks, 8, width // dp), F32),
+            pltpu.VMEM((2, blocks) + w_out.shape, BF16),
+            pltpu.VMEM((sequences, blocks // 2, piece, width), F32),
+            pltpu.VMEM((sequences, blocks // 2, piece, width), BF16),
+            pltpu.VMEM((sequences, blocks // 2, piece, width), BF16),
+            pltpu.VMEM((sequences, blocks // 2, piece, width), BF16),
+            pltpu.VMEM((sequences, blocks // 2, piece, width), BF16),
             pltpu.SemaphoreType.DMA((slots,)),
             pltpu.SemaphoreType.DMA((slots,)),
-            pltpu.SemaphoreType.DMA((24,)),
+            pltpu.SemaphoreType.DMA((32,)),
         ],
         compiler_params=pltpu.CompilerParams(
             collective_id=0, has_side_effects=True, vmem_limit_bytes=60 * 1024 * 1024
@@ -808,10 +867,10 @@
 
 
 def mlp_kernel(
-    mixed_ref, wo_ref, wc_ref, wd_ref, x_ref, g_ref, gain_ref,
-    out_ref, residual_ref, normed_ref, hidden_ref, both_ref, branch_ref, gain_grad_ref,
-    res_v, core_s, oc_v, x_s, og_v, n2_v, hidden_v, both_v, dc_v, dg_v, da_v, us_v, uc_v, ux_v, ug_v, ua_v,
-    send, recv, local, tokens_sem,
+    res_ref, wc_ref, wd_ref, g_ref, gain_ref,
+    own_ref, far_ref, residual_ref, branch_ref, down_ref, mlp_ref, gain_grad_ref,
+    core_s, x_s, n2_v, hidden_v, both_v, dc_v, dg_v, da_v, us_v, uc_v, ux_v, ua_v,
+    send, recv, local,
 ):
     links = Links(send, recv)
     sequences, blocks, piece, width = g_ref.shape
@@ -821,17 +880,14 @@
     pairs = [(n, k) for n in range(sequences) for k in range(half)]
     slots = {
         name: links.slots(half * sequences)
-        for name in ("o_core", "o_far", "normed", "grad_core", "up_core", "grad_far", "branch", "up_far")
+        for name in ("normed", "grad_core", "up_core", "grad_far", "branch")
     }
     ends = {
-        "o_core": lambda n, k: (core_s.at[n, k], oc_v.at[n, k], core),
-        "o_far": lambda n, k: (x_s.at[n, k], og_v.at[n, half - 1 - k], far),
         "normed": lambda n, k: (n2_v.at[n, k], n2_v.at[n, half + k], core),
         "grad_core": lambda n, k: (core_s.at[n, k], dc_v.at[n, k], core),
         "up_core": lambda n, k: (us_v.at[n, k], uc_v.at[n, k], core),
         "grad_far": lambda n, k: (x_s.at[n, k], dg_v.at[n, half - 1 - k], far),
         "branch": lambda n, k: (us_v.at[n, k], branch_ref.at[n, half + k], core),
-        "up_far": lambda n, k: (ux_v.at[n], ug_v.at[n], far),
     }
 
     def copy(name, n, k):
@@ -839,7 +895,7 @@
         return links.copy(src, dst, slots[name] + half * n + k, **to)
 
     def arrived(name, n, k):
-        copy(name, n, half - 1 - k if name in ("o_far", "grad_far") else k).wait_recv()
+        copy(name, n, half - 1 - k if name == "grad_far" else k).wait_recv()
 
     near_copies = []
 
@@ -849,52 +905,16 @@
         near_copies.append(made)
 
     links.greet((), (1, 2))
-    tokens = [
-        pltpu.make_async_copy(x_ref.at[n, pl.ds(0, half)], uc_v.at[n], tokens_sem.at[n])
-        for n in range(sequences)
-    ]
-    for made in tokens:
-        made.start()
     gain = gain_ref[...]
 
-    for n in range(sequences):
-
-        def out_part(i, carry):
-            b = lax.rem(i + half, blocks)
-            y = dot(mixed_ref[n, b], wo_ref[...])
-
-            @pl.when(i < half)
-            def _():
-                core_s[n, i] = y.astype(BF16)
-                copy("o_core", n, i).start()
-
-            @pl.when(i >= half)
-            def _():
-                res_v[n, i - half] = y
-
-            return carry
-
-        lax.fori_loop(0, blocks, out_part, 0)
+    def norm(n):
         for k in range(half):
-            arrived("o_core", n, k)
-            total = res_v[n, k] + oc_v[n, k].astype(F32)
-            res_v[n, k] = total
-            x_s[n, k] = total.astype(BF16)
-            copy("o_far", n, k).start()
-
-    def norm(n):
-        tokens[n].wait()
-        for k in range(half):
-            arrived("o_far", n, k)
-            residual = res_v[n, k] + og_v[n, k].astype(F32) + uc_v[n, k].astype(F32)
-            res_v[n, k] = residual
+            residual = res_ref[n, k]
             n2_v[n, k] = (residual * rms_scale(residual) * gain).astype(BF16)
             copy("normed", n, k).start()
 
     def feed(n):
         for k in range(half):
-            copy("o_core", n, k).wait_send()
-            copy("o_far", n, k).wait_send()
             arrived("normed", n, k)
 
         def step(i, carry):
@@ -939,19 +959,17 @@
 
             @pl.when(i == half)
             def _():
-                ua_v[n] = res_v[n, 0] + (up + uc_v[n, 0].astype(F32))
+                ua_v[n] = res_ref[n, 0] + (up + uc_v[n, 0].astype(F32))
 
             @pl.when(i == half + 1)
             def _():
                 ux_v[n] = (up + uc_v[n, 1].astype(F32)).astype(BF16)
-                copy("up_far", n, 0).start()
 
             return carry
 
         lax.fori_loop(0, blocks, step, 0)
-        near(n2_v.at[n], normed_ref.at[n])
-        near(hidden_v.at[n], hidden_ref.at[n])
-        near(both_v.at[n], both_ref.at[n])
+        near(ua_v.at[n], own_ref.at[n])
+        near(ux_v.at[n], far_ref.at[n])
 
     def back(n):
         for k in range(half):
@@ -959,7 +977,7 @@
         for k in range(half):
             arrived("grad_far", n, k)
             grad = da_v[n, k] + dg_v[n, k].astype(F32)
-            residual = res_v[n, k]
+            residual = res_ref[n, k]
             scale = rms_scale(residual)
             scaled = grad * gain
             grad_residual = (
@@ -975,27 +993,44 @@
                 gain_grad_ref[...] = part if n == 0 else gain_grad_ref[...] + part
                 da_v[n, 0] = grad_residual
                 near(da_v.at[n, 0], residual_ref.at[n])
-        copy("up_far", n, 0).wait_recv()
-        oc_v[n, 0] = (ua_v[n] + ug_v[n].astype(F32)).astype(BF16)
-        near(oc_v.at[n, 0], out_ref.at[n])
+
+    def weight_grads():
+        chunk = 2 * width // 8
+        flat = lambda value: value.reshape(-1, value.shape[-1])
+
+        def rows(left_v, right, out):
+            def step(m, carry):
+                cut = pl.ds(pl.multiple_of(m * chunk, chunk), chunk)
+                total = None
+                for n in range(sequences):
+                    term = t_dot(flat(left_v[n, :, :, cut]), flat(right[n]))
+                    total = term if total is None else total + term
+                out[cut, :] = total.astype(BF16)
+                return carry
+
+            lax.fori_loop(0, out.shape[0] // chunk, step, 0)
+
+        rows(hidden_v, g_ref, down_ref)
+        rows(n2_v, both_v, mlp_ref)
 
     for n in range(sequences):
         norm(n)
+    for n in range(sequences):
         feed(n)
-    for n in range(sequences):
+    for n in range(sequences - 1):
         back(n)
+    weight_grads()
+    back(sequences - 1)
     for n, k in pairs:
         arrived("branch", n, k)
     for n, k in pairs:
         for name in ("normed", "grad_core", "grad_far", "branch"):
             copy(name, n, k).wait_send()
-    for n in range(sequences):
-        copy("up_far", n, 0).wait_send()
     for made in near_copies:
         made.wait()
 
 
-def feed_forward(mixed, w_o, w_mlp, w_d, x_rel, g_rel, gain):
+def feed_forward(residual, w_mlp, w_d, g_rel, gain):
     sequences, blocks, piece, width = g_rel.shape
     half = blocks // 2
     units = w_d.shape[0]
@@ -1008,20 +1043,17 @@
         mlp_kernel,
         name="feed_forward",
         out_shape=(
+            shape((sequences, piece, width), F32),
             shape((sequences, piece, width), BF16),
             shape((sequences, piece, width), F32),
             shape((sequences, blocks, piece, width), BF16),
-            shape((sequences, blocks, piece, units), BF16),
-            shape((sequences, blocks, piece, 2 * units), BF16),
-            shape((sequences, blocks, piece, width), BF16),
+            shape((units, width), BF16),
+            shape((width, 2 * units), BF16),
             shape((1, width), F32),
         ),
-        in_specs=[vmem] * 4 + [hbm, vmem, vmem],
-        out_specs=[hbm] * 6 + [vmem],
+        in_specs=[vmem] * 5,
+        out_specs=[hbm] * 4 + [vmem] * 3,
         scratch_shapes=[
-            part(F32),
-            part(BF16),
-            part(BF16),
             part(BF16),
             part(BF16),
             pltpu.VMEM((sequences, blocks, piece, width), BF16),
@@ -1033,17 +1065,15 @@
             part(BF16),
             part(BF16),
             one(BF16),
-            one(BF16),
             one(F32),
             pltpu.SemaphoreType.DMA((16 * sequences,)),
             pltpu.SemaphoreType.DMA((16 * sequences,)),
             pltpu.SemaphoreType.DMA((16,)),
-            pltpu.SemaphoreType.DMA((sequences,)),
         ],
         compiler_params=pltpu.CompilerParams(
             collective_id=1, has_side_effects=True, vmem_limit_bytes=67043328
         ),
-    )(mixed, w_o, w_mlp, w_d, x_rel, g_rel, gain)
+    )(residual, w_mlp, w_d, g_rel, gain)
 
 
 class Scatter:
@@ -1104,8 +1134,8 @@
 
 def last_kernel(
     down_ref, mlp_ref, og_ref, branch_ref, wo_ref, qkv_ref, pre_ref, log_ref, w_ref, normed_ref,
-    x_ref, residual_ref, gain_ref, mlp_gain_ref, qg_ref, kg_ref, cos_ref, sin_ref,
-    tokens_ref, down_out, mlp_out, out_out, in_out, sums_ref,
+    x_ref, residual_ref, up_ref, gain_ref, mlp_gain_ref, qg_ref, kg_ref, cos_ref, sin_ref,
+    up_out, tokens_ref, down_out, mlp_out, out_out, in_out, sums_ref,
     d1, d2, c1, c2, c3, o1, o2, o3, a_v, a1, a2, a3,
     do_v, gr_v, dk_v, dv_v, core_s, core_r, far_s, far_r, acc_v, total_v, got_v,
     send, recv, local,
@@ -1181,6 +1211,8 @@
     links.greet((1, 2, 4), (1, 2, 3))
     upper = pltpu.make_async_copy(residual_ref, tokens_ref, local.at[0])
     upper.start()
+    up_slot = links.slots(1)
+    up_copy = links.start(up_ref, up_out, up_slot, seq=links.seq_at(2))
     mlp.start()
     down.start()
     pl.when(beside == 1)(out_z0.start)
@@ -1356,13 +1388,14 @@
     for k, copy in out_share.items():
         pl.when((across == k >> 1) & (beside == (k & 1)))(copy.wait_recv)
     mlp.end()
+    up_copy.wait_recv()
     for scatter in ins:
         scatter.end()
     links.finish()
 
 
 def last(
-    down, mlp, out, branch, w_o, qkv, pre, log_total, w_in, normed, x, residual,
+    down, mlp, out, branch, w_o, qkv, pre, log_total, w_in, normed, x, residual, up,
     gain, mlp_gain_grad, query_gain, key_gain, cosine, sine,
 ):
     sequences, blocks, piece, width = branch.shape
@@ -1375,11 +1408,13 @@
     shape = jax.ShapeDtypeStruct
     b16 = lambda *dims: pltpu.VMEM(dims, BF16)
     f32 = lambda *dims: pltpu.VMEM(dims, F32)
+    hbm = pl.BlockSpec(memory_space=pl.ANY)
     part = (blocks, rows, 4 * HEAD_SIZE)
     return pl.pallas_call(
         last_kernel,
         name="last",
         out_shape=(
+            shape(up.shape, up.dtype),
             shape((sequences, piece, width), F32),
             shape((down_rows, width), BF16),
             shape((blocks, rows, wide), BF16),
@@ -1387,8 +1422,8 @@
             shape((heads_kv,) + part, BF16),
             shape((24, 128), F32),
         ),
-        in_specs=[vmem] * 11 + [pl.BlockSpec(memory_space=pl.ANY)] + [vmem] * 6,
-        out_specs=[vmem] * 6,
+        in_specs=[vmem] * 11 + [hbm] * 2 + [vmem] * 6,
+        out_specs=[hbm] + [vmem] * 6,
         scratch_shapes=[
             b16(2, 2, down_rows, width),
             b16(2, down_rows, width),
@@ -1421,7 +1456,7 @@
             collective_id=2, has_side_effects=True, vmem_limit_bytes=67043328
         ),
     )(
-        down, mlp, out, branch, w_o, qkv, pre, log_total, w_in, normed, x, residual,
+        down, mlp, out, branch, w_o, qkv, pre, log_total, w_in, normed, x, residual, up,
         gain, mlp_gain_grad, query_gain, key_gain, cosine, sine,
     )
 
@@ -1481,7 +1516,7 @@
         gains = jnp.zeros((8, seq, width // count), F32)
         gains = lax.dynamic_update_slice(gains, own_gains.astype(F32)[:, None], (0, wires.s, 0))
         (
-            x_rel, g_rel, w_in, w_mlp, w_o, w_d, all_normed, all_qkv, all_pre, all_mixed, all_log, gains
+            x_rel, g_rel, w_in, w_mlp, w_o, w_d, all_normed, all_qkv, all_pre, all_mixed, residual, all_log, gains
         ) = first(
             package_in, package_mlp, w_out, w_down, hidden_in, cotangent, gains.reshape(8, -1),
             query_gain_row, key_gain_row, cosine, sine, dp, 2 * heads_kv // seq,
@@ -1489,9 +1524,9 @@
         w_in, w_mlp = w_in.reshape(width, -1), w_mlp.reshape(width, -1)
         w_o, w_d = w_o.reshape(-1, width), w_d.reshape(units, width)
         attn_gain_row, mlp_gain_row = gains[:1], gains[1:2]
-        (
-            all_out, all_grad_residual, all_normed_mlp, all_hidden, all_grad_both, all_branch, mlp_gain_grad
-        ) = feed_forward(all_mixed, w_o, w_mlp, w_d, x_rel, g_rel, mlp_gain_row)
+        up_own, up_far, all_grad_residual, all_branch, grad_down, grad_mlp, mlp_gain_grad = feed_forward(
+            residual, w_mlp, w_d, g_rel, mlp_gain_row
+        )
     else:
         gains = jnp.zeros((2, count, width // count), BF16)
         gains = lax.dynamic_update_slice(gains, own_gains[:, None], (0, index, 0))
@@ -1582,20 +1617,18 @@
 
     if fused:
         flat = lambda value: value.reshape(sequences * length, -1)
-        grad_mlp = t_dot(flat(all_normed_mlp), flat(all_grad_both)).astype(BF16)
-        grad_down = t_dot(flat(all_hidden), flat(g_rel)).astype(BF16)
         grad_out = t_dot(flat(all_mixed), flat(all_branch)).astype(BF16)
-        grad_tokens, grad_down, grad_mlp, grad_out, grad_in, gain_sums = last(
+        up, grad_tokens, grad_down, grad_mlp, grad_out, grad_in, gain_sums = last(
             grad_down.reshape(2, 2, 2, down_rows, width),
             grad_mlp.reshape(2, 2, 2, seq, rows, -1),
             grad_out.reshape(2, seq, -1, width),
-            all_branch, w_o, all_qkv, all_pre, all_log, w_in, all_normed, hidden_in, all_grad_residual,
+            all_branch, w_o, all_qkv, all_pre, all_log, w_in, all_normed, hidden_in, all_grad_residual, up_far,
             attn_gain_row, mlp_gain_grad, query_gain_row, key_gain_row, cosine, sine,
         )
         grad_down, grad_mlp, grad_out = grad_down.astype(F32), grad_mlp.astype(F32), grad_out.astype(F32)
         grad_in = grad_in.astype(F32).transpose(1, 2, 0, 3).reshape(seq, rows, -1)
         gain_sums = gain_sums.reshape(-1)[: 2 * width + 2 * HEAD_SIZE]
-        hidden_out = all_out
+        hidden_out = (up_own + up.astype(F32)).astype(BF16)
     else:
         def over(name):
             return jnp.concatenate([k[name] for k in kept], axis=0)

time: 408 us -> 365 us (0.89)
  Pallas kernels: 354 us -> 329 us
  matrix products: 19.4 us -> 6.14 us
  local copies, waits for them, and re-layouts: 18.4 us -> 12.7 us
    pallas_call x1, Pallas kernels: 125 us -> 70.6 us  [feed_forward(): pl.pallas_call(mlp_kernel, name='feed_forward', out_shape=(shape((sequenc...]
    pallas_call x1, Pallas kernels: 103 us -> 133 us  [first(): pl.pallas_call(functools.partial(first_kernel, heads), name='first', out_...]
    dot_general x3 -> x1, matrix products: 19.4 us -> 6.14 us  [t_dot(): lax.dot_general(a, b, (((0,), (0,)), ((), ())), preferred_element_type=F32)]
where the time goes in v5:
time: 365 us; the launch traced here: 361 us
  Pallas kernels  329 us (90%)
  local copies, waits for them, and re-layouts  12.7 us (3%)
  other arithmetic  11.5 us (3%)
  matrix products  6.14 us (2%)
    pallas_call x1, Pallas kernels, first(): pl.pallas_call(functools.partial(first_kernel, heads), name='first', out_...  133 us
    pallas_call x1, Pallas kernels, last(): pl.pallas_call(last_kernel, name='last', out_shape=(shape(up.shape, up.dt...  125 us
    pallas_call x1, Pallas kernels, feed_forward(): pl.pallas_call(mlp_kernel, name='feed_forward', out_shape=(shape((sequenc...  70.6 us

profile of v5, /device:TPU:0, one launch (start us, length us, event | category | flops | bytes accessed | tf_op | source)
XLA Modules:
  0.0 361.1 jit_solution(16973365409129981529)
XLA Ops:
  0.6 0.0 copy-start.4
  0.7 0.0 copy-start.3
  0.7 0.8 maximum_convert_fusion
  1.5 1.2 bitcast_convert_fusion.1
  2.7 0.7 reshape.155.gains_ref
  3.4 0.9 bitcast_dynamic-update-slice_fusion
  4.3 0.9 bitcast_dynamic-update-slice_fusion.2
  5.2 0.9 bitcast_dynamic-update-slice_fusion.1
  6.1 0.7 pad_maximum_fusion.3.a_ref
  6.8 0.0 copy-done.3
  6.8 0.3 reshape.151
  7.1 0.2 reshape.152
  7.4 0.0 copy-done.4
  7.4 0.3 reshape.153
  7.7 0.2 reshape.154
  7.9 0.8 pad_maximum_fusion.2.c_ref
  8.7 1.9 fusion
  10.6 1.3 pad_maximum_fusion
  11.9 133.4 %first.1 = (bf16[2,4,256,1024]{3,2,1,0:T(8,128)(2,1)}, bf16[2,4,256,1024]{3,2,1,0:T(8,128)(2,1)}, bf16[8,4,32,1024]{3,2,1,0:T(8,128)(2,1)}, bf16[8,4,32,1536]{3,...) custom-call(bf16[4,32,1024]{2,1,0:T(8,128)(2,1)} %pad_maximum_fusion, ...), custom_call_target="tpu_custom_call" | custom-call | tf_op jit(solution)/shard_map/first/pallas_call | solution.py:825
  145.3 1.4 fusion.2
  146.8 70.6 %feed_forward.1 = (f32[2,256,1024]{2,1,0:T(8,128)}, bf16[2,256,1024]{2,1,0:T(8,128)(2,1)}, f32[2,256,1024]{2,1,0:T(8,128)}, bf16[2,4,256,1024]{3,2,1,0:T(8,128)(...) custom-call(f32[2,2,256,1024]{3,2,1,0:T(8,128)} %get-tuple-element.39.res_ref, ...), custom_call_target="tpu_custom_call" | custom-call | tf_op jit(solution)/shard_map/feed_forward/pallas_call | solution.py:1042
  217.4 6.1 %bitcast_convert_fusion = bf16[512,1024]{1,0:T(8,128)(2,1)} fusion(bf16[2,4,256,512]{3,2,1,0:T(8,128)(2,1)} %get-tuple-element.47, bf16[2,4,256,1024]{3,2,1,0:T(8,128)(2,1)} %get-tuple-element.48.branch_ref), kind=kOutput, calls=%fused_computation | convolution fusion | flops 2148007936 | bytes 7340032 | tf_op jit(solution)/shard_map/dot_general | solution.py:203
  223.5 125.4 %last.1 = (bf16[2,256,1024]{2,1,0:T(8,128)(2,1)}, f32[2,256,1024]{2,1,0:T(8,128)}, bf16[96,1024]{1,0:T(8,128)(2,1)}, bf16[4,32,1536]{2,1,0:T(8,128)(2,1)}, bf16[...) custom-call(bf16[2,2,2,96,1024]{4,3,2,1,0:T(8,128)(2,1)} %bitcast.102, ...), custom_call_target="tpu_custom_call" | custom-call | tf_op jit(solution)/shard_map/last/pallas_call | solution.py:1413
  348.9 0.0 copy-start.7
  348.9 0.0 copy-start.6
  349.0 0.0 copy-start.5
  349.0 0.0 copy-start.2
  349.0 3.2 add_convert_fusion
  352.2 0.0 copy-done.7
  352.2 0.5 slice_bitcast_fusion.17
  352.7 0.6 fusion.3
  353.3 0.0 copy-done.6
  353.3 0.7 convert_element_type.63
  354.1 0.0 copy-done.5
  354.1 0.8 convert_element_type.65
  354.8 0.0 copy-done.2
  354.8 0.0 copy-start.1
  355.1 0.0 copy-start.8
  355.2 0.0 copy-start.9
  355.2 0.0 copy-start.10
  355.2 0.6 copy-done.1
  355.8 0.1 fusion.1
  355.9 0.0 copy-done.8
  355.9 0.0 copy-done.9
  355.9 0.0 copy-done.10
  355.9 0.3 reshape.171
  356.2 0.3 copy.39
  356.5 0.0 copy-start
  356.5 1.2 reshape.172
  357.7 0.3 reshape.169
  358.0 0.3 copy.38
  358.3 1.2 reshape.170
  359.5 0.0 copy-done
  359.5 1.3 copy.78
  (29 shorter events, 0.4 us)
Async XLA Ops:
  0.6 6.7 %copy-start.4 = (bf16[32,3072]{1,0:T(8,128)(2,1)S(1)}, bf16[32,3072]{1,0:T(8,128)(2,1)}, u32[]{:S(2)}) copy-start(bf16[32,3072]{1,0:T(8,128)(2,1)} %param.23) | copy-start | bytes 589828
  0.7 6.2 %copy-start.3 = (bf16[32,3072]{1,0:T(8,128)(2,1)S(1)}, bf16[32,3072]{1,0:T(8,128)(2,1)}, u32[]{:S(2)}) copy-start(bf16[32,3072]{1,0:T(8,128)(2,1)} %param.22) | copy-start | bytes 589828
  348.9 3.3 copy-start.7
  348.9 4.4 %copy-start.6 = (bf16[64,1024]{1,0:T(8,128)(2,1)S(1)}, bf16[64,1024]{1,0:T(8,128)(2,1)}, u32[]{:S(2)}) copy-start(bf16[64,1024]{1,0:T(8,128)(2,1)} %get-tuple-element.62) | copy-start | bytes 393220
  349.0 5.1 %copy-start.5 = (bf16[96,1024]{1,0:T(8,128)(2,1)S(1)}, bf16[96,1024]{1,0:T(8,128)(2,1)}, u32[]{:S(2)}) copy-start(bf16[96,1024]{1,0:T(8,128)(2,1)} %get-tuple-element.64) | copy-start | bytes 589828
  349.0 5.9 %copy-start.2 = (bf16[2,4,32,512]{3,2,1,0:T(8,128)(2,1)S(1)}, bf16[2,4,32,512]{3,2,1,0:T(8,128)(2,1)}, u32[]{:S(2)}) copy-start(bf16[2,4,32,512]{3,2,1,0:T(8,128)(2,1)} %get-tuple-element.61) | copy-start | bytes 786436
  354.8 1.0 copy-start.1
  355.1 0.8 copy-start.8
  355.2 0.7 copy-start.9
  355.2 0.7 copy-start.10
  356.5 3.0 copy-start

commit v6 on v5

--- a/solution.py
+++ b/solution.py
@@ -557,7 +557,7 @@
 def first_kernel(
     heads,
     a_ref, c_ref, out_ref, down_ref, x_ref, g_ref, gains_ref, qg_ref, kg_ref, cos_ref, sin_ref,
-    xr_ref, gr_ref, wa_ref, wc_ref, wo_ref, wd_ref, n_ref, qkv_ref, pre_ref, o_ref, residual_ref, log_ref, gain_ref,
+    xr_ref, gr_ref, wa_ref, wc_ref, wo_ref, wd_ref, n_ref, qkv_ref, pre_ref, o_ref, residual_ref, far_ref, log_ref, gain_ref,
     w_v, x_v, n_v, qkv_v, pre_v, o_v, got_v, wo_v, res_v, core_s, core_r, far_s, far_r, send, recv, local,
 ):
     links = Links(send, recv)
@@ -749,7 +749,7 @@
     }
     far_copies = {
         (n, k): links.plan(far_s.at[n, k], far_r.at[n, half - 1 - k], far_slots + half * n + k, seq=links.seq_at(2))
-        for n in range(sequences)
+        for n in range(sequences - 1)
         for k in range(half)
     }
 
@@ -775,7 +775,8 @@
                     total = part + core_r[n, k].astype(F32)
                     res_v[n, k] = total
                     far_s[n, k] = total.astype(BF16)
-                    far_copies[n, k].start()
+                    if n < sequences - 1:
+                        far_copies[n, k].start()
 
             return carry
 
@@ -783,9 +784,14 @@
 
     def residual(n):
         for k in range(half):
-            far_copies[n, half - 1 - k].wait_recv()
-            res_v[n, k] = res_v[n, k] + far_r[n, k].astype(F32) + x_v[n, k].astype(F32)
+            if n < sequences - 1:
+                far_copies[n, half - 1 - k].wait_recv()
+                res_v[n, k] = res_v[n, k] + far_r[n, k].astype(F32) + x_v[n, k].astype(F32)
+            else:
+                res_v[n, k] = res_v[n, k] + x_v[n, k].astype(F32)
         near(f"res{n}", res_v.at[n], residual_ref.at[n])
+        if n == sequences - 1:
+            near("far", far_s.at[n], far_ref)
 
     nothing = lambda: None
     project_part(0, [nothing, lambda: gather_c.relay(2), lambda: pass_on(x_copies[1]), out_last])
@@ -810,6 +816,7 @@
     for n in range(sequences):
         for name in ("g", "n", "qkv", "pre", "o", "res"):
             locals_[f"{name}{n}"].wait()
+    locals_["far"].wait()
     links.finish()
 
 
@@ -837,11 +844,12 @@
             shape((sequences, length, pre_columns), F32),
             shape((sequences, blocks, piece, heads * HEAD_SIZE), BF16),
             shape((sequences, blocks // 2, piece, width), F32),
+            shape((blocks // 2, piece, width), BF16),
             shape((sequences, heads, 1, length), F32),
             shape((8, width), F32),
         ),
         in_specs=[vmem] * 11,
-        out_specs=[hbm] * 11 + [vmem] * 2,
+        out_specs=[hbm] * 12 + [vmem] * 2,
         scratch_shapes=[
             pltpu.VMEM((dp, blocks, rows, columns), BF16),
             pltpu.VMEM((sequences, blocks, piece, width), BF16),
@@ -867,9 +875,9 @@
 
 
 def mlp_kernel(
-    res_ref, wc_ref, wd_ref, g_ref, gain_ref,
+    res_ref, last_ref, wc_ref, wd_ref, g_ref, gain_ref,
     own_ref, far_ref, residual_ref, branch_ref, down_ref, mlp_ref, gain_grad_ref,
-    core_s, x_s, n2_v, hidden_v, both_v, dc_v, dg_v, da_v, us_v, uc_v, ux_v, ua_v,
+    res_v, last_v, core_s, x_s, n2_v, hidden_v, both_v, dc_v, dg_v, da_v, us_v, uc_v, ux_v, ua_v,
     send, recv, local,
 ):
     links = Links(send, recv)
@@ -904,12 +912,25 @@
         made.start()
         near_copies.append(made)
 
+    last_slots = links.slots(half)
+    last_copies = [
+        links.plan(last_ref.at[k], last_v.at[half - 1 - k], last_slots + k, **far) for k in range(half)
+    ]
+
     links.greet((), (1, 2))
+    for made in last_copies:
+        made.start()
     gain = gain_ref[...]
+
+    def residual_of(n, k):
+        return res_ref[n, k] if n < sequences - 1 else res_v[k]
 
     def norm(n):
         for k in range(half):
-            residual = res_ref[n, k]
+            if n == sequences - 1:
+                last_copies[half - 1 - k].wait_recv()
+                res_v[k] = res_ref[n, k] + last_v[k].astype(F32)
+            residual = residual_of(n, k)
             n2_v[n, k] = (residual * rms_scale(residual) * gain).astype(BF16)
             copy("normed", n, k).start()
 
@@ -959,7 +980,7 @@
 
             @pl.when(i == half)
             def _():
-                ua_v[n] = res_ref[n, 0] + (up + uc_v[n, 0].astype(F32))
+                ua_v[n] = residual_of(n, 0) + (up + uc_v[n, 0].astype(F32))
 
             @pl.when(i == half + 1)
             def _():
@@ -977,7 +998,7 @@
         for k in range(half):
             arrived("grad_far", n, k)
             grad = da_v[n, k] + dg_v[n, k].astype(F32)
-            residual = res_ref[n, k]
+            residual = residual_of(n, k)
             scale = rms_scale(residual)
             scaled = grad * gain
             grad_residual = (
@@ -1015,7 +1036,6 @@
 
     for n in range(sequences):
         norm(n)
-    for n in range(sequences):
         feed(n)
     for n in range(sequences - 1):
         back(n)
@@ -1026,11 +1046,12 @@
     for n, k in pairs:
         for name in ("normed", "grad_core", "grad_far", "branch"):
             copy(name, n, k).wait_send()
+    links.finish()
     for made in near_copies:
         made.wait()
 
 
-def feed_forward(residual, w_mlp, w_d, g_rel, gain):
+def feed_forward(residual, last_far, w_mlp, w_d, g_rel, gain):
     sequences, blocks, piece, width = g_rel.shape
     half = blocks // 2
     units = w_d.shape[0]
@@ -1051,9 +1072,11 @@
             shape((width, 2 * units), BF16),
             shape((1, width), F32),
         ),
-        in_specs=[vmem] * 5,
+        in_specs=[vmem] * 6,
         out_specs=[hbm] * 4 + [vmem] * 3,
         scratch_shapes=[
+            pltpu.VMEM((half, piece, width), F32),
+            pltpu.VMEM((half, piece, width), BF16),
             part(BF16),
             part(BF16),
             pltpu.VMEM((sequences, blocks, piece, width), BF16),
@@ -1073,7 +1096,7 @@
         compiler_params=pltpu.CompilerParams(
             collective_id=1, has_side_effects=True, vmem_limit_bytes=67043328
         ),
-    )(residual, w_mlp, w_d, g_rel, gain)
+    )(residual, last_far, w_mlp, w_d, g_rel, gain)
 
 
 class Scatter:
@@ -1133,16 +1156,16 @@
 
 
 def last_kernel(
-    down_ref, mlp_ref, og_ref, branch_ref, wo_ref, qkv_ref, pre_ref, log_ref, w_ref, normed_ref,
+    down_ref, mlp_ref, mixed_h, branch_h, wo_ref, qkv_h, pre_h, log_ref, w_h, normed_h,
     x_ref, residual_ref, up_ref, gain_ref, mlp_gain_ref, qg_ref, kg_ref, cos_ref, sin_ref,
     up_out, tokens_ref, down_out, mlp_out, out_out, in_out, sums_ref,
-    d1, d2, c1, c2, c3, o1, o2, o3, a_v, a1, a2, a3,
+    rows_v, mixed_ref, qkv_ref, pre_ref, w_ref, og_ref, d1, d2, c1, c2, c3, o1, o2, o3, a_v, a1, a2, a3,
     do_v, gr_v, dk_v, dv_v, core_s, core_r, far_s, far_r, acc_v, total_v, got_v,
     send, recv, local,
 ):
     links = Links(send, recv)
     d, s = links.d, links.s
-    sequences, blocks, piece, width = branch_ref.shape
+    sequences, blocks, piece, width = rows_v.shape
     half = blocks // 2
     heads = log_ref.shape[1]
     heads_kv = heads // 2
@@ -1209,23 +1232,53 @@
             out_out[...] = o3[s]
 
     links.greet((1, 2, 4), (1, 2, 3))
-    upper = pltpu.make_async_copy(residual_ref, tokens_ref, local.at[0])
-    upper.start()
+    loads = {
+        name: pltpu.make_async_copy(src, dst, local.at[k])
+        for k, (name, src, dst) in enumerate(
+            (
+                ("mixed", mixed_h, mixed_ref),
+                ("branch", branch_h, rows_v),
+                ("qkv", qkv_h, qkv_ref),
+                ("pre", pre_h, pre_ref),
+                ("w", w_h, w_ref),
+                ("residual", residual_ref, tokens_ref),
+                ("normed", normed_h, rows_v),
+            )
+        )
+    }
+    for name in ("mixed", "branch", "qkv", "pre", "w", "residual"):
+        loads[name].start()
     up_slot = links.slots(1)
     up_copy = links.start(up_ref, up_out, up_slot, seq=links.seq_at(2))
     mlp.start()
     down.start()
-    pl.when(beside == 1)(out_z0.start)
     total_v[0] = jnp.zeros_like(total_v[0])
     for r in range(width // 128):
         total_v[0, 8 + r : 9 + r, :] = mlp_gain_ref[:, r * 128 : (r + 1) * 128]
 
+    def weight_out(h, carry):
+        cut = pl.ds(pl.multiple_of(h * 2 * HEAD_SIZE, 2 * HEAD_SIZE), 2 * HEAD_SIZE)
+        total = None
+        for n in range(sequences):
+            term = t_dot(
+                mixed_ref[n, :, :, cut].reshape(blocks * piece, 2 * HEAD_SIZE),
+                rows_v[n].reshape(blocks * piece, width),
+            )
+            total = term if total is None else total + term
+        og_ref[h] = total.astype(BF16).reshape(og_ref.shape[1:])
+        return carry
+
     def mixed_back(i, carry):
         n, b = lax.div(i, blocks), lax.rem(i, blocks)
-        do_v[n, b] = dot_t(branch_ref[n, b], wo_ref[...]).astype(BF16)
+        do_v[n, b] = dot_t(rows_v[n, b], wo_ref[...]).astype(BF16)
         return carry
 
+    loads["mixed"].wait()
+    loads["branch"].wait()
+    lax.fori_loop(0, heads_kv, weight_out, 0)
+    pl.when(beside == 1)(out_z0.start)
     lax.fori_loop(0, sequences * blocks, mixed_back, 0)
+    loads["normed"].start()
 
     slots = [links.slots(half * sequences), links.slots(sequences)]
     core_copies = {
@@ -1334,7 +1387,7 @@
             cut = pl.ds(pl.multiple_of(m * chunk, chunk), chunk)
             total = None
             for n in range(sequences):
-                left = normed_ref[n, :, :, cut].reshape(blocks * piece, chunk)
+                left = rows_v[n, :, :, cut].reshape(blocks * piece, chunk)
                 right = gr_v[n, :, :, j * wide : (j + 1) * wide].reshape(blocks * piece, wide)
                 term = t_dot(left, right)
                 total = term if total is None else total + term
@@ -1344,14 +1397,18 @@
         lax.fori_loop(0, width // chunk, step, 0)
         ins[j].start()
 
+    loads["qkv"].wait()
+    loads["pre"].wait()
     attention(0, [nothing, nothing, out_sum_z0])
+    loads["normed"].wait()
+    loads["w"].wait()
     weight_in(0)
     attention(1, [out_sum_z1, mlp.sum_y, lambda: input_part(0)])
     input_part(1)
     weight_in(1)
     down.sum_y()
     mlp.sum_z0()
-    upper.wait()
+    loads["residual"].wait()
     for n in range(sequences):
         input_end(n)
 
@@ -1395,15 +1452,15 @@
 
 
 def last(
-    down, mlp, out, branch, w_o, qkv, pre, log_total, w_in, normed, x, residual, up,
+    down, mlp, mixed, branch, w_o, qkv, pre, log_total, w_in, normed, x, residual, up,
     gain, mlp_gain_grad, query_gain, key_gain, cosine, sine,
 ):
     sequences, blocks, piece, width = branch.shape
     length = blocks * piece
     rows, wide = mlp.shape[-2], mlp.shape[-1]
     down_rows = down.shape[-2]
-    out_rows = out.shape[-2]
     heads_kv = qkv.shape[-1] // (4 * HEAD_SIZE)
+    out_rows = w_o.shape[0] // (heads_kv * blocks)
     vmem = pl.BlockSpec(memory_space=pltpu.VMEM)
     shape = jax.ShapeDtypeStruct
     b16 = lambda *dims: pltpu.VMEM(dims, BF16)
@@ -1422,9 +1479,15 @@
             shape((heads_kv,) + part, BF16),
             shape((24, 128), F32),
         ),
-        in_specs=[vmem] * 11 + [hbm] * 2 + [vmem] * 6,
+        in_specs=[vmem] * 2 + [hbm] * 2 + [vmem] + [hbm] * 2 + [vmem] + [hbm] * 2 + [vmem] + [hbm] * 2 + [vmem] * 6,
         out_specs=[hbm] + [vmem] * 6,
         scratch_shapes=[
+            b16(*normed.shape),
+            b16(*mixed.shape),
+            b16(*qkv.shape),
+            f32(*pre.shape),
+            b16(*w_in.shape),
+            b16(heads_kv, blocks, out_rows, width),
             b16(2, 2, down_rows, width),
             b16(2, down_rows, width),
             b16(2, 2, blocks, rows, wide),
@@ -1450,13 +1513,13 @@
             f32(5, 24, 128),
             pltpu.SemaphoreType.DMA((64,)),
             pltpu.SemaphoreType.DMA((64,)),
-            pltpu.SemaphoreType.DMA((1,)),
+            pltpu.SemaphoreType.DMA((8,)),
         ],
         compiler_params=pltpu.CompilerParams(
             collective_id=2, has_side_effects=True, vmem_limit_bytes=67043328
         ),
     )(
-        down, mlp, out, branch, w_o, qkv, pre, log_total, w_in, normed, x, residual, up,
+        down, mlp, mixed, branch, w_o, qkv, pre, log_total, w_in, normed, x, residual, up,
         gain, mlp_gain_grad, query_gain, key_gain, cosine, sine,
     )
 
@@ -1516,7 +1579,7 @@
         gains = jnp.zeros((8, seq, width // count), F32)
         gains = lax.dynamic_update_slice(gains, own_gains.astype(F32)[:, None], (0, wires.s, 0))
         (
-            x_rel, g_rel, w_in, w_mlp, w_o, w_d, all_normed, all_qkv, all_pre, all_mixed, residual, all_log, gains
+            x_rel, g_rel, w_in, w_mlp, w_o, w_d, all_normed, all_qkv, all_pre, all_mixed, residual, residual_far, all_log, gains
         ) = first(
             package_in, package_mlp, w_out, w_down, hidden_in, cotangent, gains.reshape(8, -1),
             query_gain_row, key_gain_row, cosine, sine, dp, 2 * heads_kv // seq,
@@ -1525,7 +1588,7 @@
         w_o, w_d = w_o.reshape(-1, width), w_d.reshape(units, width)
         attn_gain_row, mlp_gain_row = gains[:1], gains[1:2]
         up_own, up_far, all_grad_residual, all_branch, grad_down, grad_mlp, mlp_gain_grad = feed_forward(
-            residual, w_mlp, w_d, g_rel, mlp_gain_row
+            residual, residual_far, w_mlp, w_d, g_rel, mlp_gain_row
         )
     else:
         gains = jnp.zeros((2, count, width // count), BF16)
@@ -1616,13 +1679,10 @@
         return g.reshape(seq, rows, dp, down_rows).transpose(1, 2, 0, 3).reshape(rows, -1)
 
     if fused:
-        flat = lambda value: value.reshape(sequences * length, -1)
-        grad_out = t_dot(flat(all_mixed), flat(all_branch)).astype(BF16)
         up, grad_tokens, grad_down, grad_mlp, grad_out, grad_in, gain_sums = last(
             grad_down.reshape(2, 2, 2, down_rows, width),
             grad_mlp.reshape(2, 2, 2, seq, rows, -1),
-            grad_out.reshape(2, seq, -1, width),
-            all_branch, w_o, all_qkv, all_pre, all_log, w_in, all_normed, hidden_in, all_grad_residual, up_far,
+            all_mixed, all_branch, w_o, all_qkv, all_pre, all_log, w_in, all_normed, hidden_in, all_grad_residual, up_far,
             attn_gain_row, mlp_gain_grad, query_gain_row, key_gain_row, cosine, sine,
         )
         grad_down, grad_mlp, grad_out = grad_down.astype(F32), grad_mlp.astype(F32), grad_out.astype(F32)

time: 365 us -> 346 us (0.948)
  Pallas kernels: 329 us -> 317 us
  matrix products: 6.14 us -> 0 us
    pallas_call x1, Pallas kernels: 133 us -> 118 us  [first(): pl.pallas_call(functools.partial(first_kernel, heads), name='first', out_...]
    pallas_call x1, Pallas kernels: 70.6 us -> 80.8 us  [feed_forward(): pl.pallas_call(mlp_kernel, name='feed_forward', out_shape=(shape((sequenc...]
    pallas_call x1, Pallas kernels: 125 us -> 118 us  [last(): pl.pallas_call(last_kernel, name='last', out_shape=(shape(up.shape, up.dt...]
    dot_general x1 -> x0, matrix products: 6.14 us -> none  [t_dot(): lax.dot_general(a, b, (((0,), (0,)), ((), ())), preferred_element_type=F32)]
where the time goes in v6:
time: 346 us; the launch traced here: 342 us
  Pallas kernels  317 us (92%)
  local copies, waits for them, and re-layouts  12.7 us (4%)
  other arithmetic  11.5 us (3%)
    pallas_call x1, Pallas kernels, last(): pl.pallas_call(last_kernel, name='last', out_shape=(shape(up.shape, up.dt...  118 us
    pallas_call x1, Pallas kernels, first(): pl.pallas_call(functools.partial(first_kernel, heads), name='first', out_...  118 us
    pallas_call x1, Pallas kernels, feed_forward(): pl.pallas_call(mlp_kernel, name='feed_forward', out_shape=(shape((sequenc...  80.8 us

profile of v6, /device:TPU:0, one launch (start us, length us, event | category | flops | bytes accessed | tf_op | source)
XLA Modules:
  0.0 342.3 jit_solution(10984553900723387599)
XLA Ops:
  0.6 0.0 copy-start.4
  0.7 0.0 copy-start.3
  0.7 0.8 maximum_convert_fusion
  1.5 1.2 bitcast_convert_fusion
  2.7 0.7 reshape.150.gains_ref
  3.4 0.9 bitcast_dynamic-update-slice_fusion
  4.3 0.9 bitcast_dynamic-update-slice_fusion.2
  5.2 0.9 bitcast_dynamic-update-slice_fusion.1
  6.1 0.7 pad_maximum_fusion.3.a_ref
  6.8 0.0 copy-done.3
  6.8 0.3 reshape.146
  7.1 0.2 reshape.147
  7.4 0.0 copy-done.4
  7.4 0.3 reshape.148
  7.7 0.2 reshape.149
  7.9 0.8 pad_maximum_fusion.2.c_ref
  8.7 1.9 fusion
  10.6 1.3 pad_maximum_fusion
  11.9 117.9 %first.1 = (bf16[2,4,256,1024]{3,2,1,0:T(8,128)(2,1)}, bf16[2,4,256,1024]{3,2,1,0:T(8,128)(2,1)}, bf16[8,4,32,1024]{3,2,1,0:T(8,128)(2,1)}, bf16[8,4,32,1536]{3,...) custom-call(bf16[4,32,1024]{2,1,0:T(8,128)(2,1)} %pad_maximum_fusion, ...), custom_call_target="tpu_custom_call" | custom-call | tf_op jit(solution)/shard_map/first/pallas_call | solution.py:832
  129.7 1.4 fusion.2
  131.2 80.8 %feed_forward.1 = (f32[2,256,1024]{2,1,0:T(8,128)}, bf16[2,256,1024]{2,1,0:T(8,128)(2,1)}, f32[2,256,1024]{2,1,0:T(8,128)}, bf16[2,4,256,1024]{3,2,1,0:T(8,128)(...) custom-call(f32[2,2,256,1024]{3,2,1,0:T(8,128)} %get-tuple-element.40.res_ref, ...), custom_call_target="tpu_custom_call" | custom-call | tf_op jit(solution)/shard_map/feed_forward/pallas_call | solution.py:1063
  212.0 118.1 %last.1 = (bf16[2,256,1024]{2,1,0:T(8,128)(2,1)}, f32[2,256,1024]{2,1,0:T(8,128)}, bf16[96,1024]{1,0:T(8,128)(2,1)}, bf16[4,32,1536]{2,1,0:T(8,128)(2,1)}, bf16[...) custom-call(bf16[2,2,2,96,1024]{4,3,2,1,0:T(8,128)(2,1)} %bitcast.95, ...), custom_call_target="tpu_custom_call" | custom-call | tf_op jit(solution)/shard_map/last/pallas_call | solution.py:1470
  330.1 0.0 copy-start.7
  330.1 0.0 copy-start.6
  330.1 0.0 copy-start.5
  330.2 0.0 copy-start.2
  330.2 3.2 add_convert_fusion
  333.4 0.0 copy-done.7
  333.4 0.5 slice_bitcast_fusion.17
  333.9 0.6 fusion.3
  334.5 0.0 copy-done.6
  334.5 0.7 convert_element_type.59
  335.2 0.0 copy-done.5
  335.2 0.8 convert_element_type.61
  336.0 0.0 copy-done.2
  336.0 0.0 copy-start.1
  336.3 0.0 copy-start.8
  336.4 0.0 copy-start.9
  336.4 0.0 copy-start.10
  336.4 0.6 copy-done.1
  337.0 0.1 fusion.1
  337.1 0.0 copy-done.8
  337.1 0.0 copy-done.9
  337.1 0.0 copy-done.10
  337.1 0.3 reshape.165
  337.4 0.3 copy.37
  337.7 0.0 copy-start
  337.7 1.2 reshape.166
  338.9 0.3 reshape.163
  339.2 0.3 copy.36
  339.5 1.2 reshape.164
  340.7 0.0 copy-done
  340.7 1.3 copy.74
  (29 shorter events, 0.4 us)
Async XLA Ops:
  0.6 6.7 %copy-start.4 = (bf16[32,3072]{1,0:T(8,128)(2,1)S(1)}, bf16[32,3072]{1,0:T(8,128)(2,1)}, u32[]{:S(2)}) copy-start(bf16[32,3072]{1,0:T(8,128)(2,1)} %param.23) | copy-start | bytes 589828
  0.7 6.2 %copy-start.3 = (bf16[32,3072]{1,0:T(8,128)(2,1)S(1)}, bf16[32,3072]{1,0:T(8,128)(2,1)}, u32[]{:S(2)}) copy-start(bf16[32,3072]{1,0:T(8,128)(2,1)} %param.22) | copy-start | bytes 589828
  330.1 3.3 copy-start.7
  330.1 4.4 %copy-start.6 = (bf16[64,1024]{1,0:T(8,128)(2,1)S(1)}, bf16[64,1024]{1,0:T(8,128)(2,1)}, u32[]{:S(2)}) copy-start(bf16[64,1024]{1,0:T(8,128)(2,1)} %get-tuple-element.64) | copy-start | bytes 393220
  330.1 5.1 %copy-start.5 = (bf16[96,1024]{1,0:T(8,128)(2,1)S(1)}, bf16[96,1024]{1,0:T(8,128)(2,1)}, u32[]{:S(2)}) copy-start(bf16[96,1024]{1,0:T(8,128)(2,1)} %get-tuple-element.66) | copy-start | bytes 589828
  330.2 5.9 %copy-start.2 = (bf16[2,4,32,512]{3,2,1,0:T(8,128)(2,1)S(1)}, bf16[2,4,32,512]{3,2,1,0:T(8,128)(2,1)}, u32[]{:S(2)}) copy-start(bf16[2,4,32,512]{3,2,1,0:T(8,128)(2,1)} %get-tuple-element.63) | copy-start | bytes 786436
  336.0 1.0 copy-start.1
  336.3 0.8 copy-start.8
  336.4 0.7 copy-start.9
  336.4 0.7 copy-start.10
  337.7 3.0 copy-start

commit v7 on v6

--- a/solution.py
+++ b/solution.py
@@ -540,7 +540,7 @@
         self.copies[r].wait_recv()
 
     def first(self):
-        for mask in (4, 2, 1):
+        for mask in (2, 4, 1):
             self.copies[mask].start()
 
     def relay(self, r):

time: 346 us -> 347 us (level)
  no operation moved by 1% of the time
where the time goes in v7:
time: 347 us; the launch traced here: 343 us
  Pallas kernels  317 us (91%)
  local copies, waits for them, and re-layouts  12.7 us (4%)
  other arithmetic  11.5 us (3%)
    pallas_call x1, Pallas kernels, last(): pl.pallas_call(last_kernel, name='last', out_shape=(shape(up.shape, up.dt...  118 us
    pallas_call x1, Pallas kernels, first(): pl.pallas_call(functools.partial(first_kernel, heads), name='first', out_...  118 us
    pallas_call x1, Pallas kernels, feed_forward(): pl.pallas_call(mlp_kernel, name='feed_forward', out_shape=(shape((sequenc...  81.2 us

profile of v7, /device:TPU:0, one launch (start us, length us, event | category | flops | bytes accessed | tf_op | source)
XLA Modules:
  0.0 342.7 jit_solution(6310130146186490807)
XLA Ops:
  0.6 0.0 copy-start.4
  0.7 0.0 copy-start.3
  0.7 0.8 maximum_convert_fusion
  1.5 1.2 bitcast_convert_fusion
  2.7 0.7 reshape.150.gains_ref
  3.4 0.9 bitcast_dynamic-update-slice_fusion
  4.3 0.9 bitcast_dynamic-update-slice_fusion.2
  5.2 0.9 bitcast_dynamic-update-slice_fusion.1
  6.1 0.7 pad_maximum_fusion.3.a_ref
  6.8 0.0 copy-done.3
  6.8 0.3 reshape.146
  7.1 0.2 reshape.147
  7.4 0.0 copy-done.4
  7.4 0.3 reshape.148
  7.7 0.2 reshape.149
  7.9 0.8 pad_maximum_fusion.2.c_ref
  8.7 1.9 fusion
  10.6 1.3 pad_maximum_fusion
  11.9 118.0 %first.1 = (bf16[2,4,256,1024]{3,2,1,0:T(8,128)(2,1)}, bf16[2,4,256,1024]{3,2,1,0:T(8,128)(2,1)}, bf16[8,4,32,1024]{3,2,1,0:T(8,128)(2,1)}, bf16[8,4,32,1536]{3,...) custom-call(bf16[4,32,1024]{2,1,0:T(8,128)(2,1)} %pad_maximum_fusion, ...), custom_call_target="tpu_custom_call" | custom-call | tf_op jit(solution)/shard_map/first/pallas_call | solution.py:832
  129.9 1.4 fusion.2
  131.3 81.2 %feed_forward.1 = (f32[2,256,1024]{2,1,0:T(8,128)}, bf16[2,256,1024]{2,1,0:T(8,128)(2,1)}, f32[2,256,1024]{2,1,0:T(8,128)}, bf16[2,4,256,1024]{3,2,1,0:T(8,128)(...) custom-call(f32[2,2,256,1024]{3,2,1,0:T(8,128)} %get-tuple-element.40.res_ref, ...), custom_call_target="tpu_custom_call" | custom-call | tf_op jit(solution)/shard_map/feed_forward/pallas_call | solution.py:1063
  212.5 118.1 %last.1 = (bf16[2,256,1024]{2,1,0:T(8,128)(2,1)}, f32[2,256,1024]{2,1,0:T(8,128)}, bf16[96,1024]{1,0:T(8,128)(2,1)}, bf16[4,32,1536]{2,1,0:T(8,128)(2,1)}, bf16[...) custom-call(bf16[2,2,2,96,1024]{4,3,2,1,0:T(8,128)(2,1)} %bitcast.95, ...), custom_call_target="tpu_custom_call" | custom-call | tf_op jit(solution)/shard_map/last/pallas_call | solution.py:1470
  330.5 0.0 copy-start.7
  330.6 0.0 copy-start.6
  330.6 0.0 copy-start.5
  330.6 0.0 copy-start.2
  330.6 3.2 add_convert_fusion
  333.8 0.0 copy-done.7
  333.8 0.5 slice_bitcast_fusion.17
  334.3 0.6 fusion.3
  334.9 0.0 copy-done.6
  334.9 0.7 convert_element_type.59
  335.7 0.0 copy-done.5
  335.7 0.8 convert_element_type.61
  336.4 0.0 copy-done.2
  336.4 0.0 copy-start.1
  336.7 0.0 copy-start.8
  336.8 0.0 copy-start.9
  336.8 0.0 copy-start.10
  336.8 0.6 copy-done.1
  337.4 0.1 fusion.1
  337.5 0.0 copy-done.8
  337.5 0.0 copy-done.9
  337.5 0.0 copy-done.10
  337.5 0.3 reshape.165
  337.8 0.3 copy.37
  338.1 0.0 copy-start
  338.2 1.2 reshape.166
  339.3 0.3 reshape.163
  339.6 0.3 copy.36
  340.0 1.2 reshape.164
  341.2 0.0 copy-done
  341.2 1.3 copy.74
  (29 shorter events, 0.4 us)
Async XLA Ops:
  0.6 6.7 %copy-start.4 = (bf16[32,3072]{1,0:T(8,128)(2,1)S(1)}, bf16[32,3072]{1,0:T(8,128)(2,1)}, u32[]{:S(2)}) copy-start(bf16[32,3072]{1,0:T(8,128)(2,1)} %param.23) | copy-start | bytes 589828
  0.7 6.2 %copy-start.3 = (bf16[32,3072]{1,0:T(8,128)(2,1)S(1)}, bf16[32,3072]{1,0:T(8,128)(2,1)}, u32[]{:S(2)}) copy-start(bf16[32,3072]{1,0:T(8,128)(2,1)} %param.22) | copy-start | bytes 589828
  330.5 3.3 copy-start.7
  330.6 4.4 %copy-start.6 = (bf16[64,1024]{1,0:T(8,128)(2,1)S(1)}, bf16[64,1024]{1,0:T(8,128)(2,1)}, u32[]{:S(2)}) copy-start(bf16[64,1024]{1,0:T(8,128)(2,1)} %get-tuple-element.64) | copy-start | bytes 393220
  330.6 5.1 %copy-start.5 = (bf16[96,1024]{1,0:T(8,128)(2,1)S(1)}, bf16[96,1024]{1,0:T(8,128)(2,1)}, u32[]{:S(2)}) copy-start(bf16[96,1024]{1,0:T(8,128)(2,1)} %get-tuple-element.66) | copy-start | bytes 589828
  330.6 5.9 %copy-start.2 = (bf16[2,4,32,512]{3,2,1,0:T(8,128)(2,1)S(1)}, bf16[2,4,32,512]{3,2,1,0:T(8,128)(2,1)}, u32[]{:S(2)}) copy-start(bf16[2,4,32,512]{3,2,1,0:T(8,128)(2,1)} %get-tuple-element.63) | copy-start | bytes 786436
  336.4 1.0 copy-start.1
  336.7 0.8 copy-start.8
  336.8 0.7 copy-start.9
  336.8 0.7 copy-start.10
  338.1 3.0 copy-start
